TPU v7x, 32 devices: a whole 2x2x4 slice. The times are simulated.
32 devices in a mesh: groups: 2 (over y), strip: 4 (over z), panel: 2 (over x), sub: 2 (over core).
Axes of the slice: x: 2, y: 2, z: 4, core: 2. Of those that a mesh axis runs over, the one named last changes fastest.
Arguments:
- start_block: float32 [64, 128, 256], P('groups', ('strip', 'sub'), 'panel'), parts along dimension 0, may hold values from -120 to 120, as said below
- edge_weights: float32 [16, 128, 256], P('groups', ('strip', 'sub'), 'panel'), parts along dimension 0, may hold values from 0 to 1, as said below
- mass: float32 [256, 256], P(('groups', 'strip', 'sub'), 'panel'), parts along dimension 0, may hold values from 0.5 to 2
- locked: bfloat16 [2048, 128, 256], P(('groups', 'panel'), ('strip', 'sub')), parts along dimension 0, may hold values from -4 to 4
Outputs:
- ortho: float32 [64, 128, 256], P('groups', ('strip', 'sub'), 'panel'), parts along dimension 0
- coupling: float32 [2048, 32], P(('groups', 'panel')), parts along dimension 0
- r_factor: float32 [64, 32], P('groups'), parts along dimension 0
There are 2 independent parts, one for each index of `groups`. A program takes and returns all parts, laid end to end along the dimension named above; each array names one. Nothing has to cross between parts.
Inputs may be any that keep to these rules, and one draw needn't show every extreme that they name: `start_block`: the sum of an entry's square over the block's vertices is positive for every vector. edge_weights[k + 4] at vertex (i, j) equals edge_weights[k] at vertex (i, j) - o_k for k = 0..3, and is zero where that vertex lies outside the grid; edge_weights[0..3] are positive everywhere.
All inputs are finite; a program needn't handle non-finite values.
Results may differ from a plain program's by a relative error of at most 0.003.
Values may be sent and summed in bfloat16 or wider, within the bound.
No kernel may reach another device: no remote copies, remote signals or barrier semaphores. Data moves between devices by JAX's collectives and lax.ppermute only.
A program may use at most 64 MiB of HBM per device.

v0:
```python
import math

import jax
import jax.numpy as jnp
from jax import lax
from jax.sharding import PartitionSpec as P

DEGREE = 6
CUT_LOW = 2
CUT_HIGH = 32


OFFSETS = ((0, 1), (1, 0), (1, 1), (1, -1), (0, -1), (-1, 0), (-1, -1), (-1, 1))


def with_halo(array, sides, width):
    for axis, dim in sides:
        devices, length = (lax.axis_size(axis), array.shape[dim])
        up = [(i, (i + 1) % devices) for i in range(devices - 1)]
        down = [(j, i) for i, j in up]
        last = lax.slice_in_dim(array, length - width, length, axis=dim)
        leading = lax.slice_in_dim(array, 0, width, axis=dim)
        before = lax.ppermute(last, axis, up)
        after = lax.ppermute(leading, axis, down)
        array = jnp.concatenate([before, array, after], axis=dim)
    return array


def apply_operator(vectors, edge_weights, scaling):
    scaled = scaling * vectors
    padded = with_halo(scaled, ((("strip", "sub"), 1), ("panel", 2)), 1)
    height = scaled.shape[1]
    across = scaled.shape[2]
    summed = jnp.zeros_like(scaled)
    for direction in range(8):
        step_row, step_col = OFFSETS[direction]
        beside = padded[
            :, 1 + step_row : 1 + step_row + height, 1 + step_col : 1 + step_col + across
        ]
        summed = summed + edge_weights[direction] * (scaled - beside)
    return scaling * summed


def chebyshev(start_block, edge_weights, scaling):
    centre = 0.5 * (CUT_HIGH + CUT_LOW)
    spread = 0.5 * (CUT_HIGH - CUT_LOW)
    previous = start_block
    current = (apply_operator(start_block, edge_weights, scaling) - centre * start_block) / spread
    for order_now in range(1, DEGREE):
        following = (
            2.0 * (apply_operator(current, edge_weights, scaling) - centre * current) / spread
            - previous
        )
        previous, current = (current, following)
    return current


def block_gram(flat_block):
    return jnp.dot(
        flat_block,
        flat_block.T,
        precision=lax.Precision.HIGHEST,
        preferred_element_type=jnp.float32,
    )


def on_device(start_block, edge_weights, mass, locked):
    scaling = 1.0 / jnp.sqrt(mass)
    filtered = chebyshev(start_block, edge_weights, scaling)
    block_count = filtered.shape[0]
    vertices = (
        filtered.shape[1]
        * filtered.shape[2]
        * lax.axis_size(("strip", "sub"))
        * lax.axis_size("panel")
    )
    identity_matrix = jnp.eye(block_count, dtype=jnp.float32)
    whole_rows = lax.all_gather(filtered, "panel", axis=2, tiled=True)
    flat_whole = whole_rows.reshape(block_count, -1)
    gram_matrix = (
        lax.psum(block_gram(flat_whole), ("strip", "sub")) / vertices + 1e-06 * identity_matrix
    )
    lower_factor = jnp.linalg.cholesky(gram_matrix)
    ortho_whole = lax.linalg.triangular_solve(
        lower_factor, flat_whole, left_side=True, lower=True
    ).reshape(whole_rows.shape)
    own_width = filtered.shape[2]
    ortho = lax.dynamic_slice_in_dim(ortho_whole, lax.axis_index("panel") * own_width, own_width, 2)
    ortho_half = ortho_whole.astype(jnp.bfloat16).reshape(block_count, -1)
    locked_flat = locked.reshape(locked.shape[0], -1)
    partial_coupling = jnp.einsum(
        "kn,bn->kb", locked_flat, ortho_half, preferred_element_type=jnp.float32
    )
    coupling = lax.psum(partial_coupling, ("strip", "sub")) / math.sqrt(float(vertices))
    return (ortho, coupling, jnp.transpose(lower_factor))


def solution(mesh):
    return jax.shard_map(
        on_device,
        mesh=mesh,
        in_specs=(
            P("groups", ("strip", "sub"), "panel"),
            P("groups", ("strip", "sub"), "panel"),
            P(("groups", "strip", "sub"), "panel"),
            P(("groups", "panel"), ("strip", "sub"), None),
        ),
        out_specs=(
            P("groups", ("strip", "sub"), "panel"),
            P(("groups", "panel"), None),
            P("groups", None),
        ),
        check_vma=False,
    )
```

profile of v0, /device:TPU:0, one launch (start us, length us, event | category | flops | bytes accessed | tf_op | source)
XLA Modules:
  0.0 241.3 jit_solution(13510634319213485302)
XLA Ops:
  9.0 2.4 collective-permute-start
  11.4 1.3 collective-permute-start.1
  12.7 4.0 %collective-permute-done.1 = f32[32,1,128]{2,0,1:T(8,128)S(1)} collective-permute-done((f32[32,1,128]{2,0,1:T(8,128)S(1)}, f32[32,1,128]{2,0,1:T(8,128)S(1)}, u32[]{:S(2)}, u32[]{:S(2)}) %collective-permute-start.1) | collective-permute-done | bytes 16416 | tf_op jit(solution)/shard_map/ppermute | solution.py:24
  16.8 1.3 collective-permute-start.2
  18.1 4.6 %collective-permute-start.3 = (f32[32,18,1]{2,0,1:T(8,128)S(1)}, f32[32,18,1]{2,0,1:T(8,128)S(1)}, u32[]{:S(2)}, u32[]{:S(2)}) collective-permute-start(f32[32,18,1]{2,0,1:T(8,128)S(1)} %get-tuple-element.41), channel_id=1, source_target_pairs={{0,2},{1,3},{4,6},{5,7},{8,10},{9,11},{12,14},{13,15},{16,18},{17,... | collective-permute-start | bytes 6920 | tf_op jit(solution)/shard_map/ppermute | solution.py:23
  23.5 3.5 %collective-permute-done.2 = f32[32,18,1]{2,0,1:T(8,128)S(1)} collective-permute-done((f32[32,18,1]{2,0,1:T(8,128)S(1)}, f32[32,18,1]{2,0,1:T(8,128)S(1)}, u32[]{:S(2)}, u32[]{:S(2)}) %collective-permute-start.2) | collective-permute-done | bytes 2336 | tf_op jit(solution)/shard_map/ppermute | solution.py:24
  27.0 1.8 collective-permute-done.3
  29.5 3.3 %collective-permute-start.4 = (f32[32,1,128]{2,0,1:T(8,128)S(1)}, f32[32,1,128]{2,0,1:T(8,128)S(1)}, u32[]{:S(2)}, u32[]{:S(2)}) collective-permute-start(f32[32,1,128]{2,0,1:T(8,128)S(1)} %get-tuple-element.51), channel_id=1, source_target_pairs={{0,1},{1,4},{4,5},{5,8},{8,9},{9,12},{12,13},{2,3},{3,6},{6,7},{7,... | collective-permute-start | bytes 49160 | tf_op jit(solution)/shard_map/ppermute | solution.py:23
  32.8 1.3 collective-permute-start.5
  34.1 3.3 %collective-permute-done.5 = f32[32,1,128]{2,0,1:T(8,128)S(1)} collective-permute-done((f32[32,1,128]{2,0,1:T(8,128)S(1)}, f32[32,1,128]{2,0,1:T(8,128)S(1)}, u32[]{:S(2)}, u32[]{:S(2)}) %collective-permute-start.5) | collective-permute-done | bytes 16416 | tf_op jit(solution)/shard_map/ppermute | solution.py:24
  37.6 1.3 collective-permute-start.6
  38.9 4.6 %collective-permute-start.7 = (f32[32,18,1]{2,0,1:T(8,128)S(1)}, f32[32,18,1]{2,0,1:T(8,128)S(1)}, u32[]{:S(2)}, u32[]{:S(2)}) collective-permute-start(f32[32,18,1]{2,0,1:T(8,128)S(1)} %get-tuple-element.37), channel_id=1, source_target_pairs={{0,2},{1,3},{4,6},{5,7},{8,10},{9,11},{12,14},{13,15},{16,18},{17,... | collective-permute-start | bytes 6920 | tf_op jit(solution)/shard_map/ppermute | solution.py:23
  43.5 4.2 %collective-permute-done.6 = f32[32,18,1]{2,0,1:T(8,128)S(1)} collective-permute-done((f32[32,18,1]{2,0,1:T(8,128)S(1)}, f32[32,18,1]{2,0,1:T(8,128)S(1)}, u32[]{:S(2)}, u32[]{:S(2)}) %collective-permute-start.6) | collective-permute-done | bytes 2336 | tf_op jit(solution)/shard_map/ppermute | solution.py:24
  47.7 1.8 collective-permute-done.7
  50.2 3.4 %collective-permute-start.8 = (f32[32,1,128]{2,0,1:T(8,128)S(1)}, f32[32,1,128]{2,0,1:T(8,128)S(1)}, u32[]{:S(2)}, u32[]{:S(2)}) collective-permute-start(f32[32,1,128]{2,0,1:T(8,128)S(1)} %get-tuple-element.49), channel_id=1, source_target_pairs={{0,1},{1,4},{4,5},{5,8},{8,9},{9,12},{12,13},{2,3},{3,6},{6,7},{7,... | collective-permute-start | bytes 49160 | tf_op jit(solution)/shard_map/ppermute | solution.py:23
  53.6 1.3 collective-permute-start.9
  54.9 3.2 %collective-permute-done.9 = f32[32,1,128]{2,0,1:T(8,128)S(1)} collective-permute-done((f32[32,1,128]{2,0,1:T(8,128)S(1)}, f32[32,1,128]{2,0,1:T(8,128)S(1)}, u32[]{:S(2)}, u32[]{:S(2)}) %collective-permute-start.9) | collective-permute-done | bytes 16416 | tf_op jit(solution)/shard_map/ppermute | solution.py:24
  58.3 1.3 collective-permute-start.10
  59.6 4.6 %collective-permute-start.11 = (f32[32,18,1]{2,0,1:T(8,128)S(1)}, f32[32,18,1]{2,0,1:T(8,128)S(1)}, u32[]{:S(2)}, u32[]{:S(2)}) collective-permute-start(f32[32,18,1]{2,0,1:T(8,128)S(1)} %get-tuple-element.33), channel_id=1, source_target_pairs={{0,2},{1,3},{4,6},{5,7},{8,10},{9,11},{12,14},{13,15},{16,18},{17,... | collective-permute-start | bytes 6920 | tf_op jit(solution)/shard_map/ppermute | solution.py:23
  64.2 4.2 %collective-permute-done.10 = f32[32,18,1]{2,0,1:T(8,128)S(1)} collective-permute-done((f32[32,18,1]{2,0,1:T(8,128)S(1)}, f32[32,18,1]{2,0,1:T(8,128)S(1)}, u32[]{:S(2)}, u32[]{:S(2)}) %collective-permute-start.10) | collective-permute-done | bytes 2336 | tf_op jit(solution)/shard_map/ppermute | solution.py:24
  68.4 1.8 collective-permute-done.11
  70.8 3.4 %collective-permute-start.12 = (f32[32,1,128]{2,0,1:T(8,128)S(1)}, f32[32,1,128]{2,0,1:T(8,128)S(1)}, u32[]{:S(2)}, u32[]{:S(2)}) collective-permute-start(f32[32,1,128]{2,0,1:T(8,128)S(1)} %get-tuple-element.47), channel_id=1, source_target_pairs={{0,1},{1,4},{4,5},{5,8},{8,9},{9,12},{12,13},{2,3},{3,6},{6,7},{7,... | collective-permute-start | bytes 49160 | tf_op jit(solution)/shard_map/ppermute | solution.py:23
  74.3 1.3 collective-permute-start.13
  75.6 3.5 %collective-permute-done.13 = f32[32,1,128]{2,0,1:T(8,128)S(1)} collective-permute-done((f32[32,1,128]{2,0,1:T(8,128)S(1)}, f32[32,1,128]{2,0,1:T(8,128)S(1)}, u32[]{:S(2)}, u32[]{:S(2)}) %collective-permute-start.13) | collective-permute-done | bytes 16416 | tf_op jit(solution)/shard_map/ppermute | solution.py:24
  79.2 1.3 collective-permute-start.14
  80.5 4.6 %collective-permute-start.15 = (f32[32,18,1]{2,0,1:T(8,128)S(1)}, f32[32,18,1]{2,0,1:T(8,128)S(1)}, u32[]{:S(2)}, u32[]{:S(2)}) collective-permute-start(f32[32,18,1]{2,0,1:T(8,128)S(1)} %get-tuple-element.29), channel_id=1, source_target_pairs={{0,2},{1,3},{4,6},{5,7},{8,10},{9,11},{12,14},{13,15},{16,18},{17,... | collective-permute-start | bytes 6920 | tf_op jit(solution)/shard_map/ppermute | solution.py:23
  85.1 4.2 %collective-permute-done.14 = f32[32,18,1]{2,0,1:T(8,128)S(1)} collective-permute-done((f32[32,18,1]{2,0,1:T(8,128)S(1)}, f32[32,18,1]{2,0,1:T(8,128)S(1)}, u32[]{:S(2)}, u32[]{:S(2)}) %collective-permute-start.14) | collective-permute-done | bytes 2336 | tf_op jit(solution)/shard_map/ppermute | solution.py:24
  89.3 1.8 collective-permute-done.15
  91.8 3.4 %collective-permute-start.16 = (f32[32,1,128]{2,0,1:T(8,128)S(1)}, f32[32,1,128]{2,0,1:T(8,128)S(1)}, u32[]{:S(2)}, u32[]{:S(2)}) collective-permute-start(f32[32,1,128]{2,0,1:T(8,128)S(1)} %get-tuple-element.45), channel_id=1, source_target_pairs={{0,1},{1,4},{4,5},{5,8},{8,9},{9,12},{12,13},{2,3},{3,6},{6,7},{7,... | collective-permute-start | bytes 49160 | tf_op jit(solution)/shard_map/ppermute | solution.py:23
  95.2 1.3 collective-permute-start.17
  96.5 2.7 %collective-permute-done.17 = f32[32,1,128]{2,0,1:T(8,128)S(1)} collective-permute-done((f32[32,1,128]{2,0,1:T(8,128)S(1)}, f32[32,1,128]{2,0,1:T(8,128)S(1)}, u32[]{:S(2)}, u32[]{:S(2)}) %collective-permute-start.17) | collective-permute-done | bytes 16416 | tf_op jit(solution)/shard_map/ppermute | solution.py:24
  99.4 1.3 collective-permute-start.18
  100.7 4.6 %collective-permute-start.19 = (f32[32,18,1]{2,0,1:T(8,128)S(1)}, f32[32,18,1]{2,0,1:T(8,128)S(1)}, u32[]{:S(2)}, u32[]{:S(2)}) collective-permute-start(f32[32,18,1]{2,0,1:T(8,128)S(1)} %get-tuple-element.25), channel_id=1, source_target_pairs={{0,2},{1,3},{4,6},{5,7},{8,10},{9,11},{12,14},{13,15},{16,18},{17,... | collective-permute-start | bytes 6920 | tf_op jit(solution)/shard_map/ppermute | solution.py:23
  105.3 4.2 %collective-permute-done.18 = f32[32,18,1]{2,0,1:T(8,128)S(1)} collective-permute-done((f32[32,18,1]{2,0,1:T(8,128)S(1)}, f32[32,18,1]{2,0,1:T(8,128)S(1)}, u32[]{:S(2)}, u32[]{:S(2)}) %collective-permute-start.18) | collective-permute-done | bytes 2336 | tf_op jit(solution)/shard_map/ppermute | solution.py:24
  109.5 1.8 collective-permute-done.19
  111.9 3.4 %collective-permute-start.20 = (f32[32,1,128]{2,0,1:T(8,128)S(1)}, f32[32,1,128]{2,0,1:T(8,128)S(1)}, u32[]{:S(2)}, u32[]{:S(2)}) collective-permute-start(f32[32,1,128]{2,0,1:T(8,128)S(1)} %get-tuple-element.43), channel_id=1, source_target_pairs={{0,1},{1,4},{4,5},{5,8},{8,9},{9,12},{12,13},{2,3},{3,6},{6,7},{7,... | collective-permute-start | bytes 49160 | tf_op jit(solution)/shard_map/ppermute | solution.py:23
  115.4 1.3 collective-permute-start.21
  116.7 1.8 collective-permute-done.21
  119.9 4.6 %collective-permute-start.23 = (f32[32,18,1]{2,0,1:T(8,128)S(1)}, f32[32,18,1]{2,0,1:T(8,128)S(1)}, u32[]{:S(2)}, u32[]{:S(2)}) collective-permute-start(f32[32,18,1]{2,0,1:T(8,128)S(1)} %get-tuple-element.21), channel_id=1, source_target_pairs={{0,2},{1,3},{4,6},{5,7},{8,10},{9,11},{12,14},{13,15},{16,18},{17,... | collective-permute-start | bytes 6920 | tf_op jit(solution)/shard_map/ppermute | solution.py:23
  124.5 4.3 %collective-permute-done.22 = f32[32,18,1]{2,0,1:T(8,128)S(1)} collective-permute-done((f32[32,18,1]{2,0,1:T(8,128)S(1)}, f32[32,18,1]{2,0,1:T(8,128)S(1)}, u32[]{:S(2)}, u32[]{:S(2)}) %collective-permute-start.22) | collective-permute-done | bytes 2336 | tf_op jit(solution)/shard_map/ppermute | solution.py:24
  128.8 1.8 collective-permute-done.23
  131.2 9.9 %all_gather.3 = f32[32,16,256]{2,0,1:T(8,128)S(1)} all-gather(f32[32,16,128]{2,0,1:T(8,128)S(1)} %fusion.13), channel_id=1, replica_groups=mesh['groups'=2,'strip'=4,'panel'=2,'sub'=2] {'panel'}, dimensions={2}, use_global_device_ids=true | all-gather | bytes 786432 | tf_op jit(solution)/shard_map/all_gather | solution.py:78
  141.7 26.0 %psum.14 = f32[32,32]{1,0:T(8,128)S(1)} all-reduce(f32[32,32]{1,0:T(8,128)S(1)} %convolution_bitcast_fusion), channel_id=1, replica_groups=mesh['groups'=2,'strip'=4,'panel'=2,'sub'=2] {'strip','sub'}, use_global_device_ids=true, to_apply=%region_0.0 | all-reduce | flops 1024 | bytes 8192 | tf_op jit(solution)/shard_map/psum | solution.py:81
  167.8 2.9 %cholesky.16 = f32[32,32]{1,0:T(8,128)S(1)} custom-call(f32[32,32]{1,0:T(8,128)S(1)} %fusion.134), custom_call_target="Cholesky" | custom-call | tf_op jit(solution)/shard_map/jit(cholesky)/cholesky | solution.py:83
  172.1 2.4 %custom-call.6 = f32[1,32,32]{1,2,0:T(8,128)S(1)} custom-call(f32[1,32,32]{2,1,0:T(8,128)S(1)} %get-tuple-element.64), custom_call_target="InvertDiagBlocksLowerTriangular" | custom-call | tf_op jit(solution)/shard_map/triangular_solve | solution.py:84
  175.2 5.2 %fusion.2 = f32[512,32]{0,1:T(8,128)} fusion(bf16[512,16,256]{2,1,0:T(8,128)(2,1)} %param.7, f32[32,16,256]{2,0,1:T(8,128)S(1)} %fusion.5), kind=kOutput, calls=%fused_computation.2 | convolution fusion | flops 134348800 | bytes 4784128 | tf_op jit(solution)/shard_map/kn,bn->kb/dot_general | solution.py:91
  181.9 51.1 %all-reduce.2.cloned.1.call-done = f32[512,32]{0,1:T(8,128)} async-done(((f32[512,32]{0,1:T(8,128)}), f32[512,32]{0,1:T(8,128)}) %all-reduce.2.cloned.1.call-update) | async-done | bytes 65552 | tf_op jit(solution)/shard_map/psum | solution.py:94
  233.0 1.5 broadcast_multiply_fusion.5
  (55 shorter events, 13.3 us)
Async XLA Ops:
  7.2 21.9 %copy-start = (f32[32,16,128]{2,1,0:T(8,128)S(1)}, f32[32,16,128]{2,1,0:T(8,128)}, u32[]{:S(2)}) copy-start(f32[32,16,128]{2,1,0:T(8,128)} %param.4) | copy-start | bytes 786436
  7.2 225.8 %all-reduce.2.cloned.1.call-start = ((), (), s32[]{:S(2)}) async-start(), calls=%async_computation | async-start | bytes 131072 | tf_op jit(solution)/shard_map/psum | solution.py:94
  9.0 3.7 %collective-permute-start = (f32[32,1,128]{2,0,1:T(8,128)S(1)}, f32[32,1,128]{2,0,1:T(8,128)S(1)}, u32[]{:S(2)}, u32[]{:S(2)}) collective-permute-start(f32[32,1,128]{2,0,1:T(8,128)S(1)} %get-tuple-element.53), channel_id=1, source_target_pairs={{0,1},{1,4},{4,5},{5,8},{8,9},{9,12},{12,13},{2,3},{3,6},{6,7},{7,... | collective-permute-start | bytes 49160 | tf_op jit(solution)/shard_map/ppermute | solution.py:23
  11.4 5.3 %collective-permute-start.1 = (f32[32,1,128]{2,0,1:T(8,128)S(1)}, f32[32,1,128]{2,0,1:T(8,128)S(1)}, u32[]{:S(2)}, u32[]{:S(2)}) collective-permute-start(f32[32,1,128]{2,0,1:T(8,128)S(1)} %get-tuple-element.54), channel_id=1, source_target_pairs={{1,0},{4,1},{5,4},{8,5},{9,8},{12,9},{13,12},{3,2},{6,3},{7,6},{10... | collective-permute-start | bytes 49160 | tf_op jit(solution)/shard_map/ppermute | solution.py:24
  16.8 10.2 %collective-permute-start.2 = (f32[32,18,1]{2,0,1:T(8,128)S(1)}, f32[32,18,1]{2,0,1:T(8,128)S(1)}, u32[]{:S(2)}, u32[]{:S(2)}) collective-permute-start(f32[32,18,1]{2,0,1:T(8,128)S(1)} %get-tuple-element.42), channel_id=1, source_target_pairs={{2,0},{3,1},{6,4},{7,5},{10,8},{11,9},{14,12},{15,13},{18,16},{19,... | collective-permute-start | bytes 6920 | tf_op jit(solution)/shard_map/ppermute | solution.py:24
  18.1 10.7 %collective-permute-start.3 = (f32[32,18,1]{2,0,1:T(8,128)S(1)}, f32[32,18,1]{2,0,1:T(8,128)S(1)}, u32[]{:S(2)}, u32[]{:S(2)}) collective-permute-start(f32[32,18,1]{2,0,1:T(8,128)S(1)} %get-tuple-element.41), channel_id=1, source_target_pairs={{0,2},{1,3},{4,6},{5,7},{8,10},{9,11},{12,14},{13,15},{16,18},{17,... | collective-permute-start | bytes 6920 | tf_op jit(solution)/shard_map/ppermute | solution.py:23
  29.5 4.6 %collective-permute-start.4 = (f32[32,1,128]{2,0,1:T(8,128)S(1)}, f32[32,1,128]{2,0,1:T(8,128)S(1)}, u32[]{:S(2)}, u32[]{:S(2)}) collective-permute-start(f32[32,1,128]{2,0,1:T(8,128)S(1)} %get-tuple-element.51), channel_id=1, source_target_pairs={{0,1},{1,4},{4,5},{5,8},{8,9},{9,12},{12,13},{2,3},{3,6},{6,7},{7,... | collective-permute-start | bytes 49160 | tf_op jit(solution)/shard_map/ppermute | solution.py:23
  32.8 4.6 %collective-permute-start.5 = (f32[32,1,128]{2,0,1:T(8,128)S(1)}, f32[32,1,128]{2,0,1:T(8,128)S(1)}, u32[]{:S(2)}, u32[]{:S(2)}) collective-permute-start(f32[32,1,128]{2,0,1:T(8,128)S(1)} %get-tuple-element.52), channel_id=1, source_target_pairs={{1,0},{4,1},{5,4},{8,5},{9,8},{12,9},{13,12},{3,2},{6,3},{7,6},{10... | collective-permute-start | bytes 49160 | tf_op jit(solution)/shard_map/ppermute | solution.py:24
  37.6 10.1 %collective-permute-start.6 = (f32[32,18,1]{2,0,1:T(8,128)S(1)}, f32[32,18,1]{2,0,1:T(8,128)S(1)}, u32[]{:S(2)}, u32[]{:S(2)}) collective-permute-start(f32[32,18,1]{2,0,1:T(8,128)S(1)} %get-tuple-element.38), channel_id=1, source_target_pairs={{2,0},{3,1},{6,4},{7,5},{10,8},{11,9},{14,12},{15,13},{18,16},{19,... | collective-permute-start | bytes 6920 | tf_op jit(solution)/shard_map/ppermute | solution.py:24
  38.9 10.6 %collective-permute-start.7 = (f32[32,18,1]{2,0,1:T(8,128)S(1)}, f32[32,18,1]{2,0,1:T(8,128)S(1)}, u32[]{:S(2)}, u32[]{:S(2)}) collective-permute-start(f32[32,18,1]{2,0,1:T(8,128)S(1)} %get-tuple-element.37), channel_id=1, source_target_pairs={{0,2},{1,3},{4,6},{5,7},{8,10},{9,11},{12,14},{13,15},{16,18},{17,... | collective-permute-start | bytes 6920 | tf_op jit(solution)/shard_map/ppermute | solution.py:23
  50.2 4.7 %collective-permute-start.8 = (f32[32,1,128]{2,0,1:T(8,128)S(1)}, f32[32,1,128]{2,0,1:T(8,128)S(1)}, u32[]{:S(2)}, u32[]{:S(2)}) collective-permute-start(f32[32,1,128]{2,0,1:T(8,128)S(1)} %get-tuple-element.49), channel_id=1, source_target_pairs={{0,1},{1,4},{4,5},{5,8},{8,9},{9,12},{12,13},{2,3},{3,6},{6,7},{7,... | collective-permute-start | bytes 49160 | tf_op jit(solution)/shard_map/ppermute | solution.py:23
  53.6 4.5 %collective-permute-start.9 = (f32[32,1,128]{2,0,1:T(8,128)S(1)}, f32[32,1,128]{2,0,1:T(8,128)S(1)}, u32[]{:S(2)}, u32[]{:S(2)}) collective-permute-start(f32[32,1,128]{2,0,1:T(8,128)S(1)} %get-tuple-element.50), channel_id=1, source_target_pairs={{1,0},{4,1},{5,4},{8,5},{9,8},{12,9},{13,12},{3,2},{6,3},{7,6},{10... | collective-permute-start | bytes 49160 | tf_op jit(solution)/shard_map/ppermute | solution.py:24
  58.3 10.1 %collective-permute-start.10 = (f32[32,18,1]{2,0,1:T(8,128)S(1)}, f32[32,18,1]{2,0,1:T(8,128)S(1)}, u32[]{:S(2)}, u32[]{:S(2)}) collective-permute-start(f32[32,18,1]{2,0,1:T(8,128)S(1)} %get-tuple-element.34), channel_id=1, source_target_pairs={{2,0},{3,1},{6,4},{7,5},{10,8},{11,9},{14,12},{15,13},{18,16},{19,... | collective-permute-start | bytes 6920 | tf_op jit(solution)/shard_map/ppermute | solution.py:24
  59.6 10.6 %collective-permute-start.11 = (f32[32,18,1]{2,0,1:T(8,128)S(1)}, f32[32,18,1]{2,0,1:T(8,128)S(1)}, u32[]{:S(2)}, u32[]{:S(2)}) collective-permute-start(f32[32,18,1]{2,0,1:T(8,128)S(1)} %get-tuple-element.33), channel_id=1, source_target_pairs={{0,2},{1,3},{4,6},{5,7},{8,10},{9,11},{12,14},{13,15},{16,18},{17,... | collective-permute-start | bytes 6920 | tf_op jit(solution)/shard_map/ppermute | solution.py:23
  70.8 4.7 %collective-permute-start.12 = (f32[32,1,128]{2,0,1:T(8,128)S(1)}, f32[32,1,128]{2,0,1:T(8,128)S(1)}, u32[]{:S(2)}, u32[]{:S(2)}) collective-permute-start(f32[32,1,128]{2,0,1:T(8,128)S(1)} %get-tuple-element.47), channel_id=1, source_target_pairs={{0,1},{1,4},{4,5},{5,8},{8,9},{9,12},{12,13},{2,3},{3,6},{6,7},{7,... | collective-permute-start | bytes 49160 | tf_op jit(solution)/shard_map/ppermute | solution.py:23
  74.3 4.8 %collective-permute-start.13 = (f32[32,1,128]{2,0,1:T(8,128)S(1)}, f32[32,1,128]{2,0,1:T(8,128)S(1)}, u32[]{:S(2)}, u32[]{:S(2)}) collective-permute-start(f32[32,1,128]{2,0,1:T(8,128)S(1)} %get-tuple-element.48), channel_id=1, source_target_pairs={{1,0},{4,1},{5,4},{8,5},{9,8},{12,9},{13,12},{3,2},{6,3},{7,6},{10... | collective-permute-start | bytes 49160 | tf_op jit(solution)/shard_map/ppermute | solution.py:24
  79.2 10.1 %collective-permute-start.14 = (f32[32,18,1]{2,0,1:T(8,128)S(1)}, f32[32,18,1]{2,0,1:T(8,128)S(1)}, u32[]{:S(2)}, u32[]{:S(2)}) collective-permute-start(f32[32,18,1]{2,0,1:T(8,128)S(1)} %get-tuple-element.30), channel_id=1, source_target_pairs={{2,0},{3,1},{6,4},{7,5},{10,8},{11,9},{14,12},{15,13},{18,16},{19,... | collective-permute-start | bytes 6920 | tf_op jit(solution)/shard_map/ppermute | solution.py:24
  80.5 10.6 %collective-permute-start.15 = (f32[32,18,1]{2,0,1:T(8,128)S(1)}, f32[32,18,1]{2,0,1:T(8,128)S(1)}, u32[]{:S(2)}, u32[]{:S(2)}) collective-permute-start(f32[32,18,1]{2,0,1:T(8,128)S(1)} %get-tuple-element.29), channel_id=1, source_target_pairs={{0,2},{1,3},{4,6},{5,7},{8,10},{9,11},{12,14},{13,15},{16,18},{17,... | collective-permute-start | bytes 6920 | tf_op jit(solution)/shard_map/ppermute | solution.py:23
  91.8 4.7 %collective-permute-start.16 = (f32[32,1,128]{2,0,1:T(8,128)S(1)}, f32[32,1,128]{2,0,1:T(8,128)S(1)}, u32[]{:S(2)}, u32[]{:S(2)}) collective-permute-start(f32[32,1,128]{2,0,1:T(8,128)S(1)} %get-tuple-element.45), channel_id=1, source_target_pairs={{0,1},{1,4},{4,5},{5,8},{8,9},{9,12},{12,13},{2,3},{3,6},{6,7},{7,... | collective-permute-start | bytes 49160 | tf_op jit(solution)/shard_map/ppermute | solution.py:23
  95.2 4.0 %collective-permute-start.17 = (f32[32,1,128]{2,0,1:T(8,128)S(1)}, f32[32,1,128]{2,0,1:T(8,128)S(1)}, u32[]{:S(2)}, u32[]{:S(2)}) collective-permute-start(f32[32,1,128]{2,0,1:T(8,128)S(1)} %get-tuple-element.46), channel_id=1, source_target_pairs={{1,0},{4,1},{5,4},{8,5},{9,8},{12,9},{13,12},{3,2},{6,3},{7,6},{10... | collective-permute-start | bytes 49160 | tf_op jit(solution)/shard_map/ppermute | solution.py:24
  99.4 10.1 %collective-permute-start.18 = (f32[32,18,1]{2,0,1:T(8,128)S(1)}, f32[32,18,1]{2,0,1:T(8,128)S(1)}, u32[]{:S(2)}, u32[]{:S(2)}) collective-permute-start(f32[32,18,1]{2,0,1:T(8,128)S(1)} %get-tuple-element.26), channel_id=1, source_target_pairs={{2,0},{3,1},{6,4},{7,5},{10,8},{11,9},{14,12},{15,13},{18,16},{19,... | collective-permute-start | bytes 6920 | tf_op jit(solution)/shard_map/ppermute | solution.py:24
  100.7 10.6 %collective-permute-start.19 = (f32[32,18,1]{2,0,1:T(8,128)S(1)}, f32[32,18,1]{2,0,1:T(8,128)S(1)}, u32[]{:S(2)}, u32[]{:S(2)}) collective-permute-start(f32[32,18,1]{2,0,1:T(8,128)S(1)} %get-tuple-element.25), channel_id=1, source_target_pairs={{0,2},{1,3},{4,6},{5,7},{8,10},{9,11},{12,14},{13,15},{16,18},{17,... | collective-permute-start | bytes 6920 | tf_op jit(solution)/shard_map/ppermute | solution.py:23
  111.9 4.7 %collective-permute-start.20 = (f32[32,1,128]{2,0,1:T(8,128)S(1)}, f32[32,1,128]{2,0,1:T(8,128)S(1)}, u32[]{:S(2)}, u32[]{:S(2)}) collective-permute-start(f32[32,1,128]{2,0,1:T(8,128)S(1)} %get-tuple-element.43), channel_id=1, source_target_pairs={{0,1},{1,4},{4,5},{5,8},{8,9},{9,12},{12,13},{2,3},{3,6},{6,7},{7,... | collective-permute-start | bytes 49160 | tf_op jit(solution)/shard_map/ppermute | solution.py:23
  115.4 3.1 %collective-permute-start.21 = (f32[32,1,128]{2,0,1:T(8,128)S(1)}, f32[32,1,128]{2,0,1:T(8,128)S(1)}, u32[]{:S(2)}, u32[]{:S(2)}) collective-permute-start(f32[32,1,128]{2,0,1:T(8,128)S(1)} %get-tuple-element.44), channel_id=1, source_target_pairs={{1,0},{4,1},{5,4},{8,5},{9,8},{12,9},{13,12},{3,2},{6,3},{7,6},{10... | collective-permute-start | bytes 49160 | tf_op jit(solution)/shard_map/ppermute | solution.py:24
  118.6 10.1 %collective-permute-start.22 = (f32[32,18,1]{2,0,1:T(8,128)S(1)}, f32[32,18,1]{2,0,1:T(8,128)S(1)}, u32[]{:S(2)}, u32[]{:S(2)}) collective-permute-start(f32[32,18,1]{2,0,1:T(8,128)S(1)} %get-tuple-element.22), channel_id=1, source_target_pairs={{2,0},{3,1},{6,4},{7,5},{10,8},{11,9},{14,12},{15,13},{18,16},{19,... | collective-permute-start | bytes 6920 | tf_op jit(solution)/shard_map/ppermute | solution.py:24
  119.9 10.6 %collective-permute-start.23 = (f32[32,18,1]{2,0,1:T(8,128)S(1)}, f32[32,18,1]{2,0,1:T(8,128)S(1)}, u32[]{:S(2)}, u32[]{:S(2)}) collective-permute-start(f32[32,18,1]{2,0,1:T(8,128)S(1)} %get-tuple-element.21), channel_id=1, source_target_pairs={{0,2},{1,3},{4,6},{5,7},{8,10},{9,11},{12,14},{13,15},{16,18},{17,... | collective-permute-start | bytes 6920 | tf_op jit(solution)/shard_map/ppermute | solution.py:23
Sparse Core Ops, SparseCore 0:
  180.5 52.4 all-reduce.1
where the time goes:
time: 242 us; the launch traced here: 241 us
  waiting for transfers between devices  105 us (43%)
  starting transfers between devices  62.3 us (26%)
  blocking collectives  35.9 us (15%)
  between operations  14.5 us (6%)
  other arithmetic  14.2 us (6%)
  matrix products  6.4 us (3%)
  local copies, waits for them, and re-layouts  3.36 us (1%)
    psum x1, waiting for transfers between devices, on_device(): lax.psum(partial_coupling, ('strip', 'sub')) / math.sqrt(float(vertices))  51.1 us
    ppermute x12, starting transfers between devices, with_halo(): before = lax.ppermute(last, axis, up)  46.8 us
    ppermute x12, waiting for transfers between devices, with_halo(): after = lax.ppermute(leading, axis, down)  42.9 us
    psum x1, blocking collectives, on_device(): lax.psum(block_gram(flat_whole), ('strip', 'sub')) / vertices  26 us
    ppermute x12, starting transfers between devices, with_halo(): after = lax.ppermute(leading, axis, down)  15.5 us
    ppermute x12, waiting for transfers between devices, with_halo(): before = lax.ppermute(last, axis, up)  10.7 us
    all_gather x1, blocking collectives, on_device(): whole_rows = lax.all_gather(filtered, 'panel', axis=2, tiled=True)  9.93 us
    dot_general x1, matrix products, on_device(): jnp.einsum('kn,bn->kb', locked_flat, ortho_half, preferred_element_type=j...  5.19 us
  transfers between devices with their start and end apart: 25, of which 19 were waited for; matrix products, arithmetic and copies ran while one was open for 1% of the time, Pallas kernels for 0%

commit v1 on v0

v1 whole, which is shorter than its diff:
```python
import math

import jax
import jax.numpy as jnp
from jax import lax
from jax.experimental import pallas as pl
from jax.experimental.pallas import tpu as pltpu
from jax.sharding import PartitionSpec as P

DEGREE = 6
CUT_LOW = 2
CUT_HIGH = 32
CENTRE = 0.5 * (CUT_HIGH + CUT_LOW)
SPREAD = 0.5 * (CUT_HIGH - CUT_LOW)
HALO = DEGREE
GRID_ROWS = ("strip", "sub")


def pack_kernel(block_ref, weights_ref, mass_ref, out_ref):
    count, height, _ = block_ref.shape
    out_ref[:, 0:count, :] = pltpu.einshape("brc->rbc", block_ref[...])
    side = jnp.concatenate([weights_ref[0:4], mass_ref[...][None], mass_ref[...][None],
                            mass_ref[...][None], mass_ref[...][None]], axis=0)
    out_ref[:, count : count + 8, :] = pltpu.einshape("brc->rbc", side)


def pack(start_block, edge_weights, mass):
    count, height, width = start_block.shape
    return pl.pallas_call(
        pack_kernel,
        out_shape=jax.ShapeDtypeStruct((height, count + 8, width), jnp.float32),
        name="pack",
    )(start_block, edge_weights, mass)


def filter_kernel(panel_ref, *refs, panels, height, count, width):
    bodies = refs[0:panels]
    above = refs[panels : 2 * panels]
    below = refs[2 * panels : 3 * panels]
    locked_ref, payload_ref, own_ref, y_even, y_odd, coef, split = refs[3 * panels :]
    total = panels * width
    rows = height + 2 * HALO
    panel = panel_ref[0]

    def source(row):
        if row < HALO:
            return [a[row] for a in above]
        if row < HALO + height:
            return [b[row - HALO] for b in bodies]
        return [b[row - HALO - height] for b in below]

    lane = lax.broadcasted_iota(jnp.int32, (1, total), 1)
    column = lax.rem(lane + panel * width, total)
    not_last = (column != total - 1).astype(jnp.float32)
    not_first = (column != 0).astype(jnp.float32)

    factor = 2.0 / SPREAD

    def left(x):
        return pltpu.roll(x, total - 1, 1)

    def right(x):
        return pltpu.roll(x, 1, 1)

    weights = []
    scale = []
    for row in range(rows):
        parts = source(row)
        full = jnp.concatenate(parts, axis=1)
        y_even[row] = full[0:count]
        side = full[count : count + 8]
        mass = side[4:5]
        inside = mass > 0.0
        scale.append(jnp.where(inside, 1.0 / jnp.sqrt(jnp.where(inside, mass, 1.0)), 0.0))
        weights.append([side[d : d + 1] for d in range(4)])
    edges = []
    for row in range(rows - 1):
        s0 = scale[row]
        s1 = scale[row + 1]
        w = weights[row]
        e0 = -factor * (w[0] * (s0 * left(s0))) * not_last
        e1 = -factor * (w[1] * (s0 * s1))
        e2 = -factor * (w[2] * (s0 * left(s1))) * not_last
        e3 = -factor * (w[3] * (s0 * right(s1))) * not_first
        edges.append((e0, e1, e2, e3))
    for row in range(1, rows - 1):
        w = weights[row]
        v = weights[row - 1]
        total_weight = (
            ((w[0] + w[1]) + (w[2] + w[3]))
            + (right(w[0] * not_last) + v[1])
            + (right(v[2] * not_last) + left(v[3] * not_first))
        )
        diagonal = factor * (scale[row] * scale[row] * total_weight - CENTRE)
        e0, e1, e2, e3 = edges[row]
        u0, u1, u2, u3 = edges[row - 1]
        planes = (diagonal, e1, u1, right(e0), right(e2), u3, e0, left(e3), u2)
        for index, plane in enumerate(planes):
            coef[row, index] = jnp.broadcast_to(plane, (8, total))

    def step(order, source_ref, target_ref):
        first = order
        last = rows - order

        def body(row, carry):
            c = [jnp.concatenate([coef[row, i]] * (count // 8), axis=0) for i in range(9)]
            ym = source_ref[row - 1]
            y0 = source_ref[row]
            yp = source_ref[row + 1]
            out = c[0] * y0 + (c[1] * yp + c[2] * ym)
            to_left = c[3] * y0 + (c[4] * yp + c[5] * ym)
            to_right = c[6] * y0 + (c[7] * yp + c[8] * ym)
            out = out + (left(to_left) + right(to_right))
            if order == 1:
                out = 0.5 * out
            else:
                out = out - target_ref[row]
            target_ref[row] = out
            return carry

        lax.fori_loop(first, last, body, 0, unroll=2)

    buffers = (y_even, y_odd)
    for order in range(1, DEGREE + 1):
        step(order, buffers[(order - 1) % 2], buffers[order % 2])
    result = buffers[DEGREE % 2]

    for row in range(height):
        full = result[row + HALO]
        own_ref[row] = full[:, 0:width]
        high = full.astype(jnp.bfloat16)
        rest = full - high.astype(jnp.float32)
        middle = rest.astype(jnp.bfloat16)
        low = (rest - middle.astype(jnp.float32)).astype(jnp.bfloat16)
        stacked = jnp.concatenate([high, middle, low], axis=0)
        for t in range(panels):
            at = row * total + lax.rem(panel + t, panels) * width
            split[:, pl.ds(pl.multiple_of(at, width), width)] = stacked[:, t * width : (t + 1) * width]

    dims = (((1,), (1,)), ((), ()))
    pieces = split[...]
    products = lax.dot_general(pieces, locked_ref[...], dims, preferred_element_type=jnp.float32)
    basis = locked_ref.shape[0]
    payload_ref[:, 0:basis] = (
        products[0:count] + products[count : 2 * count] + products[2 * count : 3 * count]
    )
    gram = lax.dot_general(pieces, pieces, dims, preferred_element_type=jnp.float32)
    gram = gram[0:count] + gram[count : 2 * count] + gram[2 * count : 3 * count]
    gram = gram[:, 0:count] + gram[:, count : 2 * count] + gram[:, 2 * count : 3 * count]
    payload_ref[:, basis : basis + 128] = jnp.concatenate(
        [gram, jnp.zeros((count, 128 - count), jnp.float32)], axis=1
    )


def filter_call(panel, bodies, above, below, locked_flat):
    panels = len(bodies)
    height, planes, width = bodies[0].shape
    count = planes - 8
    basis = locked_flat.shape[0]
    total = panels * width
    rows = height + 2 * HALO
    vmem = pl.BlockSpec(memory_space=pltpu.VMEM)
    return pl.pallas_call(
        lambda *refs: filter_kernel(*refs, panels=panels, height=height, count=count, width=width),
        in_specs=[pl.BlockSpec(memory_space=pltpu.SMEM)] + [vmem] * (3 * panels + 1),
        out_specs=[vmem, vmem],
        out_shape=[
            jax.ShapeDtypeStruct((count, basis + 128), jnp.float32),
            jax.ShapeDtypeStruct((height, count, width), jnp.float32),
        ],
        scratch_shapes=[
            pltpu.VMEM((rows, count, total), jnp.float32),
            pltpu.VMEM((rows, count, total), jnp.float32),
            pltpu.VMEM((rows, 9, 8, total), jnp.float32),
            pltpu.VMEM((3 * count, height * total), jnp.bfloat16),
        ],
        compiler_params=pltpu.CompilerParams(vmem_limit_bytes=48 << 20),
        name="filter",
    )(panel, *bodies, *above, *below, locked_flat)


def finish_kernel(mine_ref, other_ref, own_ref, ortho_ref, coupling_ref, factor_ref, *, vertices):
    height, count, width = own_ref.shape
    basis = coupling_ref.shape[0]
    cut = slice(basis, basis + 128)
    gram = mine_ref[:, cut] + other_ref[:, cut]
    row = lax.broadcasted_iota(jnp.int32, (count, 128), 0)
    col = lax.broadcasted_iota(jnp.int32, (count, 128), 1)
    gram = gram * (1.0 / vertices) + jnp.where(row == col, 1e-06, 0.0)
    work = gram + jnp.where(row + count == col, 1.0, 0.0)
    for j in range(count - 1):
        pivot_row = work[j : j + 1, :]
        multiplier = work[:, j : j + 1] / work[j : j + 1, j : j + 1]
        work = work - jnp.where(row > j, multiplier * pivot_row, 0.0)
    pivots = jnp.sum(jnp.where(row == col, work, 0.0), axis=1, keepdims=True)
    work = work * (1.0 / jnp.sqrt(pivots))
    upper = jnp.where(row <= col, work, 0.0)
    factor_ref[...] = upper[:, 0:count]
    inverse = work[:, count : 2 * count]
    highest = lax.Precision.HIGHEST
    coefficients = mine_ref[:, 0:basis] + other_ref[:, 0:basis]
    coupling = lax.dot_general(
        coefficients, inverse * (1.0 / math.sqrt(vertices)), (((0,), (1,)), ((), ())),
        precision=highest, preferred_element_type=jnp.float32,
    )
    coupling_ref[...] = coupling
    flat = jnp.concatenate([own_ref[r] for r in range(height)], axis=1)
    ortho = jnp.dot(inverse, flat, precision=highest, preferred_element_type=jnp.float32)
    stacked = jnp.stack([ortho[:, r * width : (r + 1) * width] for r in range(height)], axis=0)
    ortho_ref[...] = pltpu.einshape("rbc->brc", stacked)


def finish(mine, other, own, basis, vertices):
    height, count, width = own.shape
    return pl.pallas_call(
        lambda *refs: finish_kernel(*refs, vertices=float(vertices)),
        out_shape=[
            jax.ShapeDtypeStruct((count, height, width), jnp.float32),
            jax.ShapeDtypeStruct((basis, count), jnp.float32),
            jax.ShapeDtypeStruct((count, count), jnp.float32),
        ],
        name="finish",
    )(mine, other, own)


def swap(array, axis, distance):
    size = lax.axis_size(axis)
    return lax.ppermute(array, axis, [(i, i ^ distance) for i in range(size)])


def on_device(start_block, edge_weights, mass, locked):
    panels = lax.axis_size("panel")
    lines = lax.axis_size(GRID_ROWS)
    strips = lax.axis_size("strip")
    subs = lax.axis_size("sub")
    count, height, width = start_block.shape
    vertices = height * width * lines * panels
    locked_flat = locked.reshape(locked.shape[0], -1)

    down_moves = [(i, i + 1) for i in range(lines - 1)]
    up_moves = [(i + 1, i) for i in range(lines - 1)]
    body = pack(start_block, edge_weights, mass)
    bodies = [body]
    for shift in range(1, panels):
        bodies.append(
            lax.ppermute(body, "panel", [((i + shift) % panels, i) for i in range(panels)])
        )
    above = [lax.ppermute(b[height - HALO :], GRID_ROWS, down_moves) for b in bodies]
    below = [lax.ppermute(b[:HALO], GRID_ROWS, up_moves) for b in bodies]
    panel = lax.axis_index("panel").astype(jnp.int32).reshape(1)
    payload, own = filter_call(panel, bodies, above, below, locked_flat)

    rounds = [("sub", 1 << k) for k in range(subs.bit_length() - 1)]
    rounds += [("strip", 1 << k) for k in range(strips.bit_length() - 1)]
    other = jnp.zeros_like(payload)
    for index, (axis, distance) in enumerate(rounds):
        if index > 0:
            payload = payload + other
        other = swap(payload, axis, distance)
    ortho, coupling, factor = finish(payload, other, own, locked.shape[0], vertices)
    return (ortho, coupling, factor)


def solution(mesh):
    return jax.shard_map(
        on_device,
        mesh=mesh,
        in_specs=(
            P("groups", ("strip", "sub"), "panel"),
            P("groups", ("strip", "sub"), "panel"),
            P(("groups", "strip", "sub"), "panel"),
            P(("groups", "panel"), ("strip", "sub"), None),
        ),
        out_specs=(
            P("groups", ("strip", "sub"), "panel"),
            P(("groups", "panel"), None),
            P("groups", None),
        ),
        check_vma=False,
    )
```

time: 242 us -> 53.8 us (0.22)
  waiting for transfers between devices: 105 us -> 10.7 us
  starting transfers between devices: 62.3 us -> 17.3 us
  blocking collectives: 35.9 us -> 0 us
  Pallas kernels: 0 us -> 16.2 us
  other arithmetic: 14.2 us -> 0.02 us
  between operations: 14.5 us -> 0.75 us
  matrix products: 6.4 us -> 0 us
  local copies, waits for them, and re-layouts: 3.36 us -> 8.48 us
    psum x1 -> x0, waiting for transfers between devices: 51.1 us -> none  [on_device(): lax.psum(partial_coupling, ('strip', 'sub')) / math.sqrt(float(vertices))]
    ppermute x24 -> x8, starting transfers between devices: 62.3 us -> 17.3 us  [the longest x2 6.07 us: on_device(): lax.ppermute(b[height - HALO:], GRID_ROWS, down_moves)]
    ppermute x24 -> x8, waiting for transfers between devices: 53.6 us -> 10.7 us  [the longest x3 8.15 us: swap(): return lax.ppermute(array, axis, [(i, i ^ distance) for i in range(size)])]
    psum x1 -> x0, blocking collectives: 26 us -> none  [on_device(): lax.psum(block_gram(flat_whole), ('strip', 'sub')) / vertices]
    pallas_call x0 -> x3, Pallas kernels: none -> 16.2 us  [the longest x1 9.37 us: filter_call(): pl.pallas_call(lambda *refs: filter_kernel(*refs, panels=panels, height=h...]
    all_gather x1 -> x0, blocking collectives: 9.93 us -> none  [on_device(): whole_rows = lax.all_gather(filtered, 'panel', axis=2, tiled=True)]
    another operation x4 -> x0, other arithmetic: 6.03 us -> none  [the longest x3 3.59 us: on_device(): lower_factor = jnp.linalg.cholesky(gram_matrix)]
    dot_general x2 -> x0, matrix products: 5.74 us -> none  [the longest x1 5.19 us: on_device(): jnp.einsum('kn,bn->kb', locked_flat, ortho_half, preferred_element_type=j...]
  transfers between devices with their start and end apart: 25 -> 8, of which waited for: 19 -> 4; matrix products, arithmetic and copies ran while one was open for 1% -> 10% of each run, Pallas kernels for 0% -> 0%
where the time goes in v1:
time: 53.8 us; the launch traced here: 53.5 us
  starting transfers between devices  17.3 us (32%)
  Pallas kernels  16.2 us (30%)
  waiting for transfers between devices  10.7 us (20%)
  local copies, waits for them, and re-layouts  8.48 us (16%)
  between operations  0.75 us (1%)
    pallas_call x1, Pallas kernels, filter_call(): pl.pallas_call(lambda *refs: filter_kernel(*refs, panels=panels, height=h...  9.37 us
    ppermute x3, waiting for transfers between devices, swap(): return lax.ppermute(array, axis, [(i, i ^ distance) for i in range(size)])  8.15 us
    ppermute x2, starting transfers between devices, on_device(): lax.ppermute(b[height - HALO:], GRID_ROWS, down_moves)  6.07 us
    unnamed x9, local copies, waits for them, and re-layouts  5.78 us
    ppermute x3, starting transfers between devices, swap(): return lax.ppermute(array, axis, [(i, i ^ distance) for i in range(size)])  5.75 us
    pallas_call x1, Pallas kernels, finish(): pl.pallas_call(lambda *refs: finish_kernel(*refs, vertices=float(vertices...  5.07 us
    ppermute x1, starting transfers between devices, on_device(): lax.ppermute(body, 'panel', [((i + shift) % panels, i) for i in range(pan...  2.94 us
    ppermute x2, starting transfers between devices, on_device(): below = [lax.ppermute(b[:HALO], GRID_ROWS, up_moves) for b in bodies]  2.58 us
  transfers between devices with their start and end apart: 8, of which 4 were waited for; matrix products, arithmetic and copies ran while one was open for 10% of the time, Pallas kernels for 0%

profile of v1, /device:TPU:0, one launch (start us, length us, event | category | flops | bytes accessed | tf_op | source)
XLA Modules:
  0.0 53.5 jit_solution(16618121015119490994)
XLA Ops:
  0.6 1.8 %pack.1.refs_1_ = f32[16,40,128]{2,1,0:T(8,128)} custom-call(f32[32,16,128]{2,1,0:T(8,128)} %block_ref.1, f32[8,16,128]{2,1,0:T(8,128)} %weights_ref.1, f32[16,128]{1,0:T(8,128)} %mass_ref.1), custom_call_target="tpu_custom_call" | custom-call | tf_op jit(solution)/shard_map/pack/pallas_call | solution.py:29
  2.4 2.9 %collective-permute-start = (f32[16,40,128]{2,1,0:T(8,128)}, f32[16,40,128]{2,1,0:T(8,128)S(1)}, u32[]{:S(2)}, u32[]{:S(2)}) collective-permute-start(f32[16,40,128]{2,1,0:T(8,128)} %pack.1.refs_1_), channel_id=1, source_target_pairs={{2,0},{0,2},{3,1},{1,3},{6,4},{4,6},{7,5},{5,7},{10,8},{8,10},{11,... | collective-permute-start | bytes 983048 | tf_op jit(solution)/shard_map/ppermute | solution.py:246
  5.3 1.0 %fusion.1 = (f32[6,40,128]{2,1,0:T(8,128)S(1)}, f32[6,40,128]{2,1,0:T(8,128)S(1)}) fusion(f32[16,40,128]{2,1,0:T(8,128)} %pack.1.refs_1_), kind=kLoop, calls=%fused_computation.1 | loop fusion | bytes 491520 | tf_op jit(solution)/shard_map/slice | solution.py:249
  6.3 1.3 %collective-permute-start.3 = (f32[6,40,128]{2,1,0:T(8,128)S(1)}, f32[6,40,128]{2,1,0:T(8,128)S(1)}, u32[]{:S(2)}, u32[]{:S(2)}) collective-permute-start(f32[6,40,128]{2,1,0:T(8,128)S(1)} %get-tuple-element.12), channel_id=1, source_target_pairs={{1,0},{4,1},{5,4},{8,5},{9,8},{12,9},{13,12},{3,2},{6,3},{7,6},{10... | collective-permute-start | bytes 368648 | tf_op jit(solution)/shard_map/ppermute | solution.py:249
  7.6 3.0 %collective-permute-start.1 = (f32[6,40,128]{2,1,0:T(8,128)S(1)}, f32[6,40,128]{2,1,0:T(8,128)S(1)}, u32[]{:S(2)}, u32[]{:S(2)}) collective-permute-start(f32[6,40,128]{2,1,0:T(8,128)S(1)} %get-tuple-element.13), channel_id=1, source_target_pairs={{0,1},{1,4},{4,5},{5,8},{8,9},{9,12},{12,13},{2,3},{3,6},{6,7},{7,... | collective-permute-start | bytes 368648 | tf_op jit(solution)/shard_map/ppermute | solution.py:248
  10.7 2.6 %collective-permute-done.refs_2_ = f32[16,40,128]{2,1,0:T(8,128)S(1)} collective-permute-done((f32[16,40,128]{2,1,0:T(8,128)}, f32[16,40,128]{2,1,0:T(8,128)S(1)}, u32[]{:S(2)}, u32[]{:S(2)}) %collective-permute-start) | collective-permute-done | bytes 327712 | tf_op jit(solution)/shard_map/ppermute | solution.py:246
  13.3 1.3 %collective-permute-start.4 = (f32[6,40,128]{2,1,0:T(8,128)S(1)}, f32[6,40,128]{2,1,0:T(8,128)S(1)}, u32[]{:S(2)}, u32[]{:S(2)}) collective-permute-start(f32[6,40,128]{2,1,0:T(8,128)S(1)} %get-tuple-element.10), channel_id=1, source_target_pairs={{1,0},{4,1},{5,4},{8,5},{9,8},{12,9},{13,12},{3,2},{6,3},{7,6},{10... | collective-permute-start | bytes 368648 | tf_op jit(solution)/shard_map/ppermute | solution.py:249
  14.6 3.0 %collective-permute-start.2 = (f32[6,40,128]{2,1,0:T(8,128)S(1)}, f32[6,40,128]{2,1,0:T(8,128)S(1)}, u32[]{:S(2)}, u32[]{:S(2)}) collective-permute-start(f32[6,40,128]{2,1,0:T(8,128)S(1)} %get-tuple-element.11), channel_id=1, source_target_pairs={{0,1},{1,4},{4,5},{5,8},{8,9},{9,12},{12,13},{2,3},{3,6},{6,7},{7,... | collective-permute-start | bytes 368648 | tf_op jit(solution)/shard_map/ppermute | solution.py:248
  17.6 0.0 copy-start
  17.6 4.4 %copy.8 = bf16[64,8,16,256]{3,1,2,0:T(8,128)(2,1)S(1)} copy(bf16[64,8,16,256]{3,2,1,0:T(8,128)(2,1)} %bitcast.4) | data formatting | bytes 8388608
  22.1 0.0 collective-permute-done.3.refs_5_
  22.1 0.0 collective-permute-done.1.refs_3_
  22.1 0.0 collective-permute-done.4.refs_6_
  22.1 0.0 collective-permute-done.2.refs_4_
  22.1 0.0 copy-done
  22.1 9.4 %filter.1 = (f32[32,640]{1,0:T(8,128)S(1)}, f32[16,32,128]{2,1,0:T(8,128)S(1)}) custom-call(s32[1]{0:T(128)} %bitcast.refs_0_, f32[16,40,128]{2,1,0:T(8,128)S(1)} %copy-done, f32[16,40,128]{2,1,0:T(8,128)S(1)} %collective-permute-done.refs_2_, f32[6,40,128]{2,1,0:T(8,128)S(1)} %collective-permute-done.1.refs_3_, ...), custom_call_target="tpu_custom_call" | custom-call | tf_op jit(solution)/shard_map/filter/pallas_call | solution.py:163
  31.5 0.0 copy-start.1
  31.5 0.7 %copy-done.1 = f32[16,32,128]{2,1,0:T(8,128)} copy-done((f32[16,32,128]{2,1,0:T(8,128)}, f32[16,32,128]{2,1,0:T(8,128)S(1)}, u32[]{:S(2)}) %copy-start.1) | copy-done | bytes 262168
  32.2 1.4 %collective-permute-start.5 = (f32[32,640]{1,0:T(8,128)S(1)}, f32[32,640]{1,0:T(8,128)S(1)}, u32[]{:S(2)}, u32[]{:S(2)}) collective-permute-start(f32[32,640]{1,0:T(8,128)S(1)} %get-tuple-element.5), channel_id=1, source_target_pairs={{0,1},{1,0},{2,3},{3,2},{4,5},{5,4},{6,7},{7,6},{8,9},{9,8},{10,11... | collective-permute-start | bytes 245768 | tf_op jit(solution)/shard_map/ppermute | solution.py:228
  33.7 0.9 %collective-permute-done.5 = f32[32,640]{1,0:T(8,128)S(1)} collective-permute-done((f32[32,640]{1,0:T(8,128)S(1)}, f32[32,640]{1,0:T(8,128)S(1)}, u32[]{:S(2)}, u32[]{:S(2)}) %collective-permute-start.5) | collective-permute-done | bytes 81952 | tf_op jit(solution)/shard_map/ppermute | solution.py:228
  34.6 1.6 %collective-permute-start.6 = (f32[32,640]{1,0:T(8,128)S(1)}, f32[32,640]{1,0:T(8,128)S(1)}, u32[]{:S(2)}, u32[]{:S(2)}) collective-permute-start(f32[32,640]{1,0:T(8,128)S(1)} %add.6), channel_id=1, source_target_pairs={{0,4},{4,0},{8,12},{12,8},{1,5},{5,1},{9,13},{13,9},{2,6},{6,2},{1... | collective-permute-start | bytes 245768 | tf_op jit(solution)/shard_map/ppermute | solution.py:228
  36.2 3.1 %collective-permute-done.6 = f32[32,640]{1,0:T(8,128)S(1)} collective-permute-done((f32[32,640]{1,0:T(8,128)S(1)}, f32[32,640]{1,0:T(8,128)S(1)}, u32[]{:S(2)}, u32[]{:S(2)}) %collective-permute-start.6) | collective-permute-done | bytes 81952 | tf_op jit(solution)/shard_map/ppermute | solution.py:228
  39.4 0.0 copy-start.2
  39.4 2.7 %collective-permute-start.7 = (f32[32,640]{1,0:T(8,128)S(1)}, f32[32,640]{1,0:T(8,128)S(1)}, u32[]{:S(2)}, u32[]{:S(2)}) collective-permute-start(f32[32,640]{1,0:T(8,128)S(1)} %add.7.refs_0_), channel_id=1, source_target_pairs={{0,8},{4,12},{8,0},{12,4},{1,9},{5,13},{9,1},{13,5},{2,10},{6,14},... | collective-permute-start | bytes 245768 | tf_op jit(solution)/shard_map/ppermute | solution.py:228
  42.1 4.1 %collective-permute-done.7.refs_1_ = f32[32,640]{1,0:T(8,128)S(1)} collective-permute-done((f32[32,640]{1,0:T(8,128)S(1)}, f32[32,640]{1,0:T(8,128)S(1)}, u32[]{:S(2)}, u32[]{:S(2)}) %collective-permute-start.7) | collective-permute-done | bytes 81952 | tf_op jit(solution)/shard_map/ppermute | solution.py:228
  46.1 0.0 copy-start.3
  46.2 0.0 copy-done.2
  46.2 0.6 %copy-done.3 = f32[32,640]{1,0:T(8,128)} copy-done((f32[32,640]{1,0:T(8,128)}, f32[32,640]{1,0:T(8,128)S(1)}, u32[]{:S(2)}) %copy-start.3) | copy-done | bytes 81944
  46.8 5.1 %finish.1 = (f32[32,16,128]{2,1,0:T(8,128)}, f32[512,32]{1,0:T(8,128)}, f32[32,32]{1,0:T(8,128)}) custom-call(f32[32,640]{1,0:T(8,128)} %copy-done.2, f32[32,640]{1,0:T(8,128)} %copy-done.3, f32[16,32,128]{2,1,0:T(8,128)} %copy-done.1), custom_call_target="tpu_custom_call" | custom-call | tf_op jit(solution)/shard_map/finish/pallas_call | solution.py:215
  51.8 1.7 %copy.7 = f32[512,32]{0,1:T(8,128)} copy(f32[512,32]{1,0:T(8,128)} %get-tuple-element.8) | data formatting | bytes 131072 | tf_op jit(solution)/shard_map/finish/pallas_call | solution.py:215
  (3 shorter events, 0.0 us)
Async XLA Ops:
  2.4 10.9 %collective-permute-start = (f32[16,40,128]{2,1,0:T(8,128)}, f32[16,40,128]{2,1,0:T(8,128)S(1)}, u32[]{:S(2)}, u32[]{:S(2)}) collective-permute-start(f32[16,40,128]{2,1,0:T(8,128)} %pack.1.refs_1_), channel_id=1, source_target_pairs={{2,0},{0,2},{3,1},{1,3},{6,4},{4,6},{7,5},{5,7},{10,8},{8,10},{11,... | collective-permute-start | bytes 983048 | tf_op jit(solution)/shard_map/ppermute | solution.py:246
  6.3 15.7 %collective-permute-start.3 = (f32[6,40,128]{2,1,0:T(8,128)S(1)}, f32[6,40,128]{2,1,0:T(8,128)S(1)}, u32[]{:S(2)}, u32[]{:S(2)}) collective-permute-start(f32[6,40,128]{2,1,0:T(8,128)S(1)} %get-tuple-element.12), channel_id=1, source_target_pairs={{1,0},{4,1},{5,4},{8,5},{9,8},{12,9},{13,12},{3,2},{6,3},{7,6},{10... | collective-permute-start | bytes 368648 | tf_op jit(solution)/shard_map/ppermute | solution.py:249
  7.6 14.5 %collective-permute-start.1 = (f32[6,40,128]{2,1,0:T(8,128)S(1)}, f32[6,40,128]{2,1,0:T(8,128)S(1)}, u32[]{:S(2)}, u32[]{:S(2)}) collective-permute-start(f32[6,40,128]{2,1,0:T(8,128)S(1)} %get-tuple-element.13), channel_id=1, source_target_pairs={{0,1},{1,4},{4,5},{5,8},{8,9},{9,12},{12,13},{2,3},{3,6},{6,7},{7,... | collective-permute-start | bytes 368648 | tf_op jit(solution)/shard_map/ppermute | solution.py:248
  13.3 8.8 %collective-permute-start.4 = (f32[6,40,128]{2,1,0:T(8,128)S(1)}, f32[6,40,128]{2,1,0:T(8,128)S(1)}, u32[]{:S(2)}, u32[]{:S(2)}) collective-permute-start(f32[6,40,128]{2,1,0:T(8,128)S(1)} %get-tuple-element.10), channel_id=1, source_target_pairs={{1,0},{4,1},{5,4},{8,5},{9,8},{12,9},{13,12},{3,2},{6,3},{7,6},{10... | collective-permute-start | bytes 368648 | tf_op jit(solution)/shard_map/ppermute | solution.py:249
  14.6 7.5 %collective-permute-start.2 = (f32[6,40,128]{2,1,0:T(8,128)S(1)}, f32[6,40,128]{2,1,0:T(8,128)S(1)}, u32[]{:S(2)}, u32[]{:S(2)}) collective-permute-start(f32[6,40,128]{2,1,0:T(8,128)S(1)} %get-tuple-element.11), channel_id=1, source_target_pairs={{0,1},{1,4},{4,5},{5,8},{8,9},{9,12},{12,13},{2,3},{3,6},{6,7},{7,... | collective-permute-start | bytes 368648 | tf_op jit(solution)/shard_map/ppermute | solution.py:248
  17.6 4.5 %copy-start = (f32[16,40,128]{2,1,0:T(8,128)S(1)}, f32[16,40,128]{2,1,0:T(8,128)}, u32[]{:S(2)}) copy-start(f32[16,40,128]{2,1,0:T(8,128)} %pack.1.refs_1_) | copy-start | bytes 983044
  31.5 0.7 %copy-start.1 = (f32[16,32,128]{2,1,0:T(8,128)}, f32[16,32,128]{2,1,0:T(8,128)S(1)}, u32[]{:S(2)}) copy-start(f32[16,32,128]{2,1,0:T(8,128)S(1)} %get-tuple-element.6.refs_2_) | copy-start | bytes 786436
  32.2 2.4 %collective-permute-start.5 = (f32[32,640]{1,0:T(8,128)S(1)}, f32[32,640]{1,0:T(8,128)S(1)}, u32[]{:S(2)}, u32[]{:S(2)}) collective-permute-start(f32[32,640]{1,0:T(8,128)S(1)} %get-tuple-element.5), channel_id=1, source_target_pairs={{0,1},{1,0},{2,3},{3,2},{4,5},{5,4},{6,7},{7,6},{8,9},{9,8},{10,11... | collective-permute-start | bytes 245768 | tf_op jit(solution)/shard_map/ppermute | solution.py:228
  34.6 4.8 %collective-permute-start.6 = (f32[32,640]{1,0:T(8,128)S(1)}, f32[32,640]{1,0:T(8,128)S(1)}, u32[]{:S(2)}, u32[]{:S(2)}) collective-permute-start(f32[32,640]{1,0:T(8,128)S(1)} %add.6), channel_id=1, source_target_pairs={{0,4},{4,0},{8,12},{12,8},{1,5},{5,1},{9,13},{13,9},{2,6},{6,2},{1... | collective-permute-start | bytes 245768 | tf_op jit(solution)/shard_map/ppermute | solution.py:228
  39.4 6.8 %copy-start.2 = (f32[32,640]{1,0:T(8,128)}, f32[32,640]{1,0:T(8,128)S(1)}, u32[]{:S(2)}) copy-start(f32[32,640]{1,0:T(8,128)S(1)} %add.7.refs_0_) | copy-start | bytes 245764
  39.4 6.8 %collective-permute-start.7 = (f32[32,640]{1,0:T(8,128)S(1)}, f32[32,640]{1,0:T(8,128)S(1)}, u32[]{:S(2)}, u32[]{:S(2)}) collective-permute-start(f32[32,640]{1,0:T(8,128)S(1)} %add.7.refs_0_), channel_id=1, source_target_pairs={{0,8},{4,12},{8,0},{12,4},{1,9},{5,13},{9,1},{13,5},{2,10},{6,14},... | collective-permute-start | bytes 245768 | tf_op jit(solution)/shard_map/ppermute | solution.py:228
  46.1 0.6 %copy-start.3 = (f32[32,640]{1,0:T(8,128)}, f32[32,640]{1,0:T(8,128)S(1)}, u32[]{:S(2)}) copy-start(f32[32,640]{1,0:T(8,128)S(1)} %collective-permute-done.7.refs_1_) | copy-start | bytes 245764

commit v2 on v1

v2 whole, which is shorter than its diff:
```python
import math

import jax
import jax.numpy as jnp
from jax import lax
from jax.experimental import pallas as pl
from jax.experimental.pallas import tpu as pltpu
from jax.sharding import PartitionSpec as P

DEGREE = 6
CUT_LOW = 2
CUT_HIGH = 32
CENTRE = 0.5 * (CUT_HIGH + CUT_LOW)
SPREAD = 0.5 * (CUT_HIGH - CUT_LOW)
HALO = DEGREE
GRID_ROWS = ("strip", "sub")
SIDE = 8

VMEM = pl.BlockSpec(memory_space=pltpu.VMEM)
SMEM = pl.BlockSpec(memory_space=pltpu.SMEM)
HBM = pl.BlockSpec(memory_space=pltpu.HBM)


def pack_kernel(
    sub_ref, block_hbm, weights_hbm, mass_hbm, body_ref, near_ref, far_ref,
    block_ref, weights_ref, mass_ref, sems,
):
    copies = [
        pltpu.make_async_copy(block_hbm, block_ref, sems.at[0]),
        pltpu.make_async_copy(weights_hbm.at[0:4], weights_ref, sems.at[1]),
        pltpu.make_async_copy(mass_hbm, mass_ref, sems.at[2]),
    ]
    for copy in copies:
        copy.start()
    for copy in copies:
        copy.wait()
    count, height, width = block_ref.shape
    body_ref[:, 0:count, :] = pltpu.einshape("brc->rbc", block_ref[...])
    mass = mass_ref[...][None]
    side = jnp.concatenate([weights_ref[...], mass, mass, mass, mass], axis=0)
    body_ref[:, count : count + SIDE, :] = pltpu.einshape("brc->rbc", side)
    sub = sub_ref[0]
    near_ref[...] = body_ref[pl.ds((1 - sub) * (height - HALO), HALO)]
    far_ref[...] = body_ref[pl.ds(sub * (height - HALO), HALO)]


def pack(sub, start_block, edge_weights, mass):
    count, height, width = start_block.shape
    halo = jax.ShapeDtypeStruct((HALO, count + SIDE, width), jnp.float32)
    return pl.pallas_call(
        pack_kernel,
        in_specs=[SMEM, HBM, HBM, HBM],
        out_specs=[VMEM, VMEM, VMEM],
        out_shape=[jax.ShapeDtypeStruct((height, count + SIDE, width), jnp.float32), halo, halo],
        scratch_shapes=[
            pltpu.VMEM((count, height, width), jnp.float32),
            pltpu.VMEM((4, height, width), jnp.float32),
            pltpu.VMEM((height, width), jnp.float32),
            pltpu.SemaphoreType.DMA((3,)),
        ],
        compiler_params=pltpu.CompilerParams(vmem_limit_bytes=8 << 20),
        name="pack",
    )(sub, start_block, edge_weights, mass)


def filter_kernel(panel_ref, sub_ref, *refs, panels, height, count, width):
    bodies = refs[0:panels]
    nears = refs[panels : 2 * panels]
    fars = refs[2 * panels : 3 * panels]
    locked_hbm, keep_ref, send_ref, own_ref, y_even, y_odd, split, locked_ref, sem = refs[3 * panels :]
    locked_copy = pltpu.make_async_copy(locked_hbm, locked_ref, sem)
    locked_copy.start()
    total = panels * width
    rows = height + 2 * HALO
    panel = panel_ref[0]
    first_sub = sub_ref[0] == 0

    def source(row):
        if HALO <= row < HALO + height:
            parts = [b[row - HALO] for b in bodies]
        elif row < HALO:
            parts = [jnp.where(first_sub, f[row], n[row]) for n, f in zip(nears, fars)]
        else:
            at = row - HALO - height
            parts = [jnp.where(first_sub, n[at], f[at]) for n, f in zip(nears, fars)]
        return jnp.concatenate(parts, axis=1)

    lane = lax.broadcasted_iota(jnp.int32, (1, total), 1)
    column = lax.rem(lane + panel * width, total)
    not_last = (column != total - 1).astype(jnp.float32)
    not_first = (column != 0).astype(jnp.float32)

    factor = 2.0 / SPREAD

    def left(x):
        return pltpu.roll(x, total - 1, 1)

    def right(x):
        return pltpu.roll(x, 1, 1)

    weights = []
    scale = []
    for row in range(rows):
        full = source(row)
        y_even[row] = full[0:count]
        side = full[count : count + SIDE]
        mass = side[4:5]
        inside = mass > 0.0
        scale.append(jnp.where(inside, 1.0 / jnp.sqrt(jnp.where(inside, mass, 1.0)), 0.0))
        weights.append([side[d : d + 1] for d in range(4)])
    edges = []
    for row in range(rows - 1):
        s0 = scale[row]
        s1 = scale[row + 1]
        w = weights[row]
        e0 = -factor * (w[0] * (s0 * left(s0))) * not_last
        e1 = -factor * (w[1] * (s0 * s1))
        e2 = -factor * (w[2] * (s0 * left(s1))) * not_last
        e3 = -factor * (w[3] * (s0 * right(s1))) * not_first
        edges.append((e0, e1, e2, e3))
    coefficients = [None]
    for row in range(1, rows - 1):
        w = weights[row]
        v = weights[row - 1]
        total_weight = (
            ((w[0] + w[1]) + (w[2] + w[3]))
            + (right(w[0] * not_last) + v[1])
            + (right(v[2] * not_last) + left(v[3] * not_first))
        )
        diagonal = factor * (scale[row] * scale[row] * total_weight - CENTRE)
        e0, e1, e2, e3 = edges[row]
        u0, u1, u2, u3 = edges[row - 1]
        coefficients.append((diagonal, e1, u1, right(e0), right(e2), u3, e0, left(e3), u2))

    buffers = (y_even, y_odd)
    for order in range(1, DEGREE + 1):
        source_ref = buffers[(order - 1) % 2]
        target_ref = buffers[order % 2]
        for row in range(order, rows - order):
            c = coefficients[row]
            ym = source_ref[row - 1]
            y0 = source_ref[row]
            yp = source_ref[row + 1]
            out = c[0] * y0 + (c[1] * yp + c[2] * ym)
            to_left = c[3] * y0 + (c[4] * yp + c[5] * ym)
            to_right = c[6] * y0 + (c[7] * yp + c[8] * ym)
            out = out + (left(to_left) + right(to_right))
            if order == 1:
                out = 0.5 * out
            else:
                out = out - target_ref[row]
            target_ref[row] = out
    result = buffers[DEGREE % 2]

    for row in range(height):
        full = result[row + HALO]
        own_ref[row] = full[:, 0:width]
        high = full.astype(jnp.bfloat16)
        rest = full - high.astype(jnp.float32)
        middle = rest.astype(jnp.bfloat16)
        low = (rest - middle.astype(jnp.float32)).astype(jnp.bfloat16)
        stacked = jnp.concatenate([high, middle, low], axis=0)
        for t in range(panels):
            at = row * total + lax.rem(panel + t, panels) * width
            split[:, pl.ds(pl.multiple_of(at, width), width)] = stacked[:, t * width : (t + 1) * width]

    dims = (((1,), (1,)), ((), ()))
    pieces = split[...]
    gram = lax.dot_general(pieces, pieces, dims, preferred_element_type=jnp.float32)
    gram = gram[0:count] + gram[count : 2 * count] + gram[2 * count : 3 * count]
    gram = gram[:, 0:count] + gram[:, count : 2 * count] + gram[:, 2 * count : 3 * count]
    locked_copy.wait()
    products = lax.dot_general(pieces, locked_ref[...], dims, preferred_element_type=jnp.float32)
    products = products[0:count] + products[count : 2 * count] + products[2 * count : 3 * count]
    half = products.shape[1] // 2
    lower = products[:, 0:half]
    upper = products[:, half:]
    keep_ref[0:count] = jnp.where(first_sub, lower, upper)
    send_ref[0:count] = jnp.where(first_sub, upper, lower)
    dense = fold(gram, half)
    keep_ref[count : count + 8] = dense
    send_ref[count : count + 8] = dense


def fold(gram, width):
    count = gram.shape[0]
    parts = [gram[r : r + 8] for r in range(0, count, 8)]
    spare = width - count * len(parts)
    if spare > 0:
        parts.append(jnp.zeros((8, spare), jnp.float32))
    return jnp.concatenate(parts, axis=1)


def filter_call(panel, sub, bodies, nears, fars, locked_flat):
    panels = len(bodies)
    height, planes, width = bodies[0].shape
    count = planes - SIDE
    basis = locked_flat.shape[0]
    total = panels * width
    rows = height + 2 * HALO
    payload = jax.ShapeDtypeStruct((count + 8, basis // 2), jnp.float32)
    return pl.pallas_call(
        lambda *refs: filter_kernel(*refs, panels=panels, height=height, count=count, width=width),
        in_specs=[SMEM, SMEM] + [VMEM] * (3 * panels) + [HBM],
        out_specs=[VMEM] * 3,
        out_shape=[payload, payload, jax.ShapeDtypeStruct((height, count, width), jnp.float32)],
        scratch_shapes=[
            pltpu.VMEM((rows, count, total), jnp.float32),
            pltpu.VMEM((rows, count, total), jnp.float32),
            pltpu.VMEM((3 * count, height * total), jnp.bfloat16),
            pltpu.VMEM(locked_flat.shape, jnp.bfloat16),
            pltpu.SemaphoreType.DMA(()),
        ],
        compiler_params=pltpu.CompilerParams(vmem_limit_bytes=20 << 20),
        name="filter",
    )(panel, sub, *bodies, *nears, *fars, locked_flat)


def factor_kernel(gram_ref, own_ref, ortho_ref, factor_ref, inverse_ref, *, vertices):
    height, count, width = own_ref.shape
    dense = gram_ref[...]
    groups = [dense[:, g * count : (g + 1) * count] for g in range(count // 8)]
    gram = jnp.concatenate(groups, axis=0)
    gram = jnp.concatenate([gram, jnp.zeros((count, 128 - count), jnp.float32)], axis=1)
    row = lax.broadcasted_iota(jnp.int32, (count, 128), 0)
    col = lax.broadcasted_iota(jnp.int32, (count, 128), 1)
    gram = gram * (1.0 / vertices) + jnp.where(row == col, 1e-06, 0.0)
    work = gram + jnp.where(row + count == col, 1.0, 0.0)
    for j in range(count - 1):
        pivot_row = work[j : j + 1, :]
        multiplier = work[:, j : j + 1] / work[j : j + 1, j : j + 1]
        work = work - jnp.where(row > j, multiplier * pivot_row, 0.0)
    pivots = jnp.sum(jnp.where(row == col, work, 0.0), axis=1, keepdims=True)
    work = work * (1.0 / jnp.sqrt(pivots))
    factor_ref[...] = jnp.where(row <= col, work, 0.0)[:, 0:count]
    inverse = work[:, count : 2 * count]
    inverse_ref[...] = inverse
    flat = jnp.concatenate([own_ref[r] for r in range(height)], axis=1)
    ortho = jnp.dot(
        inverse, flat, precision=lax.Precision.HIGHEST, preferred_element_type=jnp.float32
    )
    stacked = jnp.stack([ortho[:, r * width : (r + 1) * width] for r in range(height)], axis=0)
    ortho_ref[...] = pltpu.einshape("rbc->brc", stacked)


def factorize(gram, own, vertices):
    height, count, width = own.shape
    square = jax.ShapeDtypeStruct((count, count), jnp.float32)
    return pl.pallas_call(
        lambda *refs: factor_kernel(*refs, vertices=float(vertices)),
        in_specs=[VMEM, VMEM],
        out_specs=[VMEM, VMEM, VMEM],
        out_shape=[jax.ShapeDtypeStruct((count, height, width), jnp.float32), square, square],
        compiler_params=pltpu.CompilerParams(vmem_limit_bytes=8 << 20),
        name="factor",
    )(gram, own)


def coupling_kernel(sub_ref, inverse_ref, mine_ref, other_ref, out_ref, *, vertices):
    first_sub = sub_ref[0] == 0
    half = mine_ref.shape[1]
    mine = mine_ref[...]
    other = other_ref[...]
    inverse = inverse_ref[...] * (1.0 / math.sqrt(vertices))
    for index, part in enumerate(
        (jnp.where(first_sub, mine, other), jnp.where(first_sub, other, mine))
    ):
        out_ref[:, index * half : (index + 1) * half] = jnp.dot(
            inverse, part, precision=lax.Precision.HIGHEST, preferred_element_type=jnp.float32
        )


def couple(sub, inverse, mine, other, vertices):
    count, half = mine.shape
    return pl.pallas_call(
        lambda *refs: coupling_kernel(*refs, vertices=float(vertices)),
        in_specs=[SMEM, VMEM, VMEM, VMEM],
        out_specs=VMEM,
        out_shape=jax.ShapeDtypeStruct((count, 2 * half), jnp.float32),
        compiler_params=pltpu.CompilerParams(vmem_limit_bytes=8 << 20),
        name="couple",
    )(sub, inverse, mine, other)


def swap(array, axis, distance):
    size = lax.axis_size(axis)
    return lax.ppermute(array, axis, [(i, i ^ distance) for i in range(size)])


def strip_sum(part):
    strips = lax.axis_size("strip")
    distance = 1
    while distance * 4 < strips or distance * 2 == strips:
        part = part + swap(part, "strip", distance)
        distance *= 2
    if distance * 4 == strips:
        one = swap(part, "strip", distance)
        two = swap(part, "strip", 2 * distance)
        three = swap(part, "strip", 3 * distance)
        part = (part + one) + (two + three)
    return part


def on_device(start_block, edge_weights, mass, locked):
    panels = lax.axis_size("panel")
    lines = lax.axis_size(GRID_ROWS)
    count, height, width = start_block.shape
    vertices = height * width * lines * panels
    panel = lax.axis_index("panel").astype(jnp.int32).reshape(1)
    sub = lax.axis_index("sub").astype(jnp.int32).reshape(1)

    body, near, far = pack(sub, start_block, edge_weights, mass)
    bodies = [body]
    for shift in range(1, panels):
        bodies.append(
            lax.ppermute(body, "panel", [((i + shift) % panels, i) for i in range(panels)])
        )
    locked_flat = locked.reshape(locked.shape[0], -1)
    across = []
    for line in range(1, lines - 1, 2):
        across += [(line, line + 1), (line + 1, line)]

    def exchange(near, far):
        return swap(near, "sub", 1), lax.ppermute(far, GRID_ROWS, across)

    halos = [exchange(near, far)]
    rest, locked_flat = lax.optimization_barrier((bodies[1:], locked_flat))
    for other in rest:
        edge = height - HALO
        halos.append(
            exchange(
                lax.dynamic_slice_in_dim(other, (1 - sub[0]) * edge, HALO, 0),
                lax.dynamic_slice_in_dim(other, sub[0] * edge, HALO, 0),
            )
        )
    keep, send, own = filter_call(
        panel, sub, [body] + list(rest), [h[0] for h in halos], [h[1] for h in halos], locked_flat
    )
    part = strip_sum(keep + swap(send, "sub", 1))
    mine = part[:count]
    other = swap(mine, "sub", 1)
    ortho, factor, inverse = factorize(part[count:, : count * count // 8], own, vertices)
    coupling = couple(sub, inverse, mine, other, vertices)
    return (ortho, jnp.transpose(coupling), factor)


def solution(mesh):
    return jax.shard_map(
        on_device,
        mesh=mesh,
        in_specs=(
            P("groups", ("strip", "sub"), "panel"),
            P("groups", ("strip", "sub"), "panel"),
            P(("groups", "strip", "sub"), "panel"),
            P(("groups", "panel"), ("strip", "sub"), None),
        ),
        out_specs=(
            P("groups", ("strip", "sub"), "panel"),
            P(("groups", "panel"), None),
            P("groups", None),
        ),
        check_vma=False,
    )
```

time: 53.8 us -> 44.7 us (0.83)
  Pallas kernels: 16.2 us -> 10.8 us
  waiting for transfers between devices: 10.7 us -> 6.06 us
  local copies, waits for them, and re-layouts: 8.48 us -> 11.1 us
  starting transfers between devices: 17.3 us -> 15.7 us
    ppermute x4 -> x2, starting transfers between devices: 8.66 us -> 1.33 us  [exchange(): return (swap(near, 'sub', 1), lax.ppermute(far, GRID_ROWS, across))]
    ppermute x3 -> x7, starting transfers between devices: 5.75 us -> 11.3 us  [swap(): return lax.ppermute(array, axis, [(i, i ^ distance) for i in range(size)])]
    unnamed x9, local copies, waits for them, and re-layouts: 5.78 us -> 11 us
    pallas_call x1, Pallas kernels: 9.37 us -> 6.03 us  [filter_call(): pl.pallas_call(lambda *refs: filter_kernel(*refs, panels=panels, height=h...]
    ppermute x3 -> x7, waiting for transfers between devices: 8.15 us -> 5.38 us  [swap(): return lax.ppermute(array, axis, [(i, i ^ distance) for i in range(size)])]
    pallas_call x2 -> x3, Pallas kernels: 6.84 us -> 4.77 us  [the longest x1 3.76 us: factorize(): pl.pallas_call(lambda *refs: factor_kernel(*refs, vertices=float(vertices...]
    ppermute x1, waiting for transfers between devices: 2.58 us -> 0.67 us  [on_device(): lax.ppermute(body, 'panel', [((i + shift) % panels, i) for i in range(pan...]
    pallas_call x1 -> x0, local copies, waits for them, and re-layouts: 1.69 us -> none  [finish(): pl.pallas_call(lambda *refs: finish_kernel(*refs, vertices=float(vertices...]
  transfers between devices with their start and end apart: 8 -> 10, of which waited for: 4 -> 5; matrix products, arithmetic and copies ran while one was open for 10% -> 14% of each run, Pallas kernels for 0% -> 8%
where the time goes in v2:
time: 44.7 us; the launch traced here: 44.3 us
  starting transfers between devices  15.7 us (35%)
  local copies, waits for them, and re-layouts  11.1 us (25%)
  Pallas kernels  10.8 us (24%)
  waiting for transfers between devices  6.06 us (14%)
  between operations  0.73 us (2%)
    ppermute x7, starting transfers between devices, swap(): return lax.ppermute(array, axis, [(i, i ^ distance) for i in range(size)])  11.3 us
    unnamed x9, local copies, waits for them, and re-layouts  11 us
    pallas_call x1, Pallas kernels, filter_call(): pl.pallas_call(lambda *refs: filter_kernel(*refs, panels=panels, height=h...  6.03 us
    ppermute x7, waiting for transfers between devices, swap(): return lax.ppermute(array, axis, [(i, i ^ distance) for i in range(size)])  5.38 us
    pallas_call x1, Pallas kernels, factorize(): pl.pallas_call(lambda *refs: factor_kernel(*refs, vertices=float(vertices...  3.76 us
    ppermute x1, starting transfers between devices, on_device(): lax.ppermute(body, 'panel', [((i + shift) % panels, i) for i in range(pan...  3 us
    ppermute x2, starting transfers between devices, exchange(): return (swap(near, 'sub', 1), lax.ppermute(far, GRID_ROWS, across))  1.33 us
  transfers between devices with their start and end apart: 10, of which 5 were waited for; matrix products, arithmetic and copies ran while one was open for 14% of the time, Pallas kernels for 8%

profile of v2, /device:TPU:0, one launch (start us, length us, event | category | flops | bytes accessed | tf_op | source)
XLA Modules:
  0.0 44.3 jit_solution(4397159330687702866)
XLA Ops:
  0.6 0.0 copy-start.1
  0.6 0.9 %copy-done.1 = f32[32,16,128]{2,1,0:T(8,128)S(1)} copy-done((f32[32,16,128]{2,1,0:T(8,128)S(1)}, f32[32,16,128]{2,1,0:T(8,128)}, u32[]{:S(2)}) %copy-start.1) | copy-done | bytes 262168
  1.6 0.0 copy-start.2
  1.6 0.8 %copy-done.2 = f32[8,16,128]{2,1,0:T(8,128)S(1)} copy-done((f32[8,16,128]{2,1,0:T(8,128)S(1)}, f32[8,16,128]{2,1,0:T(8,128)}, u32[]{:S(2)}) %copy-start.2) | copy-done | bytes 65560
  2.4 0.0 copy-start.3
  2.4 0.7 %copy-done.3 = f32[16,128]{1,0:T(8,128)S(1)} copy-done((f32[16,128]{1,0:T(8,128)S(1)}, f32[16,128]{1,0:T(8,128)}, u32[]{:S(2)}) %copy-start.3) | copy-done | bytes 8216
  3.1 0.2 pack.1
  3.3 3.0 %collective-permute-start = (f32[16,40,128]{2,1,0:T(8,128)S(1)}, f32[16,40,128]{2,1,0:T(8,128)S(1)}, u32[]{:S(2)}, u32[]{:S(2)}) collective-permute-start(f32[16,40,128]{2,1,0:T(8,128)S(1)} %get-tuple-element.14.refs_2_), channel_id=1, source_target_pairs={{2,0},{0,2},{3,1},{1,3},{6,4},{4,6},{7,5},{5,7},{10,8},{8,10},{11,... | collective-permute-start | bytes 983048 | tf_op jit(solution)/shard_map/ppermute | solution.py:316
  6.3 0.0 collective-permute-start.1
  6.3 0.7 %collective-permute-start.3 = (f32[6,40,128]{2,1,0:T(8,128)S(1)}, f32[6,40,128]{2,1,0:T(8,128)S(1)}, u32[]{:S(2)}, u32[]{:S(2)}) collective-permute-start(f32[6,40,128]{2,1,0:T(8,128)S(1)} %get-tuple-element.17), channel_id=1, source_target_pairs={{1,4},{4,1},{5,8},{8,5},{9,12},{12,9},{3,6},{6,3},{7,10},{10,7},{1... | collective-permute-start | bytes 368648 | tf_op jit(solution)/shard_map/ppermute | solution.py:324
  7.0 6.4 %copy.7 = bf16[64,8,16,256]{3,1,2,0:T(8,128)(2,1)} copy(bf16[64,8,16,256]{3,2,1,0:T(8,128)(2,1)} %bitcast.6) | data formatting | bytes 8388608
  13.4 0.7 %collective-permute-done.refs_3_ = f32[16,40,128]{2,1,0:T(8,128)S(1)} collective-permute-done((f32[16,40,128]{2,1,0:T(8,128)S(1)}, f32[16,40,128]{2,1,0:T(8,128)S(1)}, u32[]{:S(2)}, u32[]{:S(2)}) %collective-permute-start) | collective-permute-done | bytes 327712 | tf_op jit(solution)/shard_map/ppermute | solution.py:316
  14.0 0.7 %collective-permute-start.4 = (f32[6,40,128]{2,1,0:T(8,128)S(1)}, f32[6,40,128]{2,1,0:T(8,128)S(1)}, u32[]{:S(2)}, u32[]{:S(2)}) collective-permute-start(f32[6,40,128]{2,1,0:T(8,128)S(1)} %get-tuple-element.25), channel_id=1, source_target_pairs={{1,4},{4,1},{5,8},{8,5},{9,12},{12,9},{3,6},{6,3},{7,10},{10,7},{1... | collective-permute-start | bytes 368648 | tf_op jit(solution)/shard_map/ppermute | solution.py:324
  14.7 4.1 %collective-permute-start.2 = (f32[6,40,128]{2,1,0:T(8,128)S(1)}, f32[6,40,128]{2,1,0:T(8,128)S(1)}, u32[]{:S(2)}, u32[]{:S(2)}) collective-permute-start(f32[6,40,128]{2,1,0:T(8,128)S(1)} %get-tuple-element.26), channel_id=1, source_target_pairs={{0,1},{1,0},{2,3},{3,2},{4,5},{5,4},{6,7},{7,6},{8,9},{9,8},{10,11... | collective-permute-start | bytes 368648 | tf_op jit(solution)/shard_map/ppermute | solution.py:287
  18.8 0.0 collective-permute-done.1.refs_4_
  18.8 0.0 collective-permute-done.3.refs_6_
  18.8 0.0 collective-permute-done.4.refs_7_
  18.9 1.0 %collective-permute-done.2.refs_5_ = f32[6,40,128]{2,1,0:T(8,128)S(1)} collective-permute-done((f32[6,40,128]{2,1,0:T(8,128)S(1)}, f32[6,40,128]{2,1,0:T(8,128)S(1)}, u32[]{:S(2)}, u32[]{:S(2)}) %collective-permute-start.2) | collective-permute-done | bytes 122912 | tf_op jit(solution)/shard_map/ppermute | solution.py:287
  19.8 0.0 copy-start
  19.8 2.2 %copy-done = bf16[64,8,16,256]{3,1,2,0:T(8,128)(2,1)S(1)} copy-done((bf16[64,8,16,256]{3,1,2,0:T(8,128)(2,1)S(1)}, bf16[64,8,16,256]{3,1,2,0:T(8,128)(2,1)}, u32[]{:S(2)}) %copy-start) | copy-done | bytes 4194328
  22.0 6.0 %filter.1 = (f32[40,256]{1,0:T(8,128)S(1)}, f32[40,256]{1,0:T(8,128)S(1)}, f32[16,32,128]{2,1,0:T(8,128)S(1)}) custom-call(s32[1]{0:T(128)} %bitcast.refs_0_, s32[1]{0:T(128)} %bitcast.1.sub_ref.refs_1_.refs_0_, f32[16,40,128]{2,1,0:T(8,128)S(1)} %get-tuple-element.14.refs_2_, f32[16,40,128]{2,1,0:T(8,128)S(1)} %collective-permute-done.refs_3_, ...), custom_call_target="tpu_custom_call" | custom-call | tf_op jit(solution)/shard_map/filter/pallas_call | solution.py:202
  28.0 2.7 %collective-permute-start.5 = (f32[40,256]{1,0:T(8,128)S(1)}, f32[40,256]{1,0:T(8,128)S(1)}, u32[]{:S(2)}, u32[]{:S(2)}) collective-permute-start(f32[40,256]{1,0:T(8,128)S(1)} %get-tuple-element.20), channel_id=1, source_target_pairs={{0,1},{1,0},{2,3},{3,2},{4,5},{5,4},{6,7},{7,6},{8,9},{9,8},{10,11... | collective-permute-start | bytes 122888 | tf_op jit(solution)/shard_map/ppermute | solution.py:287
  30.8 0.9 %collective-permute-done.5 = f32[40,256]{1,0:T(8,128)S(1)} collective-permute-done((f32[40,256]{1,0:T(8,128)S(1)}, f32[40,256]{1,0:T(8,128)S(1)}, u32[]{:S(2)}, u32[]{:S(2)}) %collective-permute-start.5) | collective-permute-done | bytes 40992 | tf_op jit(solution)/shard_map/ppermute | solution.py:287
  31.7 2.8 %collective-permute-start.8 = (f32[40,256]{1,0:T(8,128)S(1)}, f32[40,256]{1,0:T(8,128)S(1)}, u32[]{:S(2)}, u32[]{:S(2)}) collective-permute-start(f32[40,256]{1,0:T(8,128)S(1)} %add.20), channel_id=1, source_target_pairs={{0,12},{4,8},{8,4},{12,0},{1,13},{5,9},{9,5},{13,1},{2,14},{6,10},... | collective-permute-start | bytes 122888 | tf_op jit(solution)/shard_map/ppermute | solution.py:287
  34.5 0.2 collective-permute-start.7
  34.7 1.3 %collective-permute-start.6 = (f32[40,256]{1,0:T(8,128)S(1)}, f32[40,256]{1,0:T(8,128)S(1)}, u32[]{:S(2)}, u32[]{:S(2)}) collective-permute-start(f32[40,256]{1,0:T(8,128)S(1)} %add.20), channel_id=1, source_target_pairs={{0,4},{4,0},{8,12},{12,8},{1,5},{5,1},{9,13},{13,9},{2,6},{6,2},{1... | collective-permute-start | bytes 122888 | tf_op jit(solution)/shard_map/ppermute | solution.py:287
  36.1 1.5 %collective-permute-done.8 = f32[40,256]{1,0:T(8,128)S(1)} collective-permute-done((f32[40,256]{1,0:T(8,128)S(1)}, f32[40,256]{1,0:T(8,128)S(1)}, u32[]{:S(2)}, u32[]{:S(2)}) %collective-permute-start.8) | collective-permute-done | bytes 40992 | tf_op jit(solution)/shard_map/ppermute | solution.py:287
  37.5 2.1 %collective-permute-done.7 = f32[40,256]{1,0:T(8,128)S(1)} collective-permute-done((f32[40,256]{1,0:T(8,128)S(1)}, f32[40,256]{1,0:T(8,128)S(1)}, u32[]{:S(2)}, u32[]{:S(2)}) %collective-permute-start.7) | collective-permute-done | bytes 40992 | tf_op jit(solution)/shard_map/ppermute | solution.py:287
  39.6 0.0 collective-permute-done.6
  39.6 0.1 collective-permute-start.9
  39.7 3.8 %factor.1 = (f32[32,16,128]{2,1,0:T(8,128)}, f32[32,32]{1,0:T(8,128)}, f32[32,32]{1,0:T(8,128)S(1)}) custom-call(f32[8,128]{1,0:T(8,128)S(1)} %slice.8.refs_0_, f32[16,32,128]{2,1,0:T(8,128)S(1)} %get-tuple-element.21.refs_1_), custom_call_target="tpu_custom_call" | custom-call | tf_op jit(solution)/shard_map/factor/pallas_call | solution.py:249
  43.5 0.0 collective-permute-done.9.refs_3_
  43.5 0.8 %couple.1 = f32[32,512]{1,0:T(8,128)} custom-call(s32[1]{0:T(128)} %bitcast.1.sub_ref.refs_1_.refs_0_, f32[32,32]{1,0:T(8,128)S(1)} %get-tuple-element.23.refs_1_, f32[32,256]{1,0:T(8,128)S(1)} %slice.9.refs_2_, f32[32,256]{1,0:T(8,128)S(1)} %collective-permute-done.9.refs_3_), custom_call_target="tpu_custom_call" | custom-call | tf_op jit(solution)/shard_map/couple/pallas_call | solution.py:275
  (5 shorter events, 0.0 us)
Async XLA Ops:
  0.6 1.0 %copy-start.1 = (f32[32,16,128]{2,1,0:T(8,128)S(1)}, f32[32,16,128]{2,1,0:T(8,128)}, u32[]{:S(2)}) copy-start(f32[32,16,128]{2,1,0:T(8,128)} %block_hbm.1) | copy-start | bytes 786436
  1.6 0.8 %copy-start.2 = (f32[8,16,128]{2,1,0:T(8,128)S(1)}, f32[8,16,128]{2,1,0:T(8,128)}, u32[]{:S(2)}) copy-start(f32[8,16,128]{2,1,0:T(8,128)} %weights_hbm.1) | copy-start | bytes 196612
  2.4 0.7 %copy-start.3 = (f32[16,128]{1,0:T(8,128)S(1)}, f32[16,128]{1,0:T(8,128)}, u32[]{:S(2)}) copy-start(f32[16,128]{1,0:T(8,128)} %mass_hbm.1) | copy-start | bytes 24580
  3.3 10.7 %collective-permute-start = (f32[16,40,128]{2,1,0:T(8,128)S(1)}, f32[16,40,128]{2,1,0:T(8,128)S(1)}, u32[]{:S(2)}, u32[]{:S(2)}) collective-permute-start(f32[16,40,128]{2,1,0:T(8,128)S(1)} %get-tuple-element.14.refs_2_), channel_id=1, source_target_pairs={{2,0},{0,2},{3,1},{1,3},{6,4},{4,6},{7,5},{5,7},{10,8},{8,10},{11,... | collective-permute-start | bytes 983048 | tf_op jit(solution)/shard_map/ppermute | solution.py:316
  6.3 12.5 %collective-permute-start.1 = (f32[6,40,128]{2,1,0:T(8,128)S(1)}, f32[6,40,128]{2,1,0:T(8,128)S(1)}, u32[]{:S(2)}, u32[]{:S(2)}) collective-permute-start(f32[6,40,128]{2,1,0:T(8,128)S(1)} %get-tuple-element.16), channel_id=1, source_target_pairs={{0,1},{1,0},{2,3},{3,2},{4,5},{5,4},{6,7},{7,6},{8,9},{9,8},{10,11... | collective-permute-start | bytes 368648 | tf_op jit(solution)/shard_map/ppermute | solution.py:287
  6.3 12.5 %collective-permute-start.3 = (f32[6,40,128]{2,1,0:T(8,128)S(1)}, f32[6,40,128]{2,1,0:T(8,128)S(1)}, u32[]{:S(2)}, u32[]{:S(2)}) collective-permute-start(f32[6,40,128]{2,1,0:T(8,128)S(1)} %get-tuple-element.17), channel_id=1, source_target_pairs={{1,4},{4,1},{5,8},{8,5},{9,12},{12,9},{3,6},{6,3},{7,10},{10,7},{1... | collective-permute-start | bytes 368648 | tf_op jit(solution)/shard_map/ppermute | solution.py:324
  14.0 4.8 %collective-permute-start.4 = (f32[6,40,128]{2,1,0:T(8,128)S(1)}, f32[6,40,128]{2,1,0:T(8,128)S(1)}, u32[]{:S(2)}, u32[]{:S(2)}) collective-permute-start(f32[6,40,128]{2,1,0:T(8,128)S(1)} %get-tuple-element.25), channel_id=1, source_target_pairs={{1,4},{4,1},{5,8},{8,5},{9,12},{12,9},{3,6},{6,3},{7,10},{10,7},{1... | collective-permute-start | bytes 368648 | tf_op jit(solution)/shard_map/ppermute | solution.py:324
  14.7 5.1 %collective-permute-start.2 = (f32[6,40,128]{2,1,0:T(8,128)S(1)}, f32[6,40,128]{2,1,0:T(8,128)S(1)}, u32[]{:S(2)}, u32[]{:S(2)}) collective-permute-start(f32[6,40,128]{2,1,0:T(8,128)S(1)} %get-tuple-element.26), channel_id=1, source_target_pairs={{0,1},{1,0},{2,3},{3,2},{4,5},{5,4},{6,7},{7,6},{8,9},{9,8},{10,11... | collective-permute-start | bytes 368648 | tf_op jit(solution)/shard_map/ppermute | solution.py:287
  19.8 2.2 %copy-start = (bf16[64,8,16,256]{3,1,2,0:T(8,128)(2,1)S(1)}, bf16[64,8,16,256]{3,1,2,0:T(8,128)(2,1)}, u32[]{:S(2)}) copy-start(bf16[64,8,16,256]{3,1,2,0:T(8,128)(2,1)} %copy.7) | copy-start | bytes 12582916
  28.0 3.6 %collective-permute-start.5 = (f32[40,256]{1,0:T(8,128)S(1)}, f32[40,256]{1,0:T(8,128)S(1)}, u32[]{:S(2)}, u32[]{:S(2)}) collective-permute-start(f32[40,256]{1,0:T(8,128)S(1)} %get-tuple-element.20), channel_id=1, source_target_pairs={{0,1},{1,0},{2,3},{3,2},{4,5},{5,4},{6,7},{7,6},{8,9},{9,8},{10,11... | collective-permute-start | bytes 122888 | tf_op jit(solution)/shard_map/ppermute | solution.py:287
  31.7 5.8 %collective-permute-start.8 = (f32[40,256]{1,0:T(8,128)S(1)}, f32[40,256]{1,0:T(8,128)S(1)}, u32[]{:S(2)}, u32[]{:S(2)}) collective-permute-start(f32[40,256]{1,0:T(8,128)S(1)} %add.20), channel_id=1, source_target_pairs={{0,12},{4,8},{8,4},{12,0},{1,13},{5,9},{9,5},{13,1},{2,14},{6,10},... | collective-permute-start | bytes 122888 | tf_op jit(solution)/shard_map/ppermute | solution.py:287
  34.5 5.1 %collective-permute-start.7 = (f32[40,256]{1,0:T(8,128)S(1)}, f32[40,256]{1,0:T(8,128)S(1)}, u32[]{:S(2)}, u32[]{:S(2)}) collective-permute-start(f32[40,256]{1,0:T(8,128)S(1)} %add.20), channel_id=1, source_target_pairs={{0,8},{4,12},{8,0},{12,4},{1,9},{5,13},{9,1},{13,5},{2,10},{6,14},... | collective-permute-start | bytes 122888 | tf_op jit(solution)/shard_map/ppermute | solution.py:287
  34.7 4.9 %collective-permute-start.6 = (f32[40,256]{1,0:T(8,128)S(1)}, f32[40,256]{1,0:T(8,128)S(1)}, u32[]{:S(2)}, u32[]{:S(2)}) collective-permute-start(f32[40,256]{1,0:T(8,128)S(1)} %add.20), channel_id=1, source_target_pairs={{0,4},{4,0},{8,12},{12,8},{1,5},{5,1},{9,13},{13,9},{2,6},{6,2},{1... | collective-permute-start | bytes 122888 | tf_op jit(solution)/shard_map/ppermute | solution.py:287
  39.6 3.9 %collective-permute-start.9 = (f32[32,256]{1,0:T(8,128)S(1)}, f32[32,256]{1,0:T(8,128)S(1)}, u32[]{:S(2)}, u32[]{:S(2)}) collective-permute-start(f32[32,256]{1,0:T(8,128)S(1)} %slice.9.refs_2_), channel_id=1, source_target_pairs={{0,1},{1,0},{2,3},{3,2},{4,5},{5,4},{6,7},{7,6},{8,9},{9,8},{10,11... | collective-permute-start | bytes 98312 | tf_op jit(solution)/shard_map/ppermute | solution.py:287

commit v3 on v2

--- a/solution.py
+++ b/solution.py
@@ -60,7 +60,56 @@
         ],
         compiler_params=pltpu.CompilerParams(vmem_limit_bytes=8 << 20),
         name="pack",
-    )(sub, start_block, edge_weights, mass)
+    )(sub, *[in_hbm(x) for x in (start_block, edge_weights, mass)])
+
+
+def in_hbm(array):
+    return pltpu.with_memory_space_constraint(array, pltpu.HBM)
+
+
+def relayout_kernel(locked_hbm, out_hbm, token_ref, chunks_ref, flat_ref, read_sems, write_sems):
+    chunks, size, height, width = chunks_ref.shape
+    reads = [
+        pltpu.make_async_copy(locked_hbm.at[pl.ds(i * size, size)], chunks_ref.at[i], read_sems.at[i])
+        for i in range(chunks)
+    ]
+    writes = [
+        pltpu.make_async_copy(flat_ref.at[i], out_hbm.at[pl.ds(i * size, size)], write_sems.at[i])
+        for i in range(chunks)
+    ]
+    for read in reads:
+        read.start()
+    token_ref[...] = jnp.zeros_like(token_ref)
+    for i in range(chunks):
+        reads[i].wait()
+        rows = pltpu.einshape("krc->rkc", chunks_ref[i])
+        for r in range(height):
+            flat_ref[i, :, r * width : (r + 1) * width] = rows[r]
+        writes[i].start()
+    for write in writes:
+        write.wait()
+
+
+def relayout(locked):
+    basis, height, width = locked.shape
+    chunks = max(1, basis // 64)
+    return pl.pallas_call(
+        relayout_kernel,
+        in_specs=[HBM],
+        out_specs=[HBM, VMEM],
+        out_shape=[
+            pltpu.HBM((basis, height * width), locked.dtype),
+            jax.ShapeDtypeStruct((8, 128), jnp.float32),
+        ],
+        scratch_shapes=[
+            pltpu.VMEM((chunks, basis // chunks, height, width), locked.dtype),
+            pltpu.VMEM((chunks, basis // chunks, height * width), locked.dtype),
+            pltpu.SemaphoreType.DMA((chunks,)),
+            pltpu.SemaphoreType.DMA((chunks,)),
+        ],
+        compiler_params=pltpu.CompilerParams(vmem_limit_bytes=16 << 20),
+        name="relayout",
+    )(in_hbm(locked))
 
 
 def filter_kernel(panel_ref, sub_ref, *refs, panels, height, count, width):
@@ -213,73 +262,113 @@
         ],
         compiler_params=pltpu.CompilerParams(vmem_limit_bytes=20 << 20),
         name="filter",
-    )(panel, sub, *bodies, *nears, *fars, locked_flat)
-
-
-def factor_kernel(gram_ref, own_ref, ortho_ref, factor_ref, inverse_ref, *, vertices):
-    height, count, width = own_ref.shape
+    )(panel, sub, *bodies, *nears, *fars, in_hbm(locked_flat))
+
+
+def factor_kernel(gram_ref, factor_ref, inverse_ref, *, vertices):
+    count = factor_ref.shape[0]
+    tiles = count // 8
     dense = gram_ref[...]
-    groups = [dense[:, g * count : (g + 1) * count] for g in range(count // 8)]
-    gram = jnp.concatenate(groups, axis=0)
-    gram = jnp.concatenate([gram, jnp.zeros((count, 128 - count), jnp.float32)], axis=1)
-    row = lax.broadcasted_iota(jnp.int32, (count, 128), 0)
-    col = lax.broadcasted_iota(jnp.int32, (count, 128), 1)
-    gram = gram * (1.0 / vertices) + jnp.where(row == col, 1e-06, 0.0)
-    work = gram + jnp.where(row + count == col, 1.0, 0.0)
-    for j in range(count - 1):
-        pivot_row = work[j : j + 1, :]
-        multiplier = work[:, j : j + 1] / work[j : j + 1, j : j + 1]
-        work = work - jnp.where(row > j, multiplier * pivot_row, 0.0)
-    pivots = jnp.sum(jnp.where(row == col, work, 0.0), axis=1, keepdims=True)
-    work = work * (1.0 / jnp.sqrt(pivots))
-    factor_ref[...] = jnp.where(row <= col, work, 0.0)[:, 0:count]
-    inverse = work[:, count : 2 * count]
-    inverse_ref[...] = inverse
-    flat = jnp.concatenate([own_ref[r] for r in range(height)], axis=1)
-    ortho = jnp.dot(
-        inverse, flat, precision=lax.Precision.HIGHEST, preferred_element_type=jnp.float32
-    )
-    stacked = jnp.stack([ortho[:, r * width : (r + 1) * width] for r in range(height)], axis=0)
-    ortho_ref[...] = pltpu.einshape("rbc->brc", stacked)
-
-
-def factorize(gram, own, vertices):
-    height, count, width = own.shape
+    row = lax.broadcasted_iota(jnp.int32, (8, 128), 0)
+    col = lax.broadcasted_iota(jnp.int32, (8, 128), 1)
+    blank = jnp.zeros((8, 128 - count), jnp.float32)
+
+    def fill(x):
+        return jnp.broadcast_to(x, (8, 128))
+
+    work = []
+    for t in range(tiles):
+        gram = jnp.concatenate([dense[:, t * count : (t + 1) * count], blank], axis=1)
+        at = row + 8 * t
+        gram = gram * (1.0 / vertices) + jnp.where(at == col, 1e-06, 0.0)
+        work.append(gram + jnp.where(at + count == col, 1.0, 0.0))
+    for b in range(tiles):
+        columns = {
+            (t, k): fill(work[t][:, 8 * b + k : 8 * b + k + 1])
+            for t in range(b, tiles)
+            for k in range(8)
+        }
+        pivots = jnp.ones((8, 128), jnp.float32)
+        for j in range(8):
+            pivot = fill(columns[b, j][j : j + 1])
+            pivots = jnp.where(row == j, pivot, pivots)
+            inverse = 1.0 / pivot
+            pivot_row = fill(work[b][j : j + 1])
+            entries = {k: fill(columns[b, k][j : j + 1]) for k in range(j + 1, 8)}
+            for t in range(b, tiles):
+                multiplier = columns[t, j] * inverse
+                if t == b:
+                    multiplier = jnp.where(row > j, multiplier, 0.0)
+                for k in range(j + 1, 8):
+                    columns[t, k] = columns[t, k] - multiplier * entries[k]
+                work[t] = work[t] - multiplier * pivot_row
+        work[b] = work[b] * (1.0 / jnp.sqrt(pivots))
+    for t in range(tiles):
+        upper = jnp.where(row + 8 * t <= col, work[t], 0.0)
+        factor_ref[8 * t : 8 * t + 8, :] = upper[:, 0:count]
+        inverse_ref[8 * t : 8 * t + 8, :] = work[t][:, count : 2 * count]
+
+
+def factorize(dense, count, vertices):
     square = jax.ShapeDtypeStruct((count, count), jnp.float32)
     return pl.pallas_call(
         lambda *refs: factor_kernel(*refs, vertices=float(vertices)),
-        in_specs=[VMEM, VMEM],
-        out_specs=[VMEM, VMEM, VMEM],
-        out_shape=[jax.ShapeDtypeStruct((count, height, width), jnp.float32), square, square],
+        in_specs=[VMEM],
+        out_specs=[VMEM, VMEM],
+        out_shape=[square, square],
         compiler_params=pltpu.CompilerParams(vmem_limit_bytes=8 << 20),
         name="factor",
-    )(gram, own)
-
-
-def coupling_kernel(sub_ref, inverse_ref, mine_ref, other_ref, out_ref, *, vertices):
+    )(dense)
+
+
+def finish_kernel(
+    sub_ref, inverse_ref, own_ref, mine_ref, other_ref, ortho_hbm, coupling_hbm,
+    ortho_ref, coupling_ref, sems, *, vertices,
+):
+    height, count, width = own_ref.shape
     first_sub = sub_ref[0] == 0
     half = mine_ref.shape[1]
-    mine = mine_ref[...]
+    mine = mine_ref[0:count]
     other = other_ref[...]
-    inverse = inverse_ref[...] * (1.0 / math.sqrt(vertices))
-    for index, part in enumerate(
-        (jnp.where(first_sub, mine, other), jnp.where(first_sub, other, mine))
-    ):
-        out_ref[:, index * half : (index + 1) * half] = jnp.dot(
-            inverse, part, precision=lax.Precision.HIGHEST, preferred_element_type=jnp.float32
+    inverse = inverse_ref[...]
+
+    def times(left, right):
+        return jnp.dot(
+            left, right, precision=lax.Precision.HIGHEST, preferred_element_type=jnp.float32
         )
 
-
-def couple(sub, inverse, mine, other, vertices):
-    count, half = mine.shape
+    flat = jnp.concatenate([own_ref[r] for r in range(height)], axis=1)
+    ortho = times(inverse, flat)
+    stacked = jnp.stack([ortho[:, r * width : (r + 1) * width] for r in range(height)], axis=0)
+    ortho_ref[...] = pltpu.einshape("rbc->brc", stacked)
+    ortho_copy = pltpu.make_async_copy(ortho_ref, ortho_hbm, sems.at[0])
+    ortho_copy.start()
+    inverse = inverse * (1.0 / math.sqrt(vertices))
+    coupling_ref[:, 0:half] = times(inverse, jnp.where(first_sub, mine, other))
+    coupling_ref[:, half:] = times(inverse, jnp.where(first_sub, other, mine))
+    coupling_copy = pltpu.make_async_copy(coupling_ref, coupling_hbm, sems.at[1])
+    coupling_copy.start()
+    ortho_copy.wait()
+    coupling_copy.wait()
+
+
+def finish(sub, inverse, own, mine, other, vertices):
+    height, count, width = own.shape
+    ortho = (count, height, width)
+    coupling = (count, 2 * mine.shape[1])
     return pl.pallas_call(
-        lambda *refs: coupling_kernel(*refs, vertices=float(vertices)),
-        in_specs=[SMEM, VMEM, VMEM, VMEM],
-        out_specs=VMEM,
-        out_shape=jax.ShapeDtypeStruct((count, 2 * half), jnp.float32),
+        lambda *refs: finish_kernel(*refs, vertices=float(vertices)),
+        in_specs=[SMEM, VMEM, VMEM, VMEM, VMEM],
+        out_specs=[HBM, HBM],
+        out_shape=[jax.ShapeDtypeStruct(s, jnp.float32) for s in (ortho, coupling)],
+        scratch_shapes=[
+            pltpu.VMEM(ortho, jnp.float32),
+            pltpu.VMEM(coupling, jnp.float32),
+            pltpu.SemaphoreType.DMA((2,)),
+        ],
         compiler_params=pltpu.CompilerParams(vmem_limit_bytes=8 << 20),
-        name="couple",
-    )(sub, inverse, mine, other)
+        name="finish",
+    )(sub, inverse, own, mine, other)
 
 
 def swap(array, axis, distance):
@@ -315,7 +404,7 @@
         bodies.append(
             lax.ppermute(body, "panel", [((i + shift) % panels, i) for i in range(panels)])
         )
-    locked_flat = locked.reshape(locked.shape[0], -1)
+    locked_flat, token = relayout(locked)
     across = []
     for line in range(1, lines - 1, 2):
         across += [(line, line + 1), (line + 1, line)]
@@ -324,23 +413,22 @@
         return swap(near, "sub", 1), lax.ppermute(far, GRID_ROWS, across)
 
     halos = [exchange(near, far)]
-    rest, locked_flat = lax.optimization_barrier((bodies[1:], locked_flat))
-    for other in rest:
+    zero = token[0, 0]
+    for other in bodies[1:]:
         edge = height - HALO
         halos.append(
             exchange(
-                lax.dynamic_slice_in_dim(other, (1 - sub[0]) * edge, HALO, 0),
-                lax.dynamic_slice_in_dim(other, sub[0] * edge, HALO, 0),
+                lax.dynamic_slice_in_dim(other, (1 - sub[0]) * edge, HALO, 0) + zero,
+                lax.dynamic_slice_in_dim(other, sub[0] * edge, HALO, 0) + zero,
             )
         )
     keep, send, own = filter_call(
-        panel, sub, [body] + list(rest), [h[0] for h in halos], [h[1] for h in halos], locked_flat
+        panel, sub, bodies, [h[0] for h in halos], [h[1] for h in halos], locked_flat
     )
     part = strip_sum(keep + swap(send, "sub", 1))
-    mine = part[:count]
-    other = swap(mine, "sub", 1)
-    ortho, factor, inverse = factorize(part[count:, : count * count // 8], own, vertices)
-    coupling = couple(sub, inverse, mine, other, vertices)
+    other = swap(part[:count], "sub", 1)
+    factor, inverse = factorize(part[count:, : count * count // 8], count, vertices)
+    ortho, coupling = finish(sub, inverse, own, part, other, vertices)
     return (ortho, jnp.transpose(coupling), factor)
 
 

time: 44.7 us -> 39.4 us (0.88)
  local copies, waits for them, and re-layouts: 11.1 us -> 0.52 us
  Pallas kernels: 10.8 us -> 14.2 us
  waiting for transfers between devices: 6.06 us -> 9.22 us
  starting transfers between devices: 15.7 us -> 13.9 us
  other arithmetic: 0.02 us -> 0.69 us
    unnamed x9 -> x0, local copies, waits for them, and re-layouts: 11 us -> none
    pallas_call x1 -> x2, Pallas kernels: 0.83 us -> 4.5 us  [the longest x1 3.4 us: relayout(): pl.pallas_call(relayout_kernel, in_specs=[HBM], out_specs=[HBM, VMEM], ou...]
    ppermute x1, waiting for transfers between devices: 0.67 us -> 3.11 us  [on_device(): lax.ppermute(body, 'panel', [((i + shift) % panels, i) for i in range(pan...]
    pallas_call x1, Pallas kernels: 3.76 us -> 1.41 us  [factorize(): pl.pallas_call(lambda *refs: factor_kernel(*refs, vertices=float(vertices...]
    ppermute x7, starting transfers between devices: 11.3 us -> 9.53 us  [swap(): return lax.ppermute(array, axis, [(i, i ^ distance) for i in range(size)])]
    pallas_call x1, Pallas kernels: 6.03 us -> 7.22 us  [filter_call(): pl.pallas_call(lambda *refs: filter_kernel(*refs, panels=panels, height=h...]
    pallas_call x1, Pallas kernels: 0.18 us -> 1.06 us  [pack(): pl.pallas_call(pack_kernel, in_specs=[SMEM, HBM, HBM, HBM], out_specs=[VM...]
    ppermute x7, waiting for transfers between devices: 5.38 us -> 6.1 us  [swap(): return lax.ppermute(array, axis, [(i, i ^ distance) for i in range(size)])]
  transfers between devices with their start and end apart: 10 -> 10, of which waited for: 5 -> 5; matrix products, arithmetic and copies ran while one was open for 14% -> 3% of each run, Pallas kernels for 8% -> 12%
where the time goes in v3:
time: 39.4 us; the launch traced here: 39.2 us
  Pallas kernels  14.2 us (36%)
  starting transfers between devices  13.9 us (35%)
  waiting for transfers between devices  9.22 us (23%)
  between operations  0.73 us (2%)
  other arithmetic  0.69 us (2%)
  local copies, waits for them, and re-layouts  0.52 us (1%)
    ppermute x7, starting transfers between devices, swap(): return lax.ppermute(array, axis, [(i, i ^ distance) for i in range(size)])  9.53 us
    pallas_call x1, Pallas kernels, filter_call(): pl.pallas_call(lambda *refs: filter_kernel(*refs, panels=panels, height=h...  7.22 us
    ppermute x7, waiting for transfers between devices, swap(): return lax.ppermute(array, axis, [(i, i ^ distance) for i in range(size)])  6.1 us
    pallas_call x1, Pallas kernels, relayout(): pl.pallas_call(relayout_kernel, in_specs=[HBM], out_specs=[HBM, VMEM], ou...  3.4 us
    ppermute x1, waiting for transfers between devices, on_device(): lax.ppermute(body, 'panel', [((i + shift) % panels, i) for i in range(pan...  3.11 us
    ppermute x1, starting transfers between devices, on_device(): lax.ppermute(body, 'panel', [((i + shift) % panels, i) for i in range(pan...  3 us
    pallas_call x1, Pallas kernels, factorize(): pl.pallas_call(lambda *refs: factor_kernel(*refs, vertices=float(vertices...  1.41 us
    ppermute x2, starting transfers between devices, exchange(): return (swap(near, 'sub', 1), lax.ppermute(far, GRID_ROWS, across))  1.33 us
  transfers between devices with their start and end apart: 10, of which 5 were waited for; matrix products, arithmetic and copies ran while one was open for 3% of the time, Pallas kernels for 12%

profile of v3, /device:TPU:0, one launch (start us, length us, event | category | flops | bytes accessed | tf_op | source)
XLA Modules:
  0.0 39.2 jit_solution(4737171533805962367)
XLA Ops:
  0.6 1.1 %pack.1 = (f32[16,40,128]{2,1,0:T(8,128)S(1)}, f32[6,40,128]{2,1,0:T(8,128)S(1)}, f32[6,40,128]{2,1,0:T(8,128)S(1)}) custom-call(s32[1]{0:T(128)} %bitcast.sub_ref.refs_1_.refs_0_, f32[32,16,128]{2,1,0:T(8,128)} %block_hbm.1, f32[8,16,128]{2,1,0:T(8,128)} %weights_hbm.1, f32[16,128]{1,0:T(8,128)} %mass_hbm.1), custom_call_target="tpu_custom_call" | custom-call | tf_op jit(solution)/shard_map/pack/pallas_call | solution.py:50
  1.7 3.0 %collective-permute-start = (f32[16,40,128]{2,1,0:T(8,128)S(1)}, f32[16,40,128]{2,1,0:T(8,128)S(1)}, u32[]{:S(2)}, u32[]{:S(2)}) collective-permute-start(f32[16,40,128]{2,1,0:T(8,128)S(1)} %get-tuple-element.15.refs_2_), channel_id=1, source_target_pairs={{2,0},{0,2},{3,1},{1,3},{6,4},{4,6},{7,5},{5,7},{10,8},{8,10},{11,... | collective-permute-start | bytes 983048 | tf_op jit(solution)/shard_map/ppermute | solution.py:405
  4.7 0.0 collective-permute-start.1
  4.7 0.7 %collective-permute-start.3 = (f32[6,40,128]{2,1,0:T(8,128)S(1)}, f32[6,40,128]{2,1,0:T(8,128)S(1)}, u32[]{:S(2)}, u32[]{:S(2)}) collective-permute-start(f32[6,40,128]{2,1,0:T(8,128)S(1)} %get-tuple-element.18), channel_id=1, source_target_pairs={{1,4},{4,1},{5,8},{8,5},{9,12},{12,9},{3,6},{6,3},{7,10},{10,7},{1... | collective-permute-start | bytes 368648 | tf_op jit(solution)/shard_map/ppermute | solution.py:413
  5.4 3.4 %relayout.1 = (bf16[512,4096]{1,0:T(8,128)(2,1)}, f32[8,128]{1,0:T(8,128)S(1)}) custom-call(bf16[512,16,256]{2,1,0:T(8,128)(2,1)} %locked_hbm.1), custom_call_target="tpu_custom_call" | custom-call | tf_op jit(solution)/shard_map/relayout/pallas_call | solution.py:96
  8.8 0.5 %slice.9 = f32[1,1]{1,0:T(1,128)} slice(f32[8,128]{1,0:T(8,128)S(1)} %get-tuple-element.17), slice={[0:1], [0:1]} | slice | bytes 8 | tf_op jit(solution)/shard_map/slice | solution.py:416
  9.3 3.1 %collective-permute-done.refs_3_ = f32[16,40,128]{2,1,0:T(8,128)S(1)} collective-permute-done((f32[16,40,128]{2,1,0:T(8,128)S(1)}, f32[16,40,128]{2,1,0:T(8,128)S(1)}, u32[]{:S(2)}, u32[]{:S(2)}) %collective-permute-start) | collective-permute-done | bytes 327712 | tf_op jit(solution)/shard_map/ppermute | solution.py:405
  12.4 0.7 %dynamic-slice_add_fusion = (f32[6,40,128]{2,1,0:T(8,128)S(1)}, f32[6,40,128]{2,1,0:T(8,128)S(1)}) fusion(f32[16,40,128]{2,1,0:T(8,128)S(1)} %collective-permute-done.refs_3_, s32[]{:T(128)S(6)} %select_n.7, f32[]{:T(128)} %bitcast.2, s32[]{:T(128)S(6)} %select_n.6), kind=kLoop, calls=%fused_computation | loop fusion | flops 61440 | bytes 491532 | tf_op jit(solution)/shard_map/add | solution.py:422
  13.1 0.7 %collective-permute-start.4 = (f32[6,40,128]{2,1,0:T(8,128)S(1)}, f32[6,40,128]{2,1,0:T(8,128)S(1)}, u32[]{:S(2)}, u32[]{:S(2)}) collective-permute-start(f32[6,40,128]{2,1,0:T(8,128)S(1)} %get-tuple-element.27), channel_id=1, source_target_pairs={{1,4},{4,1},{5,8},{8,5},{9,12},{12,9},{3,6},{6,3},{7,10},{10,7},{1... | collective-permute-start | bytes 368648 | tf_op jit(solution)/shard_map/ppermute | solution.py:413
  13.8 3.2 %collective-permute-start.2 = (f32[6,40,128]{2,1,0:T(8,128)S(1)}, f32[6,40,128]{2,1,0:T(8,128)S(1)}, u32[]{:S(2)}, u32[]{:S(2)}) collective-permute-start(f32[6,40,128]{2,1,0:T(8,128)S(1)} %get-tuple-element.28), channel_id=1, source_target_pairs={{0,1},{1,0},{2,3},{3,2},{4,5},{5,4},{6,7},{7,6},{8,9},{9,8},{10,11... | collective-permute-start | bytes 368648 | tf_op jit(solution)/shard_map/ppermute | solution.py:376
  17.0 0.0 collective-permute-done.1.refs_4_
  17.0 0.0 collective-permute-done.3.refs_6_
  17.0 0.0 collective-permute-done.4.refs_7_
  17.0 1.0 %collective-permute-done.2.refs_5_ = f32[6,40,128]{2,1,0:T(8,128)S(1)} collective-permute-done((f32[6,40,128]{2,1,0:T(8,128)S(1)}, f32[6,40,128]{2,1,0:T(8,128)S(1)}, u32[]{:S(2)}, u32[]{:S(2)}) %collective-permute-start.2) | collective-permute-done | bytes 122912 | tf_op jit(solution)/shard_map/ppermute | solution.py:376
  18.0 7.2 %filter.1 = (f32[40,256]{1,0:T(8,128)S(1)}, f32[40,256]{1,0:T(8,128)S(1)}, f32[16,32,128]{2,1,0:T(8,128)S(1)}) custom-call(s32[1]{0:T(128)} %bitcast.1.refs_0_, s32[1]{0:T(128)} %bitcast.sub_ref.refs_1_.refs_0_, f32[16,40,128]{2,1,0:T(8,128)S(1)} %get-tuple-element.15.refs_2_, f32[16,40,128]{2,1,0:T(8,128)S(1)} %collective-permute-done.refs_3_, ...), custom_call_target="tpu_custom_call" | custom-call | tf_op jit(solution)/shard_map/filter/pallas_call | solution.py:251
  25.2 1.6 %collective-permute-start.5 = (f32[40,256]{1,0:T(8,128)S(1)}, f32[40,256]{1,0:T(8,128)S(1)}, u32[]{:S(2)}, u32[]{:S(2)}) collective-permute-start(f32[40,256]{1,0:T(8,128)S(1)} %get-tuple-element.21), channel_id=1, source_target_pairs={{0,1},{1,0},{2,3},{3,2},{4,5},{5,4},{6,7},{7,6},{8,9},{9,8},{10,11... | collective-permute-start | bytes 122888 | tf_op jit(solution)/shard_map/ppermute | solution.py:376
  26.8 0.9 %collective-permute-done.5 = f32[40,256]{1,0:T(8,128)S(1)} collective-permute-done((f32[40,256]{1,0:T(8,128)S(1)}, f32[40,256]{1,0:T(8,128)S(1)}, u32[]{:S(2)}, u32[]{:S(2)}) %collective-permute-start.5) | collective-permute-done | bytes 40992 | tf_op jit(solution)/shard_map/ppermute | solution.py:376
  27.7 4.0 %collective-permute-start.8 = (f32[40,256]{1,0:T(8,128)S(1)}, f32[40,256]{1,0:T(8,128)S(1)}, u32[]{:S(2)}, u32[]{:S(2)}) collective-permute-start(f32[40,256]{1,0:T(8,128)S(1)} %add.33), channel_id=1, source_target_pairs={{0,12},{4,8},{8,4},{12,0},{1,13},{5,9},{9,5},{13,1},{2,14},{6,10},... | collective-permute-start | bytes 122888 | tf_op jit(solution)/shard_map/ppermute | solution.py:376
  31.7 0.0 collective-permute-start.7
  31.7 0.6 %collective-permute-start.6 = (f32[40,256]{1,0:T(8,128)S(1)}, f32[40,256]{1,0:T(8,128)S(1)}, u32[]{:S(2)}, u32[]{:S(2)}) collective-permute-start(f32[40,256]{1,0:T(8,128)S(1)} %add.33), channel_id=1, source_target_pairs={{0,4},{4,0},{8,12},{12,8},{1,5},{5,1},{9,13},{13,9},{2,6},{6,2},{1... | collective-permute-start | bytes 122888 | tf_op jit(solution)/shard_map/ppermute | solution.py:376
  32.3 1.4 %collective-permute-done.8 = f32[40,256]{1,0:T(8,128)S(1)} collective-permute-done((f32[40,256]{1,0:T(8,128)S(1)}, f32[40,256]{1,0:T(8,128)S(1)}, u32[]{:S(2)}, u32[]{:S(2)}) %collective-permute-start.8) | collective-permute-done | bytes 40992 | tf_op jit(solution)/shard_map/ppermute | solution.py:376
  33.7 2.9 %collective-permute-done.7 = f32[40,256]{1,0:T(8,128)S(1)} collective-permute-done((f32[40,256]{1,0:T(8,128)S(1)}, f32[40,256]{1,0:T(8,128)S(1)}, u32[]{:S(2)}, u32[]{:S(2)}) %collective-permute-start.7) | collective-permute-done | bytes 40992 | tf_op jit(solution)/shard_map/ppermute | solution.py:376
  36.6 0.0 collective-permute-done.6
  36.6 0.1 collective-permute-start.9
  36.7 1.4 %factor.1 = (f32[32,32]{1,0:T(8,128)}, f32[32,32]{1,0:T(8,128)S(1)}) custom-call(f32[8,128]{1,0:T(8,128)S(1)} %slice.12.refs_0_), custom_call_target="tpu_custom_call" | custom-call | tf_op jit(solution)/shard_map/factor/pallas_call | solution.py:314
  38.1 0.0 collective-permute-done.9.refs_4_
  38.1 1.1 %finish.1 = (f32[32,16,128]{2,1,0:T(8,128)}, f32[32,512]{1,0:T(8,128)}) custom-call(s32[1]{0:T(128)} %bitcast.sub_ref.refs_1_.refs_0_, f32[32,32]{1,0:T(8,128)S(1)} %get-tuple-element.22.refs_1_, f32[16,32,128]{2,1,0:T(8,128)S(1)} %get-tuple-element.23.refs_2_, f32[40,256]{1,0:T(8,128)S(1)} %add_add_fusion.refs_3_, f32[32,256]{1,0:T(8,128)S(1)} %collective-permute-done.9.refs_4_), custom_call_target="tpu_custom_call" | custom-call | tf_op jit(solution)/shard_map/finish/pallas_call | solution.py:359
  (4 shorter events, 0.0 us)
Async XLA Ops:
  1.7 10.7 %collective-permute-start = (f32[16,40,128]{2,1,0:T(8,128)S(1)}, f32[16,40,128]{2,1,0:T(8,128)S(1)}, u32[]{:S(2)}, u32[]{:S(2)}) collective-permute-start(f32[16,40,128]{2,1,0:T(8,128)S(1)} %get-tuple-element.15.refs_2_), channel_id=1, source_target_pairs={{2,0},{0,2},{3,1},{1,3},{6,4},{4,6},{7,5},{5,7},{10,8},{8,10},{11,... | collective-permute-start | bytes 983048 | tf_op jit(solution)/shard_map/ppermute | solution.py:405
  4.7 12.3 %collective-permute-start.1 = (f32[6,40,128]{2,1,0:T(8,128)S(1)}, f32[6,40,128]{2,1,0:T(8,128)S(1)}, u32[]{:S(2)}, u32[]{:S(2)}) collective-permute-start(f32[6,40,128]{2,1,0:T(8,128)S(1)} %get-tuple-element.16), channel_id=1, source_target_pairs={{0,1},{1,0},{2,3},{3,2},{4,5},{5,4},{6,7},{7,6},{8,9},{9,8},{10,11... | collective-permute-start | bytes 368648 | tf_op jit(solution)/shard_map/ppermute | solution.py:376
  4.7 12.3 %collective-permute-start.3 = (f32[6,40,128]{2,1,0:T(8,128)S(1)}, f32[6,40,128]{2,1,0:T(8,128)S(1)}, u32[]{:S(2)}, u32[]{:S(2)}) collective-permute-start(f32[6,40,128]{2,1,0:T(8,128)S(1)} %get-tuple-element.18), channel_id=1, source_target_pairs={{1,4},{4,1},{5,8},{8,5},{9,12},{12,9},{3,6},{6,3},{7,10},{10,7},{1... | collective-permute-start | bytes 368648 | tf_op jit(solution)/shard_map/ppermute | solution.py:413
  13.1 3.9 %collective-permute-start.4 = (f32[6,40,128]{2,1,0:T(8,128)S(1)}, f32[6,40,128]{2,1,0:T(8,128)S(1)}, u32[]{:S(2)}, u32[]{:S(2)}) collective-permute-start(f32[6,40,128]{2,1,0:T(8,128)S(1)} %get-tuple-element.27), channel_id=1, source_target_pairs={{1,4},{4,1},{5,8},{8,5},{9,12},{12,9},{3,6},{6,3},{7,10},{10,7},{1... | collective-permute-start | bytes 368648 | tf_op jit(solution)/shard_map/ppermute | solution.py:413
  13.8 4.2 %collective-permute-start.2 = (f32[6,40,128]{2,1,0:T(8,128)S(1)}, f32[6,40,128]{2,1,0:T(8,128)S(1)}, u32[]{:S(2)}, u32[]{:S(2)}) collective-permute-start(f32[6,40,128]{2,1,0:T(8,128)S(1)} %get-tuple-element.28), channel_id=1, source_target_pairs={{0,1},{1,0},{2,3},{3,2},{4,5},{5,4},{6,7},{7,6},{8,9},{9,8},{10,11... | collective-permute-start | bytes 368648 | tf_op jit(solution)/shard_map/ppermute | solution.py:376
  25.2 2.4 %collective-permute-start.5 = (f32[40,256]{1,0:T(8,128)S(1)}, f32[40,256]{1,0:T(8,128)S(1)}, u32[]{:S(2)}, u32[]{:S(2)}) collective-permute-start(f32[40,256]{1,0:T(8,128)S(1)} %get-tuple-element.21), channel_id=1, source_target_pairs={{0,1},{1,0},{2,3},{3,2},{4,5},{5,4},{6,7},{7,6},{8,9},{9,8},{10,11... | collective-permute-start | bytes 122888 | tf_op jit(solution)/shard_map/ppermute | solution.py:376
  27.7 6.0 %collective-permute-start.8 = (f32[40,256]{1,0:T(8,128)S(1)}, f32[40,256]{1,0:T(8,128)S(1)}, u32[]{:S(2)}, u32[]{:S(2)}) collective-permute-start(f32[40,256]{1,0:T(8,128)S(1)} %add.33), channel_id=1, source_target_pairs={{0,12},{4,8},{8,4},{12,0},{1,13},{5,9},{9,5},{13,1},{2,14},{6,10},... | collective-permute-start | bytes 122888 | tf_op jit(solution)/shard_map/ppermute | solution.py:376
  31.7 4.9 %collective-permute-start.7 = (f32[40,256]{1,0:T(8,128)S(1)}, f32[40,256]{1,0:T(8,128)S(1)}, u32[]{:S(2)}, u32[]{:S(2)}) collective-permute-start(f32[40,256]{1,0:T(8,128)S(1)} %add.33), channel_id=1, source_target_pairs={{0,8},{4,12},{8,0},{12,4},{1,9},{5,13},{9,1},{13,5},{2,10},{6,14},... | collective-permute-start | bytes 122888 | tf_op jit(solution)/shard_map/ppermute | solution.py:376
  31.7 4.9 %collective-permute-start.6 = (f32[40,256]{1,0:T(8,128)S(1)}, f32[40,256]{1,0:T(8,128)S(1)}, u32[]{:S(2)}, u32[]{:S(2)}) collective-permute-start(f32[40,256]{1,0:T(8,128)S(1)} %add.33), channel_id=1, source_target_pairs={{0,4},{4,0},{8,12},{12,8},{1,5},{5,1},{9,13},{13,9},{2,6},{6,2},{1... | collective-permute-start | bytes 122888 | tf_op jit(solution)/shard_map/ppermute | solution.py:376
  36.6 1.5 %collective-permute-start.9 = (f32[32,256]{1,0:T(8,128)S(1)}, f32[32,256]{1,0:T(8,128)S(1)}, u32[]{:S(2)}, u32[]{:S(2)}) collective-permute-start(f32[32,256]{1,0:T(8,128)S(1)} %slice.13), channel_id=1, source_target_pairs={{0,1},{1,0},{2,3},{3,2},{4,5},{5,4},{6,7},{7,6},{8,9},{9,8},{10,11... | collective-permute-start | bytes 98312 | tf_op jit(solution)/shard_map/ppermute | solution.py:376

commit v4 on v3

--- a/solution.py
+++ b/solution.py
@@ -67,27 +67,23 @@
     return pltpu.with_memory_space_constraint(array, pltpu.HBM)
 
 
-def relayout_kernel(locked_hbm, out_hbm, token_ref, chunks_ref, flat_ref, read_sems, write_sems):
+def in_vmem(array):
+    return pltpu.with_memory_space_constraint(array, pltpu.VMEM)
+
+
+def relayout_kernel(locked_hbm, flat_ref, chunks_ref, sems):
     chunks, size, height, width = chunks_ref.shape
-    reads = [
-        pltpu.make_async_copy(locked_hbm.at[pl.ds(i * size, size)], chunks_ref.at[i], read_sems.at[i])
+    copies = [
+        pltpu.make_async_copy(locked_hbm.at[pl.ds(i * size, size)], chunks_ref.at[i], sems.at[i])
         for i in range(chunks)
     ]
-    writes = [
-        pltpu.make_async_copy(flat_ref.at[i], out_hbm.at[pl.ds(i * size, size)], write_sems.at[i])
-        for i in range(chunks)
-    ]
-    for read in reads:
-        read.start()
-    token_ref[...] = jnp.zeros_like(token_ref)
+    for copy in copies:
+        copy.start()
     for i in range(chunks):
-        reads[i].wait()
+        copies[i].wait()
         rows = pltpu.einshape("krc->rkc", chunks_ref[i])
         for r in range(height):
-            flat_ref[i, :, r * width : (r + 1) * width] = rows[r]
-        writes[i].start()
-    for write in writes:
-        write.wait()
+            flat_ref[pl.ds(i * size, size), r * width : (r + 1) * width] = rows[r]
 
 
 def relayout(locked):
@@ -96,18 +92,13 @@
     return pl.pallas_call(
         relayout_kernel,
         in_specs=[HBM],
-        out_specs=[HBM, VMEM],
-        out_shape=[
-            pltpu.HBM((basis, height * width), locked.dtype),
-            jax.ShapeDtypeStruct((8, 128), jnp.float32),
-        ],
+        out_specs=VMEM,
+        out_shape=pltpu.VMEM((basis, height * width), locked.dtype),
         scratch_shapes=[
             pltpu.VMEM((chunks, basis // chunks, height, width), locked.dtype),
-            pltpu.VMEM((chunks, basis // chunks, height * width), locked.dtype),
-            pltpu.SemaphoreType.DMA((chunks,)),
             pltpu.SemaphoreType.DMA((chunks,)),
         ],
-        compiler_params=pltpu.CompilerParams(vmem_limit_bytes=16 << 20),
+        compiler_params=pltpu.CompilerParams(vmem_limit_bytes=12 << 20),
         name="relayout",
     )(in_hbm(locked))
 
@@ -116,9 +107,7 @@
     bodies = refs[0:panels]
     nears = refs[panels : 2 * panels]
     fars = refs[2 * panels : 3 * panels]
-    locked_hbm, keep_ref, send_ref, own_ref, y_even, y_odd, split, locked_ref, sem = refs[3 * panels :]
-    locked_copy = pltpu.make_async_copy(locked_hbm, locked_ref, sem)
-    locked_copy.start()
+    locked_ref, keep_ref, send_ref, own_ref, y_even, y_odd, split = refs[3 * panels :]
     total = panels * width
     rows = height + 2 * HALO
     panel = panel_ref[0]
@@ -218,7 +207,6 @@
     gram = lax.dot_general(pieces, pieces, dims, preferred_element_type=jnp.float32)
     gram = gram[0:count] + gram[count : 2 * count] + gram[2 * count : 3 * count]
     gram = gram[:, 0:count] + gram[:, count : 2 * count] + gram[:, 2 * count : 3 * count]
-    locked_copy.wait()
     products = lax.dot_general(pieces, locked_ref[...], dims, preferred_element_type=jnp.float32)
     products = products[0:count] + products[count : 2 * count] + products[2 * count : 3 * count]
     half = products.shape[1] // 2
@@ -250,19 +238,17 @@
     payload = jax.ShapeDtypeStruct((count + 8, basis // 2), jnp.float32)
     return pl.pallas_call(
         lambda *refs: filter_kernel(*refs, panels=panels, height=height, count=count, width=width),
-        in_specs=[SMEM, SMEM] + [VMEM] * (3 * panels) + [HBM],
+        in_specs=[SMEM, SMEM] + [VMEM] * (3 * panels + 1),
         out_specs=[VMEM] * 3,
         out_shape=[payload, payload, jax.ShapeDtypeStruct((height, count, width), jnp.float32)],
         scratch_shapes=[
             pltpu.VMEM((rows, count, total), jnp.float32),
             pltpu.VMEM((rows, count, total), jnp.float32),
             pltpu.VMEM((3 * count, height * total), jnp.bfloat16),
-            pltpu.VMEM(locked_flat.shape, jnp.bfloat16),
-            pltpu.SemaphoreType.DMA(()),
         ],
         compiler_params=pltpu.CompilerParams(vmem_limit_bytes=20 << 20),
         name="filter",
-    )(panel, sub, *bodies, *nears, *fars, in_hbm(locked_flat))
+    )(panel, sub, *bodies, *nears, *fars, in_vmem(locked_flat))
 
 
 def factor_kernel(gram_ref, factor_ref, inverse_ref, *, vertices):
@@ -404,7 +390,7 @@
         bodies.append(
             lax.ppermute(body, "panel", [((i + shift) % panels, i) for i in range(panels)])
         )
-    locked_flat, token = relayout(locked)
+    locked_flat = relayout(locked)
     across = []
     for line in range(1, lines - 1, 2):
         across += [(line, line + 1), (line + 1, line)]
@@ -413,13 +399,12 @@
         return swap(near, "sub", 1), lax.ppermute(far, GRID_ROWS, across)
 
     halos = [exchange(near, far)]
-    zero = token[0, 0]
     for other in bodies[1:]:
         edge = height - HALO
         halos.append(
             exchange(
-                lax.dynamic_slice_in_dim(other, (1 - sub[0]) * edge, HALO, 0) + zero,
-                lax.dynamic_slice_in_dim(other, sub[0] * edge, HALO, 0) + zero,
+                lax.dynamic_slice_in_dim(other, (1 - sub[0]) * edge, HALO, 0),
+                lax.dynamic_slice_in_dim(other, sub[0] * edge, HALO, 0),
             )
         )
     keep, send, own = filter_call(

time: 39.4 us -> 36.6 us (0.929)
  Pallas kernels: 14.2 us -> 11 us
  waiting for transfers between devices: 9.22 us -> 12.4 us
  starting transfers between devices: 13.9 us -> 12.2 us
  other arithmetic: 0.69 us -> 0.02 us
  local copies, waits for them, and re-layouts: 0.52 us -> 0.03 us
    ppermute x1, waiting for transfers between devices: 3.11 us -> 7.03 us  [on_device(): lax.ppermute(body, 'panel', [((i + shift) % panels, i) for i in range(pan...]
    pallas_call x1, Pallas kernels: 7.22 us -> 5.11 us  [filter_call(): pl.pallas_call(lambda *refs: filter_kernel(*refs, panels=panels, height=h...]
    ppermute x7, starting transfers between devices: 9.53 us -> 7.84 us  [swap(): return lax.ppermute(array, axis, [(i, i ^ distance) for i in range(size)])]
    pallas_call x1, Pallas kernels: 3.4 us -> 2.34 us  [relayout(): pl.pallas_call(relayout_kernel, in_specs=[HBM], out_specs=VMEM, out_shape...]
    ppermute x7, waiting for transfers between devices: 6.1 us -> 5.39 us  [swap(): return lax.ppermute(array, axis, [(i, i ^ distance) for i in range(size)])]
    add x1 -> x0, other arithmetic: 0.67 us -> none  [on_device(): lax.dynamic_slice_in_dim(other, sub[0] * edge, HALO, 0) + zero]
    slice x1 -> x0, local copies, waits for them, and re-layouts: 0.51 us -> none  [on_device(): zero = token[0, 0]]
  transfers between devices with their start and end apart: 10 -> 10, of which waited for: 5 -> 4; matrix products, arithmetic and copies ran while one was open for 3% -> 0% of each run, Pallas kernels for 12% -> 10%
where the time goes in v4:
time: 36.6 us; the launch traced here: 36.4 us
  waiting for transfers between devices  12.4 us (34%)
  starting transfers between devices  12.2 us (33%)
  Pallas kernels  11 us (30%)
  between operations  0.74 us (2%)
    ppermute x7, starting transfers between devices, swap(): return lax.ppermute(array, axis, [(i, i ^ distance) for i in range(size)])  7.84 us
    ppermute x1, waiting for transfers between devices, on_device(): lax.ppermute(body, 'panel', [((i + shift) % panels, i) for i in range(pan...  7.03 us
    ppermute x7, waiting for transfers between devices, swap(): return lax.ppermute(array, axis, [(i, i ^ distance) for i in range(size)])  5.39 us
    pallas_call x1, Pallas kernels, filter_call(): pl.pallas_call(lambda *refs: filter_kernel(*refs, panels=panels, height=h...  5.11 us
    ppermute x1, starting transfers between devices, on_device(): lax.ppermute(body, 'panel', [((i + shift) % panels, i) for i in range(pan...  3 us
    pallas_call x1, Pallas kernels, relayout(): pl.pallas_call(relayout_kernel, in_specs=[HBM], out_specs=VMEM, out_shape...  2.34 us
    pallas_call x1, Pallas kernels, factorize(): pl.pallas_call(lambda *refs: factor_kernel(*refs, vertices=float(vertices...  1.41 us
    ppermute x2, starting transfers between devices, exchange(): return (swap(near, 'sub', 1), lax.ppermute(far, GRID_ROWS, across))  1.33 us
  transfers between devices with their start and end apart: 10, of which 4 were waited for; matrix products, arithmetic and copies ran while one was open for 0% of the time, Pallas kernels for 10%

profile of v4, /device:TPU:0, one launch (start us, length us, event | category | flops | bytes accessed | tf_op | source)
XLA Modules:
  0.0 36.4 jit_solution(12885676743229849199)
XLA Ops:
  0.6 1.1 %pack.1 = (f32[16,40,128]{2,1,0:T(8,128)S(1)}, f32[6,40,128]{2,1,0:T(8,128)S(1)}, f32[6,40,128]{2,1,0:T(8,128)S(1)}) custom-call(s32[1]{0:T(128)} %bitcast.sub_ref.refs_1_.refs_0_, f32[32,16,128]{2,1,0:T(8,128)} %block_hbm.1, f32[8,16,128]{2,1,0:T(8,128)} %weights_hbm.1, f32[16,128]{1,0:T(8,128)} %mass_hbm.1), custom_call_target="tpu_custom_call" | custom-call | tf_op jit(solution)/shard_map/pack/pallas_call | solution.py:50
  1.7 3.0 %collective-permute-start = (f32[16,40,128]{2,1,0:T(8,128)S(1)}, f32[16,40,128]{2,1,0:T(8,128)S(1)}, u32[]{:S(2)}, u32[]{:S(2)}) collective-permute-start(f32[16,40,128]{2,1,0:T(8,128)S(1)} %get-tuple-element.13.refs_2_), channel_id=1, source_target_pairs={{2,0},{0,2},{3,1},{1,3},{6,4},{4,6},{7,5},{5,7},{10,8},{8,10},{11,... | collective-permute-start | bytes 983048 | tf_op jit(solution)/shard_map/ppermute | solution.py:391
  4.7 0.0 collective-permute-start.1
  4.7 0.7 %collective-permute-start.3 = (f32[6,40,128]{2,1,0:T(8,128)S(1)}, f32[6,40,128]{2,1,0:T(8,128)S(1)}, u32[]{:S(2)}, u32[]{:S(2)}) collective-permute-start(f32[6,40,128]{2,1,0:T(8,128)S(1)} %get-tuple-element.15), channel_id=1, source_target_pairs={{1,4},{4,1},{5,8},{8,5},{9,12},{12,9},{3,6},{6,3},{7,10},{10,7},{1... | collective-permute-start | bytes 368648 | tf_op jit(solution)/shard_map/ppermute | solution.py:399
  5.4 7.0 %collective-permute-done.refs_3_ = f32[16,40,128]{2,1,0:T(8,128)S(1)} collective-permute-done((f32[16,40,128]{2,1,0:T(8,128)S(1)}, f32[16,40,128]{2,1,0:T(8,128)S(1)}, u32[]{:S(2)}, u32[]{:S(2)}) %collective-permute-start) | collective-permute-done | bytes 327712 | tf_op jit(solution)/shard_map/ppermute | solution.py:391
  12.4 0.7 %collective-permute-start.4 = (f32[6,40,128]{2,1,0:T(8,128)S(1)}, f32[6,40,128]{2,1,0:T(8,128)S(1)}, u32[]{:S(2)}, u32[]{:S(2)}) collective-permute-start(f32[6,40,128]{2,1,0:T(8,128)S(1)} %get-tuple-element.23), channel_id=1, source_target_pairs={{1,4},{4,1},{5,8},{8,5},{9,12},{12,9},{3,6},{6,3},{7,10},{10,7},{1... | collective-permute-start | bytes 368648 | tf_op jit(solution)/shard_map/ppermute | solution.py:399
  13.1 3.2 %collective-permute-start.2 = (f32[6,40,128]{2,1,0:T(8,128)S(1)}, f32[6,40,128]{2,1,0:T(8,128)S(1)}, u32[]{:S(2)}, u32[]{:S(2)}) collective-permute-start(f32[6,40,128]{2,1,0:T(8,128)S(1)} %get-tuple-element.24), channel_id=1, source_target_pairs={{0,1},{1,0},{2,3},{3,2},{4,5},{5,4},{6,7},{7,6},{8,9},{9,8},{10,11... | collective-permute-start | bytes 368648 | tf_op jit(solution)/shard_map/ppermute | solution.py:362
  16.4 2.3 %relayout.1.refs_8_ = bf16[512,4096]{1,0:T(8,128)(2,1)S(1)} custom-call(bf16[512,16,256]{2,1,0:T(8,128)(2,1)} %locked_hbm.1), custom_call_target="tpu_custom_call" | custom-call | tf_op jit(solution)/shard_map/relayout/pallas_call | solution.py:92
  18.7 0.0 collective-permute-done.1.refs_4_
  18.7 0.0 collective-permute-done.3.refs_6_
  18.7 0.0 collective-permute-done.4.refs_7_
  18.7 0.0 collective-permute-done.2.refs_5_
  18.8 5.1 %filter.1 = (f32[40,256]{1,0:T(8,128)S(1)}, f32[40,256]{1,0:T(8,128)S(1)}, f32[16,32,128]{2,1,0:T(8,128)S(1)}) custom-call(s32[1]{0:T(128)} %bitcast.1.refs_0_, s32[1]{0:T(128)} %bitcast.sub_ref.refs_1_.refs_0_, f32[16,40,128]{2,1,0:T(8,128)S(1)} %get-tuple-element.13.refs_2_, f32[16,40,128]{2,1,0:T(8,128)S(1)} %collective-permute-done.refs_3_, ...), custom_call_target="tpu_custom_call" | custom-call | tf_op jit(solution)/shard_map/filter/pallas_call | solution.py:239
  23.9 0.1 collective-permute-start.5
  24.0 1.1 %collective-permute-done.5 = f32[40,256]{1,0:T(8,128)S(1)} collective-permute-done((f32[40,256]{1,0:T(8,128)S(1)}, f32[40,256]{1,0:T(8,128)S(1)}, u32[]{:S(2)}, u32[]{:S(2)}) %collective-permute-start.5) | collective-permute-done | bytes 40992 | tf_op jit(solution)/shard_map/ppermute | solution.py:362
  25.1 3.7 %collective-permute-start.8 = (f32[40,256]{1,0:T(8,128)S(1)}, f32[40,256]{1,0:T(8,128)S(1)}, u32[]{:S(2)}, u32[]{:S(2)}) collective-permute-start(f32[40,256]{1,0:T(8,128)S(1)} %add.20), channel_id=1, source_target_pairs={{0,12},{4,8},{8,4},{12,0},{1,13},{5,9},{9,5},{13,1},{2,14},{6,10},... | collective-permute-start | bytes 122888 | tf_op jit(solution)/shard_map/ppermute | solution.py:362
  28.9 0.0 collective-permute-start.7
  28.9 0.7 %collective-permute-start.6 = (f32[40,256]{1,0:T(8,128)S(1)}, f32[40,256]{1,0:T(8,128)S(1)}, u32[]{:S(2)}, u32[]{:S(2)}) collective-permute-start(f32[40,256]{1,0:T(8,128)S(1)} %add.20), channel_id=1, source_target_pairs={{0,4},{4,0},{8,12},{12,8},{1,5},{5,1},{9,13},{13,9},{2,6},{6,2},{1... | collective-permute-start | bytes 122888 | tf_op jit(solution)/shard_map/ppermute | solution.py:362
  29.5 1.5 %collective-permute-done.8 = f32[40,256]{1,0:T(8,128)S(1)} collective-permute-done((f32[40,256]{1,0:T(8,128)S(1)}, f32[40,256]{1,0:T(8,128)S(1)}, u32[]{:S(2)}, u32[]{:S(2)}) %collective-permute-start.8) | collective-permute-done | bytes 40992 | tf_op jit(solution)/shard_map/ppermute | solution.py:362
  31.0 2.8 %collective-permute-done.7 = f32[40,256]{1,0:T(8,128)S(1)} collective-permute-done((f32[40,256]{1,0:T(8,128)S(1)}, f32[40,256]{1,0:T(8,128)S(1)}, u32[]{:S(2)}, u32[]{:S(2)}) %collective-permute-start.7) | collective-permute-done | bytes 40992 | tf_op jit(solution)/shard_map/ppermute | solution.py:362
  33.8 0.0 collective-permute-done.6
  33.8 0.1 collective-permute-start.9
  33.9 1.4 %factor.1 = (f32[32,32]{1,0:T(8,128)}, f32[32,32]{1,0:T(8,128)S(1)}) custom-call(f32[8,128]{1,0:T(8,128)S(1)} %slice.8.refs_0_), custom_call_target="tpu_custom_call" | custom-call | tf_op jit(solution)/shard_map/factor/pallas_call | solution.py:300
  35.3 0.0 collective-permute-done.9.refs_4_
  35.3 1.1 %finish.1 = (f32[32,16,128]{2,1,0:T(8,128)}, f32[32,512]{1,0:T(8,128)}) custom-call(s32[1]{0:T(128)} %bitcast.sub_ref.refs_1_.refs_0_, f32[32,32]{1,0:T(8,128)S(1)} %get-tuple-element.18.refs_1_, f32[16,32,128]{2,1,0:T(8,128)S(1)} %get-tuple-element.19.refs_2_, f32[40,256]{1,0:T(8,128)S(1)} %add_add_fusion.refs_3_, f32[32,256]{1,0:T(8,128)S(1)} %collective-permute-done.9.refs_4_), custom_call_target="tpu_custom_call" | custom-call | tf_op jit(solution)/shard_map/finish/pallas_call | solution.py:345
  (5 shorter events, 0.0 us)
Async XLA Ops:
  1.7 10.7 %collective-permute-start = (f32[16,40,128]{2,1,0:T(8,128)S(1)}, f32[16,40,128]{2,1,0:T(8,128)S(1)}, u32[]{:S(2)}, u32[]{:S(2)}) collective-permute-start(f32[16,40,128]{2,1,0:T(8,128)S(1)} %get-tuple-element.13.refs_2_), channel_id=1, source_target_pairs={{2,0},{0,2},{3,1},{1,3},{6,4},{4,6},{7,5},{5,7},{10,8},{8,10},{11,... | collective-permute-start | bytes 983048 | tf_op jit(solution)/shard_map/ppermute | solution.py:391
  4.7 14.0 %collective-permute-start.1 = (f32[6,40,128]{2,1,0:T(8,128)S(1)}, f32[6,40,128]{2,1,0:T(8,128)S(1)}, u32[]{:S(2)}, u32[]{:S(2)}) collective-permute-start(f32[6,40,128]{2,1,0:T(8,128)S(1)} %get-tuple-element.14), channel_id=1, source_target_pairs={{0,1},{1,0},{2,3},{3,2},{4,5},{5,4},{6,7},{7,6},{8,9},{9,8},{10,11... | collective-permute-start | bytes 368648 | tf_op jit(solution)/shard_map/ppermute | solution.py:362
  4.7 14.0 %collective-permute-start.3 = (f32[6,40,128]{2,1,0:T(8,128)S(1)}, f32[6,40,128]{2,1,0:T(8,128)S(1)}, u32[]{:S(2)}, u32[]{:S(2)}) collective-permute-start(f32[6,40,128]{2,1,0:T(8,128)S(1)} %get-tuple-element.15), channel_id=1, source_target_pairs={{1,4},{4,1},{5,8},{8,5},{9,12},{12,9},{3,6},{6,3},{7,10},{10,7},{1... | collective-permute-start | bytes 368648 | tf_op jit(solution)/shard_map/ppermute | solution.py:399
  12.4 6.3 %collective-permute-start.4 = (f32[6,40,128]{2,1,0:T(8,128)S(1)}, f32[6,40,128]{2,1,0:T(8,128)S(1)}, u32[]{:S(2)}, u32[]{:S(2)}) collective-permute-start(f32[6,40,128]{2,1,0:T(8,128)S(1)} %get-tuple-element.23), channel_id=1, source_target_pairs={{1,4},{4,1},{5,8},{8,5},{9,12},{12,9},{3,6},{6,3},{7,10},{10,7},{1... | collective-permute-start | bytes 368648 | tf_op jit(solution)/shard_map/ppermute | solution.py:399
  13.1 5.6 %collective-permute-start.2 = (f32[6,40,128]{2,1,0:T(8,128)S(1)}, f32[6,40,128]{2,1,0:T(8,128)S(1)}, u32[]{:S(2)}, u32[]{:S(2)}) collective-permute-start(f32[6,40,128]{2,1,0:T(8,128)S(1)} %get-tuple-element.24), channel_id=1, source_target_pairs={{0,1},{1,0},{2,3},{3,2},{4,5},{5,4},{6,7},{7,6},{8,9},{9,8},{10,11... | collective-permute-start | bytes 368648 | tf_op jit(solution)/shard_map/ppermute | solution.py:362
  23.9 1.3 %collective-permute-start.5 = (f32[40,256]{1,0:T(8,128)S(1)}, f32[40,256]{1,0:T(8,128)S(1)}, u32[]{:S(2)}, u32[]{:S(2)}) collective-permute-start(f32[40,256]{1,0:T(8,128)S(1)} %get-tuple-element.17), channel_id=1, source_target_pairs={{0,1},{1,0},{2,3},{3,2},{4,5},{5,4},{6,7},{7,6},{8,9},{9,8},{10,11... | collective-permute-start | bytes 122888 | tf_op jit(solution)/shard_map/ppermute | solution.py:362
  25.1 5.8 %collective-permute-start.8 = (f32[40,256]{1,0:T(8,128)S(1)}, f32[40,256]{1,0:T(8,128)S(1)}, u32[]{:S(2)}, u32[]{:S(2)}) collective-permute-start(f32[40,256]{1,0:T(8,128)S(1)} %add.20), channel_id=1, source_target_pairs={{0,12},{4,8},{8,4},{12,0},{1,13},{5,9},{9,5},{13,1},{2,14},{6,10},... | collective-permute-start | bytes 122888 | tf_op jit(solution)/shard_map/ppermute | solution.py:362
  28.9 4.9 %collective-permute-start.7 = (f32[40,256]{1,0:T(8,128)S(1)}, f32[40,256]{1,0:T(8,128)S(1)}, u32[]{:S(2)}, u32[]{:S(2)}) collective-permute-start(f32[40,256]{1,0:T(8,128)S(1)} %add.20), channel_id=1, source_target_pairs={{0,8},{4,12},{8,0},{12,4},{1,9},{5,13},{9,1},{13,5},{2,10},{6,14},... | collective-permute-start | bytes 122888 | tf_op jit(solution)/shard_map/ppermute | solution.py:362
  28.9 4.9 %collective-permute-start.6 = (f32[40,256]{1,0:T(8,128)S(1)}, f32[40,256]{1,0:T(8,128)S(1)}, u32[]{:S(2)}, u32[]{:S(2)}) collective-permute-start(f32[40,256]{1,0:T(8,128)S(1)} %add.20), channel_id=1, source_target_pairs={{0,4},{4,0},{8,12},{12,8},{1,5},{5,1},{9,13},{13,9},{2,6},{6,2},{1... | collective-permute-start | bytes 122888 | tf_op jit(solution)/shard_map/ppermute | solution.py:362
  33.8 1.5 %collective-permute-start.9 = (f32[32,256]{1,0:T(8,128)S(1)}, f32[32,256]{1,0:T(8,128)S(1)}, u32[]{:S(2)}, u32[]{:S(2)}) collective-permute-start(f32[32,256]{1,0:T(8,128)S(1)} %slice.9), channel_id=1, source_target_pairs={{0,1},{1,0},{2,3},{3,2},{4,5},{5,4},{6,7},{7,6},{8,9},{9,8},{10,11... | collective-permute-start | bytes 98312 | tf_op jit(solution)/shard_map/ppermute | solution.py:362

commit v5 on v4

v5 whole, which is shorter than its diff:
```python
import math

import jax
import jax.numpy as jnp
from jax import lax
from jax.experimental import pallas as pl
from jax.experimental.pallas import tpu as pltpu
from jax.sharding import PartitionSpec as P

DEGREE = 6
CUT_LOW = 2
CUT_HIGH = 32
CENTRE = 0.5 * (CUT_HIGH + CUT_LOW)
SPREAD = 0.5 * (CUT_HIGH - CUT_LOW)
HALO = DEGREE
GRID_ROWS = ("strip", "sub")
SIDE = 8
SLOT = 16
LOW_SHARE = 3

VMEM = pl.BlockSpec(memory_space=pltpu.VMEM)
SMEM = pl.BlockSpec(memory_space=pltpu.SMEM)
HBM = pl.BlockSpec(memory_space=pltpu.HBM)


def pack_kernel(
    sub_ref, block_hbm, weights_hbm, mass_hbm, body_ref, near_ref, far_ref, packet_ref,
    block_ref, weights_ref, mass_ref, sems,
):
    copies = [
        pltpu.make_async_copy(block_hbm, block_ref, sems.at[0]),
        pltpu.make_async_copy(weights_hbm.at[0:4], weights_ref, sems.at[1]),
        pltpu.make_async_copy(mass_hbm, mass_ref, sems.at[2]),
    ]
    for copy in copies:
        copy.start()
    for copy in copies:
        copy.wait()
    count, height, width = block_ref.shape
    body_ref[:, 0:count, :] = pltpu.einshape("brc->rbc", block_ref[...])
    mass = mass_ref[...][None]
    side = jnp.concatenate([weights_ref[...], mass, mass, mass, mass], axis=0)
    body_ref[:, count : count + SIDE, :] = pltpu.einshape("brc->rbc", side)
    sub = sub_ref[0]
    near_ref[...] = body_ref[pl.ds((1 - sub) * (height - HALO), HALO)]
    far_ref[...] = body_ref[pl.ds(sub * (height - HALO), HALO)]
    lane = lax.broadcasted_iota(jnp.int32, (count + SIDE, width), 1)
    for tile in range(height // 8):
        packet = pltpu.roll(body_ref[8 * tile], HALO, 1)
        for i in range(1, 8):
            moved = pltpu.roll(body_ref[8 * tile + i], HALO + SLOT * i, 1)
            packet = jnp.where(lane >= SLOT * i, moved, packet)
        packet_ref[tile] = packet


def pack(sub, start_block, edge_weights, mass):
    count, height, width = start_block.shape
    halo = jax.ShapeDtypeStruct((HALO, count + SIDE, width), jnp.float32)
    return pl.pallas_call(
        pack_kernel,
        in_specs=[SMEM, HBM, HBM, HBM],
        out_specs=[VMEM] * 4,
        out_shape=[
            jax.ShapeDtypeStruct((height, count + SIDE, width), jnp.float32),
            halo,
            halo,
            jax.ShapeDtypeStruct((height // 8, count + SIDE, width), jnp.float32),
        ],
        scratch_shapes=[
            pltpu.VMEM((count, height, width), jnp.float32),
            pltpu.VMEM((4, height, width), jnp.float32),
            pltpu.VMEM((height, width), jnp.float32),
            pltpu.SemaphoreType.DMA((3,)),
        ],
        compiler_params=pltpu.CompilerParams(vmem_limit_bytes=8 << 20),
        name="pack",
    )(sub, *[in_hbm(x) for x in (start_block, edge_weights, mass)])


def in_hbm(array):
    return pltpu.with_memory_space_constraint(array, pltpu.HBM)


def in_vmem(array):
    return pltpu.with_memory_space_constraint(array, pltpu.VMEM)


def relayout_kernel(locked_hbm, flat_ref, chunks_ref, sems, *, panels):
    chunks, size, height, total = chunks_ref.shape
    width = total // panels
    copies = [
        pltpu.make_async_copy(locked_hbm.at[pl.ds(i * size, size)], chunks_ref.at[i], sems.at[i])
        for i in range(chunks)
    ]
    for copy in copies:
        copy.start()
    for i in range(chunks):
        copies[i].wait()
        rows = pltpu.einshape("krc->rkc", chunks_ref[i])
        for r in range(height):
            for t in range(panels):
                at = (t * height + r) * width
                flat_ref[pl.ds(i * size, size), at : at + width] = rows[
                    r, :, t * width : (t + 1) * width
                ]


def relayout(locked, panels):
    basis, height, width = locked.shape
    chunks = max(1, basis // 64)
    return pl.pallas_call(
        lambda *refs: relayout_kernel(*refs, panels=panels),
        in_specs=[HBM],
        out_specs=VMEM,
        out_shape=pltpu.VMEM((basis, height * width), locked.dtype),
        scratch_shapes=[
            pltpu.VMEM((chunks, basis // chunks, height, width), locked.dtype),
            pltpu.SemaphoreType.DMA((chunks,)),
        ],
        compiler_params=pltpu.CompilerParams(vmem_limit_bytes=12 << 20),
        name="relayout",
    )(in_hbm(locked))


def filter_kernel(panel_ref, sub_ref, *refs, packets, first, panels):
    body_ref, near_ref, far_ref = refs[0:3]
    packet_refs = refs[3 : 3 + packets]
    if first:
        own_ref, coef_ref, y_even, y_odd = refs[4 + packets :]
    else:
        coef_ref, own_ref, y_even, y_odd = refs[3 + packets :]
    height, planes, width = body_ref.shape
    count = own_ref.shape[1]
    total = 2 * width
    rows = height + 2 * HALO
    start = 0 if first else planes - SIDE - count
    first_sub = sub_ref[0] == 0

    def unpack(tiles, i, lane):
        moved = [pltpu.roll(t, width - HALO - SLOT * i, 1) for t in tiles]
        after = jnp.where(lane < HALO, moved[0], 0.0)
        return jnp.where(lane >= width - HALO, moved[-1], after)

    def source(row, at, size):
        cut = slice(at, at + size)
        lane = lax.broadcasted_iota(jnp.int32, (size, width), 1)
        if HALO <= row < HALO + height:
            line = row - HALO
            own = body_ref[line, cut]
            tiles = [p[line // 8, cut] for p in packet_refs]
            i = line % 8
        else:
            if row < HALO:
                upper, lower, line, i = far_ref, near_ref, row, row + 8 - HALO
            else:
                upper, lower, line, i = near_ref, far_ref, row - HALO - height, row - HALO - height
            own = jnp.where(first_sub, upper[line, cut], lower[line, cut])
            tiles = [
                jnp.where(first_sub, upper[HALO + q, cut], lower[HALO + q, cut])
                for q in range(packets)
            ]
        return jnp.concatenate([own, unpack(tiles, i, lane)], axis=1)

    def left(x):
        return pltpu.roll(x, total - 1, 1)

    def right(x):
        return pltpu.roll(x, 1, 1)

    for row in range(rows):
        y_even[row] = source(row, start, count)

    if first:
        whole = panels * width
        lane = lax.broadcasted_iota(jnp.int32, (1, total), 1)
        lane = jnp.where(lane < width + width // 2, lane, lane - total + whole)
        column = lax.rem(lane + panel_ref[0] * width, whole)
        not_last = (column != whole - 1).astype(jnp.float32)
        not_first = (column != 0).astype(jnp.float32)
        factor = 2.0 / SPREAD
        weights = []
        scale = []
        for row in range(rows):
            side = source(row, planes - SIDE, SIDE)
            mass = side[4:5]
            inside = mass > 0.0
            scale.append(jnp.where(inside, 1.0 / jnp.sqrt(jnp.where(inside, mass, 1.0)), 0.0))
            weights.append([side[d : d + 1] for d in range(4)])
        edges = []
        for row in range(rows - 1):
            s0 = scale[row]
            s1 = scale[row + 1]
            w = weights[row]
            e0 = -factor * (w[0] * (s0 * left(s0))) * not_last
            e1 = -factor * (w[1] * (s0 * s1))
            e2 = -factor * (w[2] * (s0 * left(s1))) * not_last
            e3 = -factor * (w[3] * (s0 * right(s1))) * not_first
            edges.append((e0, e1, e2, e3))
        for row in range(1, rows - 1):
            w = weights[row]
            v = weights[row - 1]
            total_weight = (
                ((w[0] + w[1]) + (w[2] + w[3]))
                + (right(w[0] * not_last) + v[1])
                + (right(v[2] * not_last) + left(v[3] * not_first))
            )
            diagonal = factor * (scale[row] * scale[row] * total_weight - CENTRE)
            e0, e1, e2, e3 = edges[row]
            u0, u1, u2, u3 = edges[row - 1]
            planes_here = (diagonal, e1, u1, right(e0), right(e2), u3, e0, left(e3), u2)
            for index, plane in enumerate(planes_here):
                coef_ref[row, index : index + 1] = plane

    buffers = (y_even, y_odd)
    for order in range(1, DEGREE + 1):
        source_ref = buffers[(order - 1) % 2]
        target_ref = buffers[order % 2]
        for row in range(order, rows - order):
            c = [coef_ref[row, i : i + 1] for i in range(9)]
            ym = source_ref[row - 1]
            y0 = source_ref[row]
            yp = source_ref[row + 1]
            out = c[0] * y0 + (c[1] * yp + c[2] * ym)
            to_left = c[3] * y0 + (c[4] * yp + c[5] * ym)
            to_right = c[6] * y0 + (c[7] * yp + c[8] * ym)
            out = out + (left(to_left) + right(to_right))
            if order == 1:
                out = 0.5 * out
            else:
                out = out - target_ref[row]
            if order == DEGREE:
                own_ref[row - HALO] = out[:, 0:width]
            else:
                target_ref[row] = out


def filter_part(panel, sub, body, near, far, packets, panels, coef=None, ahead=None):
    height, planes, width = body.shape
    first = coef is None
    low = LOW_SHARE * (planes - SIDE) // 4
    count = low if first else planes - SIDE - low
    rows = height + 2 * HALO
    own = jax.ShapeDtypeStruct((height, count, width), jnp.float32)
    out = [own, jax.ShapeDtypeStruct((rows, 16, 2 * width), jnp.float32)] if first else own
    operands = [panel, sub, body, near, far, *packets, ahead if first else coef]
    buffer = pltpu.VMEM((rows, count, 2 * width), jnp.float32)
    return pl.pallas_call(
        lambda *refs: filter_kernel(*refs, packets=len(packets), first=first, panels=panels),
        in_specs=[SMEM, SMEM] + [VMEM] * (len(operands) - 2),
        out_specs=[VMEM, VMEM] if first else VMEM,
        out_shape=out,
        scratch_shapes=[buffer, buffer],
        compiler_params=pltpu.CompilerParams(vmem_limit_bytes=16 << 20),
        cost_estimate=pl.CostEstimate(flops=1, transcendentals=0, bytes_accessed=1),
        name="filter",
    )(*operands)


def product_kernel(block_ref, sub_ref, *refs, begin, last):
    part_refs = refs[0:2]
    locked_ref = refs[2]
    split = refs[-1]
    height, _, width = part_refs[0].shape
    count = part_refs[0].shape[1] + part_refs[1].shape[1]
    for row in range(height):
        full = jnp.concatenate([part[row] for part in part_refs], axis=0)
        high = full.astype(jnp.bfloat16)
        rest = full - high.astype(jnp.float32)
        middle = rest.astype(jnp.bfloat16)
        low = (rest - middle.astype(jnp.float32)).astype(jnp.bfloat16)
        split[:, row * width : (row + 1) * width] = jnp.concatenate([high, middle, low], axis=0)

    dims = (((1,), (1,)), ((), ()))
    pieces = split[...]
    gram = lax.dot_general(pieces, pieces, dims, preferred_element_type=jnp.float32)
    gram = gram[0:count] + gram[count : 2 * count] + gram[2 * count : 3 * count]
    gram = gram[:, 0:count] + gram[:, count : 2 * count] + gram[:, 2 * count : 3 * count]
    span = height * width
    at = pl.multiple_of(block_ref[0] * span, span)
    products = lax.dot_general(
        pieces, locked_ref[:, pl.ds(at, span)], dims, preferred_element_type=jnp.float32
    )
    products = products[0:count] + products[count : 2 * count] + products[2 * count : 3 * count]
    basis = products.shape[1]
    half = basis // 2
    dense = fold(gram, half)
    if not begin:
        sum_ref = refs[3]
        products = products + sum_ref[0:count]
        dense = dense + sum_ref[count : count + 8, 0:half]
    if last:
        keep_ref, send_ref = refs[-3], refs[-2]
        first_sub = sub_ref[0] == 0
        lower = products[:, 0:half]
        upper = products[:, half:]
        keep_ref[0:count] = jnp.where(first_sub, lower, upper)
        send_ref[0:count] = jnp.where(first_sub, upper, lower)
        keep_ref[count : count + 8] = dense
        send_ref[count : count + 8] = dense
    else:
        out_ref = refs[-2]
        out_ref[0:count] = products
        out_ref[count : count + 8, 0:half] = dense


def fold(gram, width):
    count = gram.shape[0]
    parts = [gram[r : r + 8] for r in range(0, count, 8)]
    spare = width - count * len(parts)
    if spare > 0:
        parts.append(jnp.zeros((8, spare), jnp.float32))
    return jnp.concatenate(parts, axis=1)


def products(block, sub, parts, locked_flat, before, last):
    height, _, width = parts[0].shape
    count = parts[0].shape[1] + parts[1].shape[1]
    basis = locked_flat.shape[0]
    begin = before is None
    operands = [block, sub, *parts, in_vmem(locked_flat)] + ([] if begin else [before])
    whole = jax.ShapeDtypeStruct((count + 8, basis), jnp.float32)
    half = jax.ShapeDtypeStruct((count + 8, basis // 2), jnp.float32)
    return pl.pallas_call(
        lambda *refs: product_kernel(*refs, begin=begin, last=last),
        in_specs=[SMEM, SMEM] + [VMEM] * (len(operands) - 2),
        out_specs=[VMEM, VMEM] if last else VMEM,
        out_shape=[half, half] if last else whole,
        scratch_shapes=[pltpu.VMEM((3 * count, height * width), jnp.bfloat16)],
        compiler_params=pltpu.CompilerParams(vmem_limit_bytes=12 << 20),
        cost_estimate=pl.CostEstimate(flops=1, transcendentals=0, bytes_accessed=1),
        name="products",
    )(*operands)


def factor_kernel(gram_ref, factor_ref, inverse_ref, *, vertices):
    count = factor_ref.shape[0]
    tiles = count // 8
    dense = gram_ref[...]
    row = lax.broadcasted_iota(jnp.int32, (8, 128), 0)
    col = lax.broadcasted_iota(jnp.int32, (8, 128), 1)
    blank = jnp.zeros((8, 128 - count), jnp.float32)

    def fill(x):
        return jnp.broadcast_to(x, (8, 128))

    work = []
    for t in range(tiles):
        gram = jnp.concatenate([dense[:, t * count : (t + 1) * count], blank], axis=1)
        at = row + 8 * t
        gram = gram * (1.0 / vertices) + jnp.where(at == col, 1e-06, 0.0)
        work.append(gram + jnp.where(at + count == col, 1.0, 0.0))
    for b in range(tiles):
        columns = {
            (t, k): fill(work[t][:, 8 * b + k : 8 * b + k + 1])
            for t in range(b, tiles)
            for k in range(8)
        }
        pivots = jnp.ones((8, 128), jnp.float32)
        for j in range(8):
            pivot = fill(columns[b, j][j : j + 1])
            pivots = jnp.where(row == j, pivot, pivots)
            inverse = 1.0 / pivot
            pivot_row = fill(work[b][j : j + 1])
            entries = {k: fill(columns[b, k][j : j + 1]) for k in range(j + 1, 8)}
            for t in range(b, tiles):
                multiplier = columns[t, j] * inverse
                if t == b:
                    multiplier = jnp.where(row > j, multiplier, 0.0)
                for k in range(j + 1, 8):
                    columns[t, k] = columns[t, k] - multiplier * entries[k]
                work[t] = work[t] - multiplier * pivot_row
        work[b] = work[b] * (1.0 / jnp.sqrt(pivots))
    for t in range(tiles):
        upper = jnp.where(row + 8 * t <= col, work[t], 0.0)
        factor_ref[8 * t : 8 * t + 8, :] = upper[:, 0:count]
        inverse_ref[8 * t : 8 * t + 8, :] = work[t][:, count : 2 * count]


def factorize(dense, count, vertices):
    square = jax.ShapeDtypeStruct((count, count), jnp.float32)
    return pl.pallas_call(
        lambda *refs: factor_kernel(*refs, vertices=float(vertices)),
        in_specs=[VMEM],
        out_specs=[VMEM, VMEM],
        out_shape=[square, square],
        compiler_params=pltpu.CompilerParams(vmem_limit_bytes=8 << 20),
        name="factor",
    )(dense)


def finish_kernel(
    sub_ref, inverse_ref, low_ref, high_ref, mine_ref, other_ref, ortho_hbm, coupling_hbm,
    ortho_ref, coupling_ref, sems, *, vertices,
):
    count, height, width = ortho_ref.shape
    first_sub = sub_ref[0] == 0
    half = mine_ref.shape[1]
    mine = mine_ref[0:count]
    other = other_ref[...]
    inverse = inverse_ref[...]

    def times(left, right):
        return jnp.dot(
            left, right, precision=lax.Precision.HIGHEST, preferred_element_type=jnp.float32
        )

    flat = jnp.concatenate(
        [jnp.concatenate([low_ref[r], high_ref[r]], axis=0) for r in range(height)], axis=1
    )
    ortho = times(inverse, flat)
    stacked = jnp.stack([ortho[:, r * width : (r + 1) * width] for r in range(height)], axis=0)
    ortho_ref[...] = pltpu.einshape("rbc->brc", stacked)
    ortho_copy = pltpu.make_async_copy(ortho_ref, ortho_hbm, sems.at[0])
    ortho_copy.start()
    inverse = inverse * (1.0 / math.sqrt(vertices))
    coupling_ref[:, 0:half] = times(inverse, jnp.where(first_sub, mine, other))
    coupling_ref[:, half:] = times(inverse, jnp.where(first_sub, other, mine))
    coupling_copy = pltpu.make_async_copy(coupling_ref, coupling_hbm, sems.at[1])
    coupling_copy.start()
    ortho_copy.wait()
    coupling_copy.wait()


def finish(sub, inverse, parts, mine, other, vertices):
    height, _, width = parts[0].shape
    count = parts[0].shape[1] + parts[1].shape[1]
    ortho = (count, height, width)
    coupling = (count, 2 * mine.shape[1])
    return pl.pallas_call(
        lambda *refs: finish_kernel(*refs, vertices=float(vertices)),
        in_specs=[SMEM] + [VMEM] * 5,
        out_specs=[HBM, HBM],
        out_shape=[jax.ShapeDtypeStruct(s, jnp.float32) for s in (ortho, coupling)],
        scratch_shapes=[
            pltpu.VMEM(ortho, jnp.float32),
            pltpu.VMEM(coupling, jnp.float32),
            pltpu.SemaphoreType.DMA((2,)),
        ],
        compiler_params=pltpu.CompilerParams(vmem_limit_bytes=8 << 20),
        name="finish",
    )(sub, inverse, *parts, mine, other)


def swap(array, axis, distance):
    size = lax.axis_size(axis)
    return lax.ppermute(array, axis, [(i, i ^ distance) for i in range(size)])


def shifted(array, shift):
    size = lax.axis_size("panel")
    return lax.ppermute(array, "panel", [((i + shift) % size, i) for i in range(size)])


def strip_sum(part):
    strips = lax.axis_size("strip")
    distance = 1
    while distance * 4 < strips or distance * 2 == strips:
        part = part + swap(part, "strip", distance)
        distance *= 2
    if distance * 4 == strips:
        one = swap(part, "strip", distance)
        two = swap(part, "strip", 2 * distance)
        three = swap(part, "strip", 3 * distance)
        part = (part + one) + (two + three)
    return part


def on_device(start_block, edge_weights, mass, locked):
    panels = lax.axis_size("panel")
    lines = lax.axis_size(GRID_ROWS)
    count, height, width = start_block.shape
    vertices = height * width * lines * panels
    panel = lax.axis_index("panel").astype(jnp.int32).reshape(1)
    sub = lax.axis_index("sub").astype(jnp.int32).reshape(1)

    body, near, far, packet = pack(sub, start_block, edge_weights, mass)
    packets = [shifted(packet, 1)]
    if panels > 2:
        packets.append(shifted(packet, panels - 1))
    locked_flat = relayout(locked, panels)
    across = []
    for line in range(1, lines - 1, 2):
        across += [(line, line + 1), (line + 1, line)]
    tiles = height // 8 - 1

    def with_edges(rows, tile):
        edges = [lax.dynamic_slice_in_dim(p, tile * tiles, 1, 0) for p in packets]
        return jnp.concatenate([rows] + edges, axis=0)

    near = swap(with_edges(near, 1 - sub[0]), "sub", 1)
    far = lax.ppermute(with_edges(far, sub[0]), GRID_ROWS, across)
    low, coef = filter_part(
        panel, sub, body, near, far, packets, panels, ahead=in_vmem(locked_flat)
    )
    blocks = [[low]]
    blocks += [[shifted(low, t)] for t in range(1, panels)]
    high = filter_part(panel, sub, body, near, far, packets, panels, coef)
    blocks[0].append(high)
    for t in range(1, panels):
        blocks[t].append(shifted(high, t))
    total = None
    for t in range(panels):
        block = lax.rem(panel + t, panels)
        total = products(block, sub, blocks[t], locked_flat, total, t == panels - 1)
    keep, send = total
    part = strip_sum(keep + swap(send, "sub", 1))
    other = swap(part[:count], "sub", 1)
    factor, inverse = factorize(part[count:, : count * count // 8], count, vertices)
    ortho, coupling = finish(sub, inverse, blocks[0], part, other, vertices)
    return (ortho, jnp.transpose(coupling), factor)


def solution(mesh):
    return jax.shard_map(
        on_device,
        mesh=mesh,
        in_specs=(
            P("groups", ("strip", "sub"), "panel"),
            P("groups", ("strip", "sub"), "panel"),
            P(("groups", "strip", "sub"), "panel"),
            P(("groups", "panel"), ("strip", "sub"), None),
        ),
        out_specs=(
            P("groups", ("strip", "sub"), "panel"),
            P(("groups", "panel"), None),
            P("groups", None),
        ),
        check_vma=False,
    )
```

time: 36.6 us -> 39.2 us (1.071)
  starting transfers between devices: 12.2 us -> 13.9 us
  Pallas kernels: 11 us -> 12.2 us
  waiting for transfers between devices: 12.4 us -> 12 us
    ppermute x3 -> x4, starting transfers between devices: 4.33 us -> 5.83 us  [the longest x3 5.16 us: shifted(): lax.ppermute(array, 'panel', [((i + shift) % size, i) for i in range(size)])]
    pallas_call x2 -> x5, Pallas kernels: 7.45 us -> 8.52 us  [the longest x2 4.22 us: filter_part(): pl.pallas_call(lambda *refs: filter_kernel(*refs, packets=len(packets), f...]
    ppermute x3 -> x4, waiting for transfers between devices: 7.04 us -> 6.39 us  [the longest x3 6.38 us: shifted(): lax.ppermute(array, 'panel', [((i + shift) % size, i) for i in range(size)])]
    ppermute x7 -> x6, waiting for transfers between devices: 5.39 us -> 5.66 us  [swap(): return lax.ppermute(array, axis, [(i, i ^ distance) for i in range(size)])]
    ppermute x7 -> x6, starting transfers between devices: 7.84 us -> 8.05 us  [swap(): return lax.ppermute(array, axis, [(i, i ^ distance) for i in range(size)])]
  transfers between devices with their start and end apart: 10 -> 10, of which waited for: 4 -> 5; matrix products, arithmetic and copies ran while one was open for 0% -> 0% of each run, Pallas kernels for 10% -> 15%
where the time goes in v5:
time: 39.2 us; the launch traced here: 39 us
  starting transfers between devices  13.9 us (35%)
  Pallas kernels  12.2 us (31%)
  waiting for transfers between devices  12 us (31%)
  between operations  0.76 us (2%)
    ppermute x6, starting transfers between devices, swap(): return lax.ppermute(array, axis, [(i, i ^ distance) for i in range(size)])  8.05 us
    ppermute x3, waiting for transfers between devices, shifted(): lax.ppermute(array, 'panel', [((i + shift) % size, i) for i in range(size)])  6.38 us
    ppermute x6, waiting for transfers between devices, swap(): return lax.ppermute(array, axis, [(i, i ^ distance) for i in range(size)])  5.66 us
    ppermute x3, starting transfers between devices, shifted(): lax.ppermute(array, 'panel', [((i + shift) % size, i) for i in range(size)])  5.16 us
    pallas_call x2, Pallas kernels, filter_part(): pl.pallas_call(lambda *refs: filter_kernel(*refs, packets=len(packets), f...  4.22 us
    pallas_call x1, Pallas kernels, relayout(): pl.pallas_call(lambda *refs: relayout_kernel(*refs, panels=panels), in_sp...  2.61 us
    pallas_call x2, Pallas kernels, products(): pl.pallas_call(lambda *refs: product_kernel(*refs, begin=begin, last=last...  1.69 us
    pallas_call x1, Pallas kernels, factorize(): pl.pallas_call(lambda *refs: factor_kernel(*refs, vertices=float(vertices...  1.41 us
  transfers between devices with their start and end apart: 10, of which 5 were waited for; matrix products, arithmetic and copies ran while one was open for 0% of the time, Pallas kernels for 15%

profile of v5, /device:TPU:0, one launch (start us, length us, event | category | flops | bytes accessed | tf_op | source)
XLA Modules:
  0.0 39.0 jit_solution(16989054082853899812)
XLA Ops:
  0.6 1.2 %pack.1 = (f32[16,40,128]{2,1,0:T(8,128)S(1)}, f32[6,40,128]{2,1,0:T(8,128)S(1)}, f32[6,40,128]{2,1,0:T(8,128)S(1)}, f32[2,40,128]{2,1,0:T(8,128)S(1)}) custom-call(s32[1]{0:T(128)} %bitcast.sub_ref.refs_1_.refs_0_, f32[32,16,128]{2,1,0:T(8,128)} %block_hbm.1, f32[8,16,128]{2,1,0:T(8,128)} %weights_hbm.1, f32[16,128]{1,0:T(8,128)} %mass_hbm.1), custom_call_target="tpu_custom_call" | custom-call | tf_op jit(solution)/shard_map/pack/pallas_call | solution.py:59
  1.8 3.0 %collective-permute-start = (f32[2,40,128]{2,1,0:T(8,128)S(1)}, f32[2,40,128]{2,1,0:T(8,128)S(1)}, u32[]{:S(2)}, u32[]{:S(2)}) collective-permute-start(f32[2,40,128]{2,1,0:T(8,128)S(1)} %get-tuple-element.17), channel_id=1, source_target_pairs={{2,0},{0,2},{3,1},{1,3},{6,4},{4,6},{7,5},{5,7},{10,8},{8,10},{11,... | collective-permute-start | bytes 122888 | tf_op jit(solution)/shard_map/ppermute | solution.py:451
  4.8 2.0 %collective-permute-done.refs_5_ = f32[2,40,128]{2,1,0:T(8,128)S(1)} collective-permute-done((f32[2,40,128]{2,1,0:T(8,128)S(1)}, f32[2,40,128]{2,1,0:T(8,128)S(1)}, u32[]{:S(2)}, u32[]{:S(2)}) %collective-permute-start) | collective-permute-done | bytes 40992 | tf_op jit(solution)/shard_map/ppermute | solution.py:451
  6.8 0.7 %collective-permute-start.2 = (f32[7,40,128]{2,1,0:T(8,128)S(1)}, f32[7,40,128]{2,1,0:T(8,128)S(1)}, u32[]{:S(2)}, u32[]{:S(2)}) collective-permute-start(f32[7,40,128]{2,1,0:T(8,128)S(1)} %pad_maximum_fusion.1), channel_id=1, source_target_pairs={{1,4},{4,1},{5,8},{8,5},{9,12},{12,9},{3,6},{6,3},{7,10},{10,7},{1... | collective-permute-start | bytes 430088 | tf_op jit(solution)/shard_map/ppermute | solution.py:491
  7.5 3.5 %collective-permute-start.1 = (f32[7,40,128]{2,1,0:T(8,128)S(1)}, f32[7,40,128]{2,1,0:T(8,128)S(1)}, u32[]{:S(2)}, u32[]{:S(2)}) collective-permute-start(f32[7,40,128]{2,1,0:T(8,128)S(1)} %pad_maximum_fusion), channel_id=1, source_target_pairs={{0,1},{1,0},{2,3},{3,2},{4,5},{5,4},{6,7},{7,6},{8,9},{9,8},{10,11... | collective-permute-start | bytes 430088 | tf_op jit(solution)/shard_map/ppermute | solution.py:446
  11.1 2.6 %relayout.1.refs_6_.refs_4_ = bf16[512,4096]{1,0:T(8,128)(2,1)S(1)} custom-call(bf16[512,16,256]{2,1,0:T(8,128)(2,1)} %refs_0_.1), custom_call_target="tpu_custom_call" | custom-call | tf_op jit(solution)/shard_map/relayout/pallas_call | solution.py:111
  13.7 0.0 collective-permute-done.2.refs_4_
  13.7 0.0 collective-permute-done.1.refs_3_
  13.7 3.3 %filter.2 = (f32[16,24,128]{2,1,0:T(8,128)S(1)}, f32[28,16,256]{2,1,0:T(8,128)S(1)}) custom-call(s32[1]{0:T(128)} %bitcast.1.refs_0_, s32[1]{0:T(128)} %bitcast.sub_ref.refs_1_.refs_0_, f32[16,40,128]{2,1,0:T(8,128)S(1)} %get-tuple-element.15.refs_2_, f32[7,40,128]{2,1,0:T(8,128)S(1)} %collective-permute-done.1.refs_3_, ...), custom_call_target="tpu_custom_call" | custom-call | flops 1 | bytes 1 | tf_op jit(solution)/shard_map/filter/pallas_call | solution.py:247
  17.0 1.6 %collective-permute-start.3 = (f32[16,24,128]{2,1,0:T(8,128)S(1)}, f32[16,24,128]{2,1,0:T(8,128)S(1)}, u32[]{:S(2)}, u32[]{:S(2)}) collective-permute-start(f32[16,24,128]{2,1,0:T(8,128)S(1)} %get-tuple-element.19.refs_2_), channel_id=1, source_target_pairs={{2,0},{0,2},{3,1},{1,3},{6,4},{4,6},{7,5},{5,7},{10,8},{8,10},{11,... | collective-permute-start | bytes 589832 | tf_op jit(solution)/shard_map/ppermute | solution.py:451
  18.6 0.9 %filter.3.refs_3_ = f32[16,8,128]{2,1,0:T(8,128)S(1)} custom-call(s32[1]{0:T(128)} %bitcast.1.refs_0_, s32[1]{0:T(128)} %bitcast.sub_ref.refs_1_.refs_0_, f32[16,40,128]{2,1,0:T(8,128)S(1)} %get-tuple-element.15.refs_2_, f32[7,40,128]{2,1,0:T(8,128)S(1)} %collective-permute-done.1.refs_3_, f32[7,40,128]{2,1,0:T(8,128)S(1)} %collective-permute-done.2.refs_4_, ...), custom_call_target="tpu_custom_call" | custom-call | flops 1 | bytes 1 | tf_op jit(solution)/shard_map/filter/pallas_call | solution.py:247
  19.5 0.6 %collective-permute-start.4 = (f32[16,8,128]{2,1,0:T(8,128)S(1)}, f32[16,8,128]{2,1,0:T(8,128)S(1)}, u32[]{:S(2)}, u32[]{:S(2)}) collective-permute-start(f32[16,8,128]{2,1,0:T(8,128)S(1)} %filter.3.refs_3_), channel_id=1, source_target_pairs={{2,0},{0,2},{3,1},{1,3},{6,4},{4,6},{7,5},{5,7},{10,8},{8,10},{11,... | collective-permute-start | bytes 196616 | tf_op jit(solution)/shard_map/ppermute | solution.py:451
  20.1 0.8 %products.2.refs_5_ = f32[40,512]{1,0:T(8,128)S(1)} custom-call(s32[1]{0:T(128)S(6)} %rem.37.refs_0_, s32[1]{0:T(128)} %bitcast.sub_ref.refs_1_.refs_0_, f32[16,24,128]{2,1,0:T(8,128)S(1)} %get-tuple-element.19.refs_2_, f32[16,8,128]{2,1,0:T(8,128)S(1)} %filter.3.refs_3_, bf16[512,4096]{1,0:T(8,128)(2,1)S(1)} %relayout.1.refs_6_.refs_4_), custom_call_target="tpu_custom_call" | custom-call | flops 1 | bytes 1 | tf_op jit(solution)/shard_map/products/pallas_call | solution.py:323
  20.9 4.4 %collective-permute-done.4.refs_3_ = f32[16,8,128]{2,1,0:T(8,128)S(1)} collective-permute-done((f32[16,8,128]{2,1,0:T(8,128)S(1)}, f32[16,8,128]{2,1,0:T(8,128)S(1)}, u32[]{:S(2)}, u32[]{:S(2)}) %collective-permute-start.4) | collective-permute-done | bytes 65568 | tf_op jit(solution)/shard_map/ppermute | solution.py:451
  25.3 0.0 collective-permute-done.3.refs_2_
  25.3 0.9 %products.3 = (f32[40,256]{1,0:T(8,128)S(1)}, f32[40,256]{1,0:T(8,128)S(1)}) custom-call(s32[1]{0:T(128)S(6)} %rem.31.refs_0_, s32[1]{0:T(128)} %bitcast.sub_ref.refs_1_.refs_0_, f32[16,24,128]{2,1,0:T(8,128)S(1)} %collective-permute-done.3.refs_2_, f32[16,8,128]{2,1,0:T(8,128)S(1)} %collective-permute-done.4.refs_3_, ...), custom_call_target="tpu_custom_call" | custom-call | flops 1 | bytes 1 | tf_op jit(solution)/shard_map/products/pallas_call | solution.py:323
  26.2 0.1 collective-permute-start.5
  26.3 1.2 %collective-permute-done.5 = f32[40,256]{1,0:T(8,128)S(1)} collective-permute-done((f32[40,256]{1,0:T(8,128)S(1)}, f32[40,256]{1,0:T(8,128)S(1)}, u32[]{:S(2)}, u32[]{:S(2)}) %collective-permute-start.5) | collective-permute-done | bytes 40992 | tf_op jit(solution)/shard_map/ppermute | solution.py:446
  27.5 1.7 %collective-permute-start.6 = (f32[40,256]{1,0:T(8,128)S(1)}, f32[40,256]{1,0:T(8,128)S(1)}, u32[]{:S(2)}, u32[]{:S(2)}) collective-permute-start(f32[40,256]{1,0:T(8,128)S(1)} %add.25), channel_id=1, source_target_pairs={{0,4},{4,0},{8,12},{12,8},{1,5},{5,1},{9,13},{13,9},{2,6},{6,2},{1... | collective-permute-start | bytes 122888 | tf_op jit(solution)/shard_map/ppermute | solution.py:446
  29.2 1.3 %collective-permute-start.7 = (f32[40,256]{1,0:T(8,128)S(1)}, f32[40,256]{1,0:T(8,128)S(1)}, u32[]{:S(2)}, u32[]{:S(2)}) collective-permute-start(f32[40,256]{1,0:T(8,128)S(1)} %add.25), channel_id=1, source_target_pairs={{0,8},{4,12},{8,0},{12,4},{1,9},{5,13},{9,1},{13,5},{2,10},{6,14},... | collective-permute-start | bytes 122888 | tf_op jit(solution)/shard_map/ppermute | solution.py:446
  30.5 1.3 %collective-permute-start.8 = (f32[40,256]{1,0:T(8,128)S(1)}, f32[40,256]{1,0:T(8,128)S(1)}, u32[]{:S(2)}, u32[]{:S(2)}) collective-permute-start(f32[40,256]{1,0:T(8,128)S(1)} %add.25), channel_id=1, source_target_pairs={{0,12},{4,8},{8,4},{12,0},{1,13},{5,9},{9,5},{13,1},{2,14},{6,10},... | collective-permute-start | bytes 122888 | tf_op jit(solution)/shard_map/ppermute | solution.py:446
  31.9 0.0 collective-permute-done.6
  31.9 3.5 %collective-permute-done.7 = f32[40,256]{1,0:T(8,128)S(1)} collective-permute-done((f32[40,256]{1,0:T(8,128)S(1)}, f32[40,256]{1,0:T(8,128)S(1)}, u32[]{:S(2)}, u32[]{:S(2)}) %collective-permute-start.7) | collective-permute-done | bytes 40992 | tf_op jit(solution)/shard_map/ppermute | solution.py:446
  35.4 0.9 %collective-permute-done.8 = f32[40,256]{1,0:T(8,128)S(1)} collective-permute-done((f32[40,256]{1,0:T(8,128)S(1)}, f32[40,256]{1,0:T(8,128)S(1)}, u32[]{:S(2)}, u32[]{:S(2)}) %collective-permute-start.8) | collective-permute-done | bytes 40992 | tf_op jit(solution)/shard_map/ppermute | solution.py:446
  36.4 0.1 collective-permute-start.9
  36.5 1.4 %factor.1 = (f32[32,32]{1,0:T(8,128)}, f32[32,32]{1,0:T(8,128)S(1)}) custom-call(f32[8,128]{1,0:T(8,128)S(1)} %slice.8.refs_0_), custom_call_target="tpu_custom_call" | custom-call | tf_op jit(solution)/shard_map/factor/pallas_call | solution.py:381
  37.9 0.0 collective-permute-done.9.refs_5_
  37.9 1.1 %finish.1 = (f32[32,16,128]{2,1,0:T(8,128)}, f32[32,512]{1,0:T(8,128)}) custom-call(s32[1]{0:T(128)} %bitcast.sub_ref.refs_1_.refs_0_, f32[32,32]{1,0:T(8,128)S(1)} %get-tuple-element.23.refs_1_, f32[16,24,128]{2,1,0:T(8,128)S(1)} %get-tuple-element.19.refs_2_, f32[16,8,128]{2,1,0:T(8,128)S(1)} %filter.3.refs_3_, f32[40,256]{1,0:T(8,128)S(1)} %add_add_fusion.refs_4_, ...), custom_call_target="tpu_custom_call" | custom-call | tf_op jit(solution)/shard_map/finish/pallas_call | solution.py:429
  (7 shorter events, 0.1 us)
Async XLA Ops:
  1.8 5.0 %collective-permute-start = (f32[2,40,128]{2,1,0:T(8,128)S(1)}, f32[2,40,128]{2,1,0:T(8,128)S(1)}, u32[]{:S(2)}, u32[]{:S(2)}) collective-permute-start(f32[2,40,128]{2,1,0:T(8,128)S(1)} %get-tuple-element.17), channel_id=1, source_target_pairs={{2,0},{0,2},{3,1},{1,3},{6,4},{4,6},{7,5},{5,7},{10,8},{8,10},{11,... | collective-permute-start | bytes 122888 | tf_op jit(solution)/shard_map/ppermute | solution.py:451
  6.8 6.8 %collective-permute-start.2 = (f32[7,40,128]{2,1,0:T(8,128)S(1)}, f32[7,40,128]{2,1,0:T(8,128)S(1)}, u32[]{:S(2)}, u32[]{:S(2)}) collective-permute-start(f32[7,40,128]{2,1,0:T(8,128)S(1)} %pad_maximum_fusion.1), channel_id=1, source_target_pairs={{1,4},{4,1},{5,8},{8,5},{9,12},{12,9},{3,6},{6,3},{7,10},{10,7},{1... | collective-permute-start | bytes 430088 | tf_op jit(solution)/shard_map/ppermute | solution.py:491
  7.5 6.2 %collective-permute-start.1 = (f32[7,40,128]{2,1,0:T(8,128)S(1)}, f32[7,40,128]{2,1,0:T(8,128)S(1)}, u32[]{:S(2)}, u32[]{:S(2)}) collective-permute-start(f32[7,40,128]{2,1,0:T(8,128)S(1)} %pad_maximum_fusion), channel_id=1, source_target_pairs={{0,1},{1,0},{2,3},{3,2},{4,5},{5,4},{6,7},{7,6},{8,9},{9,8},{10,11... | collective-permute-start | bytes 430088 | tf_op jit(solution)/shard_map/ppermute | solution.py:446
  17.0 8.3 %collective-permute-start.3 = (f32[16,24,128]{2,1,0:T(8,128)S(1)}, f32[16,24,128]{2,1,0:T(8,128)S(1)}, u32[]{:S(2)}, u32[]{:S(2)}) collective-permute-start(f32[16,24,128]{2,1,0:T(8,128)S(1)} %get-tuple-element.19.refs_2_), channel_id=1, source_target_pairs={{2,0},{0,2},{3,1},{1,3},{6,4},{4,6},{7,5},{5,7},{10,8},{8,10},{11,... | collective-permute-start | bytes 589832 | tf_op jit(solution)/shard_map/ppermute | solution.py:451
  19.5 5.8 %collective-permute-start.4 = (f32[16,8,128]{2,1,0:T(8,128)S(1)}, f32[16,8,128]{2,1,0:T(8,128)S(1)}, u32[]{:S(2)}, u32[]{:S(2)}) collective-permute-start(f32[16,8,128]{2,1,0:T(8,128)S(1)} %filter.3.refs_3_), channel_id=1, source_target_pairs={{2,0},{0,2},{3,1},{1,3},{6,4},{4,6},{7,5},{5,7},{10,8},{8,10},{11,... | collective-permute-start | bytes 196616 | tf_op jit(solution)/shard_map/ppermute | solution.py:451
  26.2 1.3 %collective-permute-start.5 = (f32[40,256]{1,0:T(8,128)S(1)}, f32[40,256]{1,0:T(8,128)S(1)}, u32[]{:S(2)}, u32[]{:S(2)}) collective-permute-start(f32[40,256]{1,0:T(8,128)S(1)} %get-tuple-element.22), channel_id=1, source_target_pairs={{0,1},{1,0},{2,3},{3,2},{4,5},{5,4},{6,7},{7,6},{8,9},{9,8},{10,11... | collective-permute-start | bytes 122888 | tf_op jit(solution)/shard_map/ppermute | solution.py:446
  27.5 4.4 %collective-permute-start.6 = (f32[40,256]{1,0:T(8,128)S(1)}, f32[40,256]{1,0:T(8,128)S(1)}, u32[]{:S(2)}, u32[]{:S(2)}) collective-permute-start(f32[40,256]{1,0:T(8,128)S(1)} %add.25), channel_id=1, source_target_pairs={{0,4},{4,0},{8,12},{12,8},{1,5},{5,1},{9,13},{13,9},{2,6},{6,2},{1... | collective-permute-start | bytes 122888 | tf_op jit(solution)/shard_map/ppermute | solution.py:446
  29.2 6.2 %collective-permute-start.7 = (f32[40,256]{1,0:T(8,128)S(1)}, f32[40,256]{1,0:T(8,128)S(1)}, u32[]{:S(2)}, u32[]{:S(2)}) collective-permute-start(f32[40,256]{1,0:T(8,128)S(1)} %add.25), channel_id=1, source_target_pairs={{0,8},{4,12},{8,0},{12,4},{1,9},{5,13},{9,1},{13,5},{2,10},{6,14},... | collective-permute-start | bytes 122888 | tf_op jit(solution)/shard_map/ppermute | solution.py:446
  30.5 5.8 %collective-permute-start.8 = (f32[40,256]{1,0:T(8,128)S(1)}, f32[40,256]{1,0:T(8,128)S(1)}, u32[]{:S(2)}, u32[]{:S(2)}) collective-permute-start(f32[40,256]{1,0:T(8,128)S(1)} %add.25), channel_id=1, source_target_pairs={{0,12},{4,8},{8,4},{12,0},{1,13},{5,9},{9,5},{13,1},{2,14},{6,10},... | collective-permute-start | bytes 122888 | tf_op jit(solution)/shard_map/ppermute | solution.py:446
  36.4 1.5 %collective-permute-start.9 = (f32[32,256]{1,0:T(8,128)S(1)}, f32[32,256]{1,0:T(8,128)S(1)}, u32[]{:S(2)}, u32[]{:S(2)}) collective-permute-start(f32[32,256]{1,0:T(8,128)S(1)} %slice.9), channel_id=1, source_target_pairs={{0,1},{1,0},{2,3},{3,2},{4,5},{5,4},{6,7},{7,6},{8,9},{9,8},{10,11... | collective-permute-start | bytes 98312 | tf_op jit(solution)/shard_map/ppermute | solution.py:446

commit v6 on v4

--- a/solution.py
+++ b/solution.py
@@ -248,7 +248,7 @@
         ],
         compiler_params=pltpu.CompilerParams(vmem_limit_bytes=20 << 20),
         name="filter",
-    )(panel, sub, *bodies, *nears, *fars, in_vmem(locked_flat))
+    )(panel, sub, *bodies, *nears, *fars, locked_flat)
 
 
 def factor_kernel(gram_ref, factor_ref, inverse_ref, *, vertices):
@@ -391,25 +391,24 @@
             lax.ppermute(body, "panel", [((i + shift) % panels, i) for i in range(panels)])
         )
     locked_flat = relayout(locked)
-    across = []
-    for line in range(1, lines - 1, 2):
-        across += [(line, line + 1), (line + 1, line)]
-
-    def exchange(near, far):
-        return swap(near, "sub", 1), lax.ppermute(far, GRID_ROWS, across)
-
-    halos = [exchange(near, far)]
+
+    def far_moves(shift):
+        moves = []
+        for line in range(1, lines - 1, 2):
+            for a, b in ((line, line + 1), (line + 1, line)):
+                for p in range(panels):
+                    q = (p - shift) % panels
+                    moves.append((((a // 2) * panels + p) * 2 + a % 2, ((b // 2) * panels + q) * 2 + b % 2))
+        return moves
+
+    fars = [
+        lax.ppermute(far, ("strip", "panel", "sub"), far_moves(shift)) for shift in range(panels)
+    ]
+    nears = [swap(near, "sub", 1)]
+    first = (1 - sub[0]) * (height - HALO)
     for other in bodies[1:]:
-        edge = height - HALO
-        halos.append(
-            exchange(
-                lax.dynamic_slice_in_dim(other, (1 - sub[0]) * edge, HALO, 0),
-                lax.dynamic_slice_in_dim(other, sub[0] * edge, HALO, 0),
-            )
-        )
-    keep, send, own = filter_call(
-        panel, sub, bodies, [h[0] for h in halos], [h[1] for h in halos], locked_flat
-    )
+        nears.append(swap(lax.dynamic_slice_in_dim(other, first, HALO, 0), "sub", 1))
+    keep, send, own = filter_call(panel, sub, bodies, nears, fars, in_vmem(locked_flat))
     part = strip_sum(keep + swap(send, "sub", 1))
     other = swap(part[:count], "sub", 1)
     factor, inverse = factorize(part[count:, : count * count // 8], count, vertices)

time: 36.6 us -> 34.7 us (0.948)
  waiting for transfers between devices: 12.4 us -> 8.67 us
  starting transfers between devices: 12.2 us -> 14 us
    ppermute x1, waiting for transfers between devices: 7.03 us -> 3.43 us  [on_device(): lax.ppermute(body, 'panel', [((i + shift) % panels, i) for i in range(pan...]
    ppermute x7, starting transfers between devices: 7.84 us -> 9.65 us  [swap(): return lax.ppermute(array, axis, [(i, i ^ distance) for i in range(size)])]
  transfers between devices with their start and end apart: 10 -> 10, of which waited for: 4 -> 5; matrix products, arithmetic and copies ran while one was open for 0% -> 0% of each run, Pallas kernels for 10% -> 11%
where the time goes in v6:
time: 34.7 us; the launch traced here: 34.5 us
  starting transfers between devices  14 us (40%)
  Pallas kernels  11 us (32%)
  waiting for transfers between devices  8.67 us (25%)
  between operations  0.75 us (2%)
    ppermute x7, starting transfers between devices, swap(): return lax.ppermute(array, axis, [(i, i ^ distance) for i in range(size)])  9.65 us
    ppermute x7, waiting for transfers between devices, swap(): return lax.ppermute(array, axis, [(i, i ^ distance) for i in range(size)])  5.23 us
    pallas_call x1, Pallas kernels, filter_call(): pl.pallas_call(lambda *refs: filter_kernel(*refs, panels=panels, height=h...  5.11 us
    ppermute x1, waiting for transfers between devices, on_device(): lax.ppermute(body, 'panel', [((i + shift) % panels, i) for i in range(pan...  3.43 us
    ppermute x1, starting transfers between devices, on_device(): lax.ppermute(body, 'panel', [((i + shift) % panels, i) for i in range(pan...  3 us
    pallas_call x1, Pallas kernels, relayout(): pl.pallas_call(relayout_kernel, in_specs=[HBM], out_specs=VMEM, out_shape...  2.35 us
    pallas_call x1, Pallas kernels, factorize(): pl.pallas_call(lambda *refs: factor_kernel(*refs, vertices=float(vertices...  1.41 us
    ppermute x2, starting transfers between devices, on_device(): lax.ppermute(far, ('strip', 'panel', 'sub'), far_moves(shift))  1.32 us
  transfers between devices with their start and end apart: 10, of which 5 were waited for; matrix products, arithmetic and copies ran while one was open for 0% of the time, Pallas kernels for 11%

profile of v6, /device:TPU:0, one launch (start us, length us, event | category | flops | bytes accessed | tf_op | source)
XLA Modules:
  0.0 34.5 jit_solution(3714594244546301805)
XLA Ops:
  0.6 1.1 %pack.1 = (f32[16,40,128]{2,1,0:T(8,128)S(1)}, f32[6,40,128]{2,1,0:T(8,128)S(1)}, f32[6,40,128]{2,1,0:T(8,128)S(1)}) custom-call(s32[1]{0:T(128)} %bitcast.sub_ref.refs_1_.refs_0_, f32[32,16,128]{2,1,0:T(8,128)} %block_hbm.1, f32[8,16,128]{2,1,0:T(8,128)} %weights_hbm.1, f32[16,128]{1,0:T(8,128)} %mass_hbm.1), custom_call_target="tpu_custom_call" | custom-call | tf_op jit(solution)/shard_map/pack/pallas_call | solution.py:50
  1.7 3.0 %collective-permute-start = (f32[16,40,128]{2,1,0:T(8,128)S(1)}, f32[16,40,128]{2,1,0:T(8,128)S(1)}, u32[]{:S(2)}, u32[]{:S(2)}) collective-permute-start(f32[16,40,128]{2,1,0:T(8,128)S(1)} %get-tuple-element.13.refs_2_), channel_id=1, source_target_pairs={{2,0},{0,2},{3,1},{1,3},{6,4},{4,6},{7,5},{5,7},{10,8},{8,10},{11,... | collective-permute-start | bytes 983048 | tf_op jit(solution)/shard_map/ppermute | solution.py:391
  4.7 0.7 %collective-permute-start.4 = (f32[6,40,128]{2,1,0:T(8,128)S(1)}, f32[6,40,128]{2,1,0:T(8,128)S(1)}, u32[]{:S(2)}, u32[]{:S(2)}) collective-permute-start(f32[6,40,128]{2,1,0:T(8,128)S(1)} %get-tuple-element.15), channel_id=1, source_target_pairs={{1,6},{3,4},{4,3},{6,1},{5,10},{7,8},{8,7},{10,5},{9,14},{11,12},{... | collective-permute-start | bytes 368648 | tf_op jit(solution)/shard_map/ppermute | solution.py:405
  5.4 0.7 %collective-permute-start.3 = (f32[6,40,128]{2,1,0:T(8,128)S(1)}, f32[6,40,128]{2,1,0:T(8,128)S(1)}, u32[]{:S(2)}, u32[]{:S(2)}) collective-permute-start(f32[6,40,128]{2,1,0:T(8,128)S(1)} %get-tuple-element.15), channel_id=1, source_target_pairs={{1,4},{3,6},{4,1},{6,3},{5,8},{7,10},{8,5},{10,7},{9,12},{11,14},{... | collective-permute-start | bytes 368648 | tf_op jit(solution)/shard_map/ppermute | solution.py:405
  6.0 4.2 %collective-permute-start.1 = (f32[6,40,128]{2,1,0:T(8,128)S(1)}, f32[6,40,128]{2,1,0:T(8,128)S(1)}, u32[]{:S(2)}, u32[]{:S(2)}) collective-permute-start(f32[6,40,128]{2,1,0:T(8,128)S(1)} %get-tuple-element.14), channel_id=1, source_target_pairs={{0,1},{1,0},{2,3},{3,2},{4,5},{5,4},{6,7},{7,6},{8,9},{9,8},{10,11... | collective-permute-start | bytes 368648 | tf_op jit(solution)/shard_map/ppermute | solution.py:362
  10.3 3.4 %collective-permute-done.refs_3_ = f32[16,40,128]{2,1,0:T(8,128)S(1)} collective-permute-done((f32[16,40,128]{2,1,0:T(8,128)S(1)}, f32[16,40,128]{2,1,0:T(8,128)S(1)}, u32[]{:S(2)}, u32[]{:S(2)}) %collective-permute-start) | collective-permute-done | bytes 327712 | tf_op jit(solution)/shard_map/ppermute | solution.py:391
  13.7 0.1 collective-permute-start.2
  13.8 2.3 %relayout.1.refs_8_ = bf16[512,4096]{1,0:T(8,128)(2,1)S(1)} custom-call(bf16[512,16,256]{2,1,0:T(8,128)(2,1)} %locked_hbm.1), custom_call_target="tpu_custom_call" | custom-call | tf_op jit(solution)/shard_map/relayout/pallas_call | solution.py:92
  16.2 0.0 collective-permute-done.1.refs_4_
  16.2 0.0 collective-permute-done.4.refs_7_
  16.2 0.0 collective-permute-done.3.refs_6_
  16.2 0.0 collective-permute-done.2.refs_5_
  16.2 5.1 %filter.1 = (f32[40,256]{1,0:T(8,128)S(1)}, f32[40,256]{1,0:T(8,128)S(1)}, f32[16,32,128]{2,1,0:T(8,128)S(1)}) custom-call(s32[1]{0:T(128)} %bitcast.1.refs_0_, s32[1]{0:T(128)} %bitcast.sub_ref.refs_1_.refs_0_, f32[16,40,128]{2,1,0:T(8,128)S(1)} %get-tuple-element.13.refs_2_, f32[16,40,128]{2,1,0:T(8,128)S(1)} %collective-permute-done.refs_3_, ...), custom_call_target="tpu_custom_call" | custom-call | tf_op jit(solution)/shard_map/filter/pallas_call | solution.py:239
  21.3 0.5 %collective-permute-start.5 = (f32[40,256]{1,0:T(8,128)S(1)}, f32[40,256]{1,0:T(8,128)S(1)}, u32[]{:S(2)}, u32[]{:S(2)}) collective-permute-start(f32[40,256]{1,0:T(8,128)S(1)} %get-tuple-element.17), channel_id=1, source_target_pairs={{0,1},{1,0},{2,3},{3,2},{4,5},{5,4},{6,7},{7,6},{8,9},{9,8},{10,11... | collective-permute-start | bytes 122888 | tf_op jit(solution)/shard_map/ppermute | solution.py:362
  21.9 0.9 %collective-permute-done.5 = f32[40,256]{1,0:T(8,128)S(1)} collective-permute-done((f32[40,256]{1,0:T(8,128)S(1)}, f32[40,256]{1,0:T(8,128)S(1)}, u32[]{:S(2)}, u32[]{:S(2)}) %collective-permute-start.5) | collective-permute-done | bytes 40992 | tf_op jit(solution)/shard_map/ppermute | solution.py:362
  22.7 3.9 %collective-permute-start.8 = (f32[40,256]{1,0:T(8,128)S(1)}, f32[40,256]{1,0:T(8,128)S(1)}, u32[]{:S(2)}, u32[]{:S(2)}) collective-permute-start(f32[40,256]{1,0:T(8,128)S(1)} %add.16), channel_id=1, source_target_pairs={{0,12},{4,8},{8,4},{12,0},{1,13},{5,9},{9,5},{13,1},{2,14},{6,10},... | collective-permute-start | bytes 122888 | tf_op jit(solution)/shard_map/ppermute | solution.py:362
  26.6 0.8 %collective-permute-start.7 = (f32[40,256]{1,0:T(8,128)S(1)}, f32[40,256]{1,0:T(8,128)S(1)}, u32[]{:S(2)}, u32[]{:S(2)}) collective-permute-start(f32[40,256]{1,0:T(8,128)S(1)} %add.16), channel_id=1, source_target_pairs={{0,8},{4,12},{8,0},{12,4},{1,9},{5,13},{9,1},{13,5},{2,10},{6,14},... | collective-permute-start | bytes 122888 | tf_op jit(solution)/shard_map/ppermute | solution.py:362
  27.4 0.1 collective-permute-start.6
  27.5 1.2 %collective-permute-done.8 = f32[40,256]{1,0:T(8,128)S(1)} collective-permute-done((f32[40,256]{1,0:T(8,128)S(1)}, f32[40,256]{1,0:T(8,128)S(1)}, u32[]{:S(2)}, u32[]{:S(2)}) %collective-permute-start.8) | collective-permute-done | bytes 40992 | tf_op jit(solution)/shard_map/ppermute | solution.py:362
  28.7 2.9 %collective-permute-done.7 = f32[40,256]{1,0:T(8,128)S(1)} collective-permute-done((f32[40,256]{1,0:T(8,128)S(1)}, f32[40,256]{1,0:T(8,128)S(1)}, u32[]{:S(2)}, u32[]{:S(2)}) %collective-permute-start.7) | collective-permute-done | bytes 40992 | tf_op jit(solution)/shard_map/ppermute | solution.py:362
  31.6 0.2 collective-permute-done.6
  31.9 0.1 collective-permute-start.9
  31.9 1.4 %factor.1 = (f32[32,32]{1,0:T(8,128)}, f32[32,32]{1,0:T(8,128)S(1)}) custom-call(f32[8,128]{1,0:T(8,128)S(1)} %slice.8.refs_0_), custom_call_target="tpu_custom_call" | custom-call | tf_op jit(solution)/shard_map/factor/pallas_call | solution.py:300
  33.4 0.0 collective-permute-done.9.refs_4_
  33.4 1.1 %finish.1 = (f32[32,16,128]{2,1,0:T(8,128)}, f32[32,512]{1,0:T(8,128)}) custom-call(s32[1]{0:T(128)} %bitcast.sub_ref.refs_1_.refs_0_, f32[32,32]{1,0:T(8,128)S(1)} %get-tuple-element.18.refs_1_, f32[16,32,128]{2,1,0:T(8,128)S(1)} %get-tuple-element.19.refs_2_, f32[40,256]{1,0:T(8,128)S(1)} %add_add_fusion.refs_3_, f32[32,256]{1,0:T(8,128)S(1)} %collective-permute-done.9.refs_4_), custom_call_target="tpu_custom_call" | custom-call | tf_op jit(solution)/shard_map/finish/pallas_call | solution.py:345
  (5 shorter events, 0.0 us)
Async XLA Ops:
  1.7 12.0 %collective-permute-start = (f32[16,40,128]{2,1,0:T(8,128)S(1)}, f32[16,40,128]{2,1,0:T(8,128)S(1)}, u32[]{:S(2)}, u32[]{:S(2)}) collective-permute-start(f32[16,40,128]{2,1,0:T(8,128)S(1)} %get-tuple-element.13.refs_2_), channel_id=1, source_target_pairs={{2,0},{0,2},{3,1},{1,3},{6,4},{4,6},{7,5},{5,7},{10,8},{8,10},{11,... | collective-permute-start | bytes 983048 | tf_op jit(solution)/shard_map/ppermute | solution.py:391
  4.7 11.5 %collective-permute-start.4 = (f32[6,40,128]{2,1,0:T(8,128)S(1)}, f32[6,40,128]{2,1,0:T(8,128)S(1)}, u32[]{:S(2)}, u32[]{:S(2)}) collective-permute-start(f32[6,40,128]{2,1,0:T(8,128)S(1)} %get-tuple-element.15), channel_id=1, source_target_pairs={{1,6},{3,4},{4,3},{6,1},{5,10},{7,8},{8,7},{10,5},{9,14},{11,12},{... | collective-permute-start | bytes 368648 | tf_op jit(solution)/shard_map/ppermute | solution.py:405
  5.4 10.8 %collective-permute-start.3 = (f32[6,40,128]{2,1,0:T(8,128)S(1)}, f32[6,40,128]{2,1,0:T(8,128)S(1)}, u32[]{:S(2)}, u32[]{:S(2)}) collective-permute-start(f32[6,40,128]{2,1,0:T(8,128)S(1)} %get-tuple-element.15), channel_id=1, source_target_pairs={{1,4},{3,6},{4,1},{6,3},{5,8},{7,10},{8,5},{10,7},{9,12},{11,14},{... | collective-permute-start | bytes 368648 | tf_op jit(solution)/shard_map/ppermute | solution.py:405
  6.0 10.1 %collective-permute-start.1 = (f32[6,40,128]{2,1,0:T(8,128)S(1)}, f32[6,40,128]{2,1,0:T(8,128)S(1)}, u32[]{:S(2)}, u32[]{:S(2)}) collective-permute-start(f32[6,40,128]{2,1,0:T(8,128)S(1)} %get-tuple-element.14), channel_id=1, source_target_pairs={{0,1},{1,0},{2,3},{3,2},{4,5},{5,4},{6,7},{7,6},{8,9},{9,8},{10,11... | collective-permute-start | bytes 368648 | tf_op jit(solution)/shard_map/ppermute | solution.py:362
  13.7 2.5 %collective-permute-start.2 = (f32[6,40,128]{2,1,0:T(8,128)S(1)}, f32[6,40,128]{2,1,0:T(8,128)S(1)}, u32[]{:S(2)}, u32[]{:S(2)}) collective-permute-start(f32[6,40,128]{2,1,0:T(8,128)S(1)} %constant_dynamic-slice_fusion), channel_id=1, source_target_pairs={{0,1},{1,0},{2,3},{3,2},{4,5},{5,4},{6,7},{7,6},{8,9},{9,8},{10,11... | collective-permute-start | bytes 368648 | tf_op jit(solution)/shard_map/ppermute | solution.py:362
  21.3 1.4 %collective-permute-start.5 = (f32[40,256]{1,0:T(8,128)S(1)}, f32[40,256]{1,0:T(8,128)S(1)}, u32[]{:S(2)}, u32[]{:S(2)}) collective-permute-start(f32[40,256]{1,0:T(8,128)S(1)} %get-tuple-element.17), channel_id=1, source_target_pairs={{0,1},{1,0},{2,3},{3,2},{4,5},{5,4},{6,7},{7,6},{8,9},{9,8},{10,11... | collective-permute-start | bytes 122888 | tf_op jit(solution)/shard_map/ppermute | solution.py:362
  22.7 6.0 %collective-permute-start.8 = (f32[40,256]{1,0:T(8,128)S(1)}, f32[40,256]{1,0:T(8,128)S(1)}, u32[]{:S(2)}, u32[]{:S(2)}) collective-permute-start(f32[40,256]{1,0:T(8,128)S(1)} %add.16), channel_id=1, source_target_pairs={{0,12},{4,8},{8,4},{12,0},{1,13},{5,9},{9,5},{13,1},{2,14},{6,10},... | collective-permute-start | bytes 122888 | tf_op jit(solution)/shard_map/ppermute | solution.py:362
  26.6 5.0 %collective-permute-start.7 = (f32[40,256]{1,0:T(8,128)S(1)}, f32[40,256]{1,0:T(8,128)S(1)}, u32[]{:S(2)}, u32[]{:S(2)}) collective-permute-start(f32[40,256]{1,0:T(8,128)S(1)} %add.16), channel_id=1, source_target_pairs={{0,8},{4,12},{8,0},{12,4},{1,9},{5,13},{9,1},{13,5},{2,10},{6,14},... | collective-permute-start | bytes 122888 | tf_op jit(solution)/shard_map/ppermute | solution.py:362
  27.4 4.5 %collective-permute-start.6 = (f32[40,256]{1,0:T(8,128)S(1)}, f32[40,256]{1,0:T(8,128)S(1)}, u32[]{:S(2)}, u32[]{:S(2)}) collective-permute-start(f32[40,256]{1,0:T(8,128)S(1)} %add.16), channel_id=1, source_target_pairs={{0,4},{4,0},{8,12},{12,8},{1,5},{5,1},{9,13},{13,9},{2,6},{6,2},{1... | collective-permute-start | bytes 122888 | tf_op jit(solution)/shard_map/ppermute | solution.py:362
  31.9 1.5 %collective-permute-start.9 = (f32[32,256]{1,0:T(8,128)S(1)}, f32[32,256]{1,0:T(8,128)S(1)}, u32[]{:S(2)}, u32[]{:S(2)}) collective-permute-start(f32[32,256]{1,0:T(8,128)S(1)} %slice.9), channel_id=1, source_target_pairs={{0,1},{1,0},{2,3},{3,2},{4,5},{5,4},{6,7},{7,6},{8,9},{9,8},{10,11... | collective-permute-start | bytes 98312 | tf_op jit(solution)/shard_map/ppermute | solution.py:362

commit v7 on v6

--- a/solution.py
+++ b/solution.py
@@ -22,7 +22,7 @@
 
 
 def pack_kernel(
-    sub_ref, block_hbm, weights_hbm, mass_hbm, body_ref, near_ref, far_ref,
+    panel_ref, sub_ref, block_hbm, weights_hbm, mass_hbm, body_ref, near_ref, far_ref,
     block_ref, weights_ref, mass_ref, sems,
 ):
     copies = [
@@ -44,12 +44,12 @@
     far_ref[...] = body_ref[pl.ds(sub * (height - HALO), HALO)]
 
 
-def pack(sub, start_block, edge_weights, mass):
+def pack(panel, sub, start_block, edge_weights, mass):
     count, height, width = start_block.shape
     halo = jax.ShapeDtypeStruct((HALO, count + SIDE, width), jnp.float32)
     return pl.pallas_call(
         pack_kernel,
-        in_specs=[SMEM, HBM, HBM, HBM],
+        in_specs=[SMEM, SMEM, HBM, HBM, HBM],
         out_specs=[VMEM, VMEM, VMEM],
         out_shape=[jax.ShapeDtypeStruct((height, count + SIDE, width), jnp.float32), halo, halo],
         scratch_shapes=[
@@ -60,7 +60,7 @@
         ],
         compiler_params=pltpu.CompilerParams(vmem_limit_bytes=8 << 20),
         name="pack",
-    )(sub, *[in_hbm(x) for x in (start_block, edge_weights, mass)])
+    )(panel, sub, *[in_hbm(x) for x in (start_block, edge_weights, mass)])
 
 
 def in_hbm(array):
@@ -101,6 +101,22 @@
         compiler_params=pltpu.CompilerParams(vmem_limit_bytes=12 << 20),
         name="relayout",
     )(in_hbm(locked))
+
+
+def near_kernel(sub_ref, body_ref, ahead_ref, near_ref):
+    height = body_ref.shape[0]
+    near_ref[...] = body_ref[pl.ds((1 - sub_ref[0]) * (height - HALO), HALO)]
+
+
+def near_rows(sub, body, ahead):
+    return pl.pallas_call(
+        near_kernel,
+        in_specs=[SMEM, VMEM, VMEM],
+        out_specs=VMEM,
+        out_shape=jax.ShapeDtypeStruct((HALO,) + body.shape[1:], body.dtype),
+        compiler_params=pltpu.CompilerParams(vmem_limit_bytes=2 << 20),
+        name="near_rows",
+    )(sub, body, ahead)
 
 
 def filter_kernel(panel_ref, sub_ref, *refs, panels, height, count, width):
@@ -384,7 +400,7 @@
     panel = lax.axis_index("panel").astype(jnp.int32).reshape(1)
     sub = lax.axis_index("sub").astype(jnp.int32).reshape(1)
 
-    body, near, far = pack(sub, start_block, edge_weights, mass)
+    body, near, far = pack(panel, sub, start_block, edge_weights, mass)
     bodies = [body]
     for shift in range(1, panels):
         bodies.append(
@@ -405,10 +421,10 @@
         lax.ppermute(far, ("strip", "panel", "sub"), far_moves(shift)) for shift in range(panels)
     ]
     nears = [swap(near, "sub", 1)]
-    first = (1 - sub[0]) * (height - HALO)
+    locked_flat = in_vmem(locked_flat)
     for other in bodies[1:]:
-        nears.append(swap(lax.dynamic_slice_in_dim(other, first, HALO, 0), "sub", 1))
-    keep, send, own = filter_call(panel, sub, bodies, nears, fars, in_vmem(locked_flat))
+        nears.append(swap(near_rows(sub, other, locked_flat), "sub", 1))
+    keep, send, own = filter_call(panel, sub, bodies, nears, fars, locked_flat)
     part = strip_sum(keep + swap(send, "sub", 1))
     other = swap(part[:count], "sub", 1)
     factor, inverse = factorize(part[count:, : count * count // 8], count, vertices)

time: 34.7 us -> 33.5 us (0.965)
  waiting for transfers between devices: 8.67 us -> 7.78 us
  starting transfers between devices: 14 us -> 13.6 us
    ppermute x1, waiting for transfers between devices: 3.43 us -> 1.08 us  [on_device(): lax.ppermute(body, 'panel', [((i + shift) % panels, i) for i in range(pan...]
    ppermute x7, waiting for transfers between devices: 5.23 us -> 6.69 us  [swap(): return lax.ppermute(array, axis, [(i, i ^ distance) for i in range(size)])]
    pallas_call x1 -> x2, Pallas kernels: 1.06 us -> 1.07 us  [the longest x1 1.06 us: pack(): pl.pallas_call(pack_kernel, in_specs=[SMEM, SMEM, HBM, HBM, HBM], out_spe...]
  transfers between devices with their start and end apart: 10 -> 10, of which waited for: 5 -> 6; matrix products, arithmetic and copies ran while one was open for 0% -> 0% of each run, Pallas kernels for 11% -> 11%
where the time goes in v7:
time: 33.5 us; the launch traced here: 33.3 us
  starting transfers between devices  13.6 us (41%)
  Pallas kernels  11.1 us (33%)
  waiting for transfers between devices  7.78 us (23%)
  between operations  0.74 us (2%)
    ppermute x7, starting transfers between devices, swap(): return lax.ppermute(array, axis, [(i, i ^ distance) for i in range(size)])  9.31 us
    ppermute x7, waiting for transfers between devices, swap(): return lax.ppermute(array, axis, [(i, i ^ distance) for i in range(size)])  6.69 us
    pallas_call x1, Pallas kernels, filter_call(): pl.pallas_call(lambda *refs: filter_kernel(*refs, panels=panels, height=h...  5.17 us
    ppermute x1, starting transfers between devices, on_device(): lax.ppermute(body, 'panel', [((i + shift) % panels, i) for i in range(pan...  3 us
    pallas_call x1, Pallas kernels, relayout(): pl.pallas_call(relayout_kernel, in_specs=[HBM], out_specs=VMEM, out_shape...  2.34 us
    pallas_call x1, Pallas kernels, factorize(): pl.pallas_call(lambda *refs: factor_kernel(*refs, vertices=float(vertices...  1.41 us
    ppermute x2, starting transfers between devices, on_device(): lax.ppermute(far, ('strip', 'panel', 'sub'), far_moves(shift))  1.32 us
    pallas_call x1, Pallas kernels, finish(): pl.pallas_call(lambda *refs: finish_kernel(*refs, vertices=float(vertices...  1.1 us
  transfers between devices with their start and end apart: 10, of which 6 were waited for; matrix products, arithmetic and copies ran while one was open for 0% of the time, Pallas kernels for 11%

profile of v7, /device:TPU:0, one launch (start us, length us, event | category | flops | bytes accessed | tf_op | source)
XLA Modules:
  0.0 33.3 jit_solution(14343383103603106890)
XLA Ops:
  0.6 1.1 %pack.1 = (f32[16,40,128]{2,1,0:T(8,128)S(1)}, f32[6,40,128]{2,1,0:T(8,128)S(1)}, f32[6,40,128]{2,1,0:T(8,128)S(1)}) custom-call(s32[1]{0:T(128)} %bitcast.1.panel_ref.refs_0_, s32[1]{0:T(128)} %bitcast.sub_ref.refs_1_.refs_0_, f32[32,16,128]{2,1,0:T(8,128)} %block_hbm.1, f32[8,16,128]{2,1,0:T(8,128)} %weights_hbm.1, f32[16,128]{1,0:T(8,128)} %mass_hbm.1), custom_call_target="tpu_custom_call" | custom-call | tf_op jit(solution)/shard_map/pack/pallas_call | solution.py:50
  1.7 3.0 %collective-permute-start = (f32[16,40,128]{2,1,0:T(8,128)S(1)}, f32[16,40,128]{2,1,0:T(8,128)S(1)}, u32[]{:S(2)}, u32[]{:S(2)}) collective-permute-start(f32[16,40,128]{2,1,0:T(8,128)S(1)} %get-tuple-element.13.refs_2_), channel_id=1, source_target_pairs={{2,0},{0,2},{3,1},{1,3},{6,4},{4,6},{7,5},{5,7},{10,8},{8,10},{11,... | collective-permute-start | bytes 983048 | tf_op jit(solution)/shard_map/ppermute | solution.py:407
  4.7 0.7 %collective-permute-start.4 = (f32[6,40,128]{2,1,0:T(8,128)S(1)}, f32[6,40,128]{2,1,0:T(8,128)S(1)}, u32[]{:S(2)}, u32[]{:S(2)}) collective-permute-start(f32[6,40,128]{2,1,0:T(8,128)S(1)} %get-tuple-element.15), channel_id=1, source_target_pairs={{1,6},{3,4},{4,3},{6,1},{5,10},{7,8},{8,7},{10,5},{9,14},{11,12},{... | collective-permute-start | bytes 368648 | tf_op jit(solution)/shard_map/ppermute | solution.py:421
  5.4 0.7 %collective-permute-start.3 = (f32[6,40,128]{2,1,0:T(8,128)S(1)}, f32[6,40,128]{2,1,0:T(8,128)S(1)}, u32[]{:S(2)}, u32[]{:S(2)}) collective-permute-start(f32[6,40,128]{2,1,0:T(8,128)S(1)} %get-tuple-element.15), channel_id=1, source_target_pairs={{1,4},{3,6},{4,1},{6,3},{5,8},{7,10},{8,5},{10,7},{9,12},{11,14},{... | collective-permute-start | bytes 368648 | tf_op jit(solution)/shard_map/ppermute | solution.py:421
  6.0 4.2 %collective-permute-start.1 = (f32[6,40,128]{2,1,0:T(8,128)S(1)}, f32[6,40,128]{2,1,0:T(8,128)S(1)}, u32[]{:S(2)}, u32[]{:S(2)}) collective-permute-start(f32[6,40,128]{2,1,0:T(8,128)S(1)} %get-tuple-element.14), channel_id=1, source_target_pairs={{0,1},{1,0},{2,3},{3,2},{4,5},{5,4},{6,7},{7,6},{8,9},{9,8},{10,11... | collective-permute-start | bytes 368648 | tf_op jit(solution)/shard_map/ppermute | solution.py:378
  10.3 2.3 %relayout.1.ahead_ref.refs_8_ = bf16[512,4096]{1,0:T(8,128)(2,1)S(1)} custom-call(bf16[512,16,256]{2,1,0:T(8,128)(2,1)} %locked_hbm.1), custom_call_target="tpu_custom_call" | custom-call | tf_op jit(solution)/shard_map/relayout/pallas_call | solution.py:92
  12.6 1.1 %collective-permute-done.body_ref.refs_3_ = f32[16,40,128]{2,1,0:T(8,128)S(1)} collective-permute-done((f32[16,40,128]{2,1,0:T(8,128)S(1)}, f32[16,40,128]{2,1,0:T(8,128)S(1)}, u32[]{:S(2)}, u32[]{:S(2)}) %collective-permute-start) | collective-permute-done | bytes 327712 | tf_op jit(solution)/shard_map/ppermute | solution.py:407
  13.7 0.1 collective-permute-start.2
  13.8 0.0 collective-permute-done.1.refs_4_
  13.8 0.0 collective-permute-done.4.refs_7_
  13.8 0.0 collective-permute-done.3.refs_6_
  13.9 1.3 %collective-permute-done.2.refs_5_ = f32[6,40,128]{2,1,0:T(8,128)S(1)} collective-permute-done((f32[6,40,128]{2,1,0:T(8,128)S(1)}, f32[6,40,128]{2,1,0:T(8,128)S(1)}, u32[]{:S(2)}, u32[]{:S(2)}) %collective-permute-start.2) | collective-permute-done | bytes 122912 | tf_op jit(solution)/shard_map/ppermute | solution.py:378
  15.1 5.2 %filter.1 = (f32[40,256]{1,0:T(8,128)S(1)}, f32[40,256]{1,0:T(8,128)S(1)}, f32[16,32,128]{2,1,0:T(8,128)S(1)}) custom-call(s32[1]{0:T(128)} %bitcast.1.panel_ref.refs_0_, s32[1]{0:T(128)} %bitcast.sub_ref.refs_1_.refs_0_, f32[16,40,128]{2,1,0:T(8,128)S(1)} %get-tuple-element.13.refs_2_, f32[16,40,128]{2,1,0:T(8,128)S(1)} %collective-permute-done.body_ref.refs_3_, ...), custom_call_target="tpu_custom_call" | custom-call | tf_op jit(solution)/shard_map/filter/pallas_call | solution.py:255
  20.3 0.2 collective-permute-start.5
  20.5 1.1 %collective-permute-done.5 = f32[40,256]{1,0:T(8,128)S(1)} collective-permute-done((f32[40,256]{1,0:T(8,128)S(1)}, f32[40,256]{1,0:T(8,128)S(1)}, u32[]{:S(2)}, u32[]{:S(2)}) %collective-permute-start.5) | collective-permute-done | bytes 40992 | tf_op jit(solution)/shard_map/ppermute | solution.py:378
  21.6 3.8 %collective-permute-start.8 = (f32[40,256]{1,0:T(8,128)S(1)}, f32[40,256]{1,0:T(8,128)S(1)}, u32[]{:S(2)}, u32[]{:S(2)}) collective-permute-start(f32[40,256]{1,0:T(8,128)S(1)} %add.12), channel_id=1, source_target_pairs={{0,12},{4,8},{8,4},{12,0},{1,13},{5,9},{9,5},{13,1},{2,14},{6,10},... | collective-permute-start | bytes 122888 | tf_op jit(solution)/shard_map/ppermute | solution.py:378
  25.4 0.8 %collective-permute-start.7 = (f32[40,256]{1,0:T(8,128)S(1)}, f32[40,256]{1,0:T(8,128)S(1)}, u32[]{:S(2)}, u32[]{:S(2)}) collective-permute-start(f32[40,256]{1,0:T(8,128)S(1)} %add.12), channel_id=1, source_target_pairs={{0,8},{4,12},{8,0},{12,4},{1,9},{5,13},{9,1},{13,5},{2,10},{6,14},... | collective-permute-start | bytes 122888 | tf_op jit(solution)/shard_map/ppermute | solution.py:378
  26.2 0.1 collective-permute-start.6
  26.3 1.2 %collective-permute-done.8 = f32[40,256]{1,0:T(8,128)S(1)} collective-permute-done((f32[40,256]{1,0:T(8,128)S(1)}, f32[40,256]{1,0:T(8,128)S(1)}, u32[]{:S(2)}, u32[]{:S(2)}) %collective-permute-start.8) | collective-permute-done | bytes 40992 | tf_op jit(solution)/shard_map/ppermute | solution.py:378
  27.5 2.9 %collective-permute-done.7 = f32[40,256]{1,0:T(8,128)S(1)} collective-permute-done((f32[40,256]{1,0:T(8,128)S(1)}, f32[40,256]{1,0:T(8,128)S(1)}, u32[]{:S(2)}, u32[]{:S(2)}) %collective-permute-start.7) | collective-permute-done | bytes 40992 | tf_op jit(solution)/shard_map/ppermute | solution.py:378
  30.5 0.2 collective-permute-done.6
  30.7 0.1 collective-permute-start.9
  30.8 1.4 %factor.1 = (f32[32,32]{1,0:T(8,128)}, f32[32,32]{1,0:T(8,128)S(1)}) custom-call(f32[8,128]{1,0:T(8,128)S(1)} %slice.8.refs_0_), custom_call_target="tpu_custom_call" | custom-call | tf_op jit(solution)/shard_map/factor/pallas_call | solution.py:316
  32.2 0.0 collective-permute-done.9.refs_4_
  32.2 1.1 %finish.1 = (f32[32,16,128]{2,1,0:T(8,128)}, f32[32,512]{1,0:T(8,128)}) custom-call(s32[1]{0:T(128)} %bitcast.sub_ref.refs_1_.refs_0_, f32[32,32]{1,0:T(8,128)S(1)} %get-tuple-element.18.refs_1_, f32[16,32,128]{2,1,0:T(8,128)S(1)} %get-tuple-element.19.refs_2_, f32[40,256]{1,0:T(8,128)S(1)} %add_add_fusion.refs_3_, f32[32,256]{1,0:T(8,128)S(1)} %collective-permute-done.9.refs_4_), custom_call_target="tpu_custom_call" | custom-call | tf_op jit(solution)/shard_map/finish/pallas_call | solution.py:361
  (5 shorter events, 0.0 us)
Async XLA Ops:
  1.7 12.0 %collective-permute-start = (f32[16,40,128]{2,1,0:T(8,128)S(1)}, f32[16,40,128]{2,1,0:T(8,128)S(1)}, u32[]{:S(2)}, u32[]{:S(2)}) collective-permute-start(f32[16,40,128]{2,1,0:T(8,128)S(1)} %get-tuple-element.13.refs_2_), channel_id=1, source_target_pairs={{2,0},{0,2},{3,1},{1,3},{6,4},{4,6},{7,5},{5,7},{10,8},{8,10},{11,... | collective-permute-start | bytes 983048 | tf_op jit(solution)/shard_map/ppermute | solution.py:407
  4.7 9.1 %collective-permute-start.4 = (f32[6,40,128]{2,1,0:T(8,128)S(1)}, f32[6,40,128]{2,1,0:T(8,128)S(1)}, u32[]{:S(2)}, u32[]{:S(2)}) collective-permute-start(f32[6,40,128]{2,1,0:T(8,128)S(1)} %get-tuple-element.15), channel_id=1, source_target_pairs={{1,6},{3,4},{4,3},{6,1},{5,10},{7,8},{8,7},{10,5},{9,14},{11,12},{... | collective-permute-start | bytes 368648 | tf_op jit(solution)/shard_map/ppermute | solution.py:421
  5.4 8.5 %collective-permute-start.3 = (f32[6,40,128]{2,1,0:T(8,128)S(1)}, f32[6,40,128]{2,1,0:T(8,128)S(1)}, u32[]{:S(2)}, u32[]{:S(2)}) collective-permute-start(f32[6,40,128]{2,1,0:T(8,128)S(1)} %get-tuple-element.15), channel_id=1, source_target_pairs={{1,4},{3,6},{4,1},{6,3},{5,8},{7,10},{8,5},{10,7},{9,12},{11,14},{... | collective-permute-start | bytes 368648 | tf_op jit(solution)/shard_map/ppermute | solution.py:421
  6.0 7.8 %collective-permute-start.1 = (f32[6,40,128]{2,1,0:T(8,128)S(1)}, f32[6,40,128]{2,1,0:T(8,128)S(1)}, u32[]{:S(2)}, u32[]{:S(2)}) collective-permute-start(f32[6,40,128]{2,1,0:T(8,128)S(1)} %get-tuple-element.14), channel_id=1, source_target_pairs={{0,1},{1,0},{2,3},{3,2},{4,5},{5,4},{6,7},{7,6},{8,9},{9,8},{10,11... | collective-permute-start | bytes 368648 | tf_op jit(solution)/shard_map/ppermute | solution.py:378
  13.7 1.4 %collective-permute-start.2 = (f32[6,40,128]{2,1,0:T(8,128)S(1)}, f32[6,40,128]{2,1,0:T(8,128)S(1)}, u32[]{:S(2)}, u32[]{:S(2)}) collective-permute-start(f32[6,40,128]{2,1,0:T(8,128)S(1)} %near_rows.1), channel_id=1, source_target_pairs={{0,1},{1,0},{2,3},{3,2},{4,5},{5,4},{6,7},{7,6},{8,9},{9,8},{10,11... | collective-permute-start | bytes 368648 | tf_op jit(solution)/shard_map/ppermute | solution.py:378
  20.3 1.3 %collective-permute-start.5 = (f32[40,256]{1,0:T(8,128)S(1)}, f32[40,256]{1,0:T(8,128)S(1)}, u32[]{:S(2)}, u32[]{:S(2)}) collective-permute-start(f32[40,256]{1,0:T(8,128)S(1)} %get-tuple-element.17), channel_id=1, source_target_pairs={{0,1},{1,0},{2,3},{3,2},{4,5},{5,4},{6,7},{7,6},{8,9},{9,8},{10,11... | collective-permute-start | bytes 122888 | tf_op jit(solution)/shard_map/ppermute | solution.py:378
  21.6 5.9 %collective-permute-start.8 = (f32[40,256]{1,0:T(8,128)S(1)}, f32[40,256]{1,0:T(8,128)S(1)}, u32[]{:S(2)}, u32[]{:S(2)}) collective-permute-start(f32[40,256]{1,0:T(8,128)S(1)} %add.12), channel_id=1, source_target_pairs={{0,12},{4,8},{8,4},{12,0},{1,13},{5,9},{9,5},{13,1},{2,14},{6,10},... | collective-permute-start | bytes 122888 | tf_op jit(solution)/shard_map/ppermute | solution.py:378
  25.4 5.0 %collective-permute-start.7 = (f32[40,256]{1,0:T(8,128)S(1)}, f32[40,256]{1,0:T(8,128)S(1)}, u32[]{:S(2)}, u32[]{:S(2)}) collective-permute-start(f32[40,256]{1,0:T(8,128)S(1)} %add.12), channel_id=1, source_target_pairs={{0,8},{4,12},{8,0},{12,4},{1,9},{5,13},{9,1},{13,5},{2,10},{6,14},... | collective-permute-start | bytes 122888 | tf_op jit(solution)/shard_map/ppermute | solution.py:378
  26.2 4.4 %collective-permute-start.6 = (f32[40,256]{1,0:T(8,128)S(1)}, f32[40,256]{1,0:T(8,128)S(1)}, u32[]{:S(2)}, u32[]{:S(2)}) collective-permute-start(f32[40,256]{1,0:T(8,128)S(1)} %add.12), channel_id=1, source_target_pairs={{0,4},{4,0},{8,12},{12,8},{1,5},{5,1},{9,13},{13,9},{2,6},{6,2},{1... | collective-permute-start | bytes 122888 | tf_op jit(solution)/shard_map/ppermute | solution.py:378
  30.7 1.5 %collective-permute-start.9 = (f32[32,256]{1,0:T(8,128)S(1)}, f32[32,256]{1,0:T(8,128)S(1)}, u32[]{:S(2)}, u32[]{:S(2)}) collective-permute-start(f32[32,256]{1,0:T(8,128)S(1)} %slice.9), channel_id=1, source_target_pairs={{0,1},{1,0},{2,3},{3,2},{4,5},{5,4},{6,7},{7,6},{8,9},{9,8},{10,11... | collective-permute-start | bytes 98312 | tf_op jit(solution)/shard_map/ppermute | solution.py:378

commit v8 on v6

--- a/solution.py
+++ b/solution.py
@@ -14,7 +14,7 @@
 SPREAD = 0.5 * (CUT_HIGH - CUT_LOW)
 HALO = DEGREE
 GRID_ROWS = ("strip", "sub")
-SIDE = 8
+SIDE = 5
 
 VMEM = pl.BlockSpec(memory_space=pltpu.VMEM)
 SMEM = pl.BlockSpec(memory_space=pltpu.SMEM)
@@ -22,7 +22,7 @@
 
 
 def pack_kernel(
-    sub_ref, block_hbm, weights_hbm, mass_hbm, body_ref, near_ref, far_ref,
+    panel_ref, sub_ref, block_hbm, weights_hbm, mass_hbm, body_ref,
     block_ref, weights_ref, mass_ref, sems,
 ):
     copies = [
@@ -35,23 +35,20 @@
     for copy in copies:
         copy.wait()
     count, height, width = block_ref.shape
-    body_ref[:, 0:count, :] = pltpu.einshape("brc->rbc", block_ref[...])
-    mass = mass_ref[...][None]
-    side = jnp.concatenate([weights_ref[...], mass, mass, mass, mass], axis=0)
-    body_ref[:, count : count + SIDE, :] = pltpu.einshape("brc->rbc", side)
-    sub = sub_ref[0]
-    near_ref[...] = body_ref[pl.ds((1 - sub) * (height - HALO), HALO)]
-    far_ref[...] = body_ref[pl.ds(sub * (height - HALO), HALO)]
-
-
-def pack(sub, start_block, edge_weights, mass):
+    body_ref[0 : height * count] = pltpu.einshape("brc->rbc", block_ref[...]).reshape(-1, width)
+    for d in range(SIDE - 1):
+        at = height * (count + d)
+        body_ref[at : at + height] = weights_ref[d]
+    body_ref[height * (count + SIDE - 1) :] = mass_ref[...]
+
+
+def pack(panel, sub, start_block, edge_weights, mass):
     count, height, width = start_block.shape
-    halo = jax.ShapeDtypeStruct((HALO, count + SIDE, width), jnp.float32)
     return pl.pallas_call(
         pack_kernel,
-        in_specs=[SMEM, HBM, HBM, HBM],
-        out_specs=[VMEM, VMEM, VMEM],
-        out_shape=[jax.ShapeDtypeStruct((height, count + SIDE, width), jnp.float32), halo, halo],
+        in_specs=[SMEM, SMEM, HBM, HBM, HBM],
+        out_specs=VMEM,
+        out_shape=jax.ShapeDtypeStruct((height * (count + SIDE), width), jnp.float32),
         scratch_shapes=[
             pltpu.VMEM((count, height, width), jnp.float32),
             pltpu.VMEM((4, height, width), jnp.float32),
@@ -60,7 +57,7 @@
         ],
         compiler_params=pltpu.CompilerParams(vmem_limit_bytes=8 << 20),
         name="pack",
-    )(sub, *[in_hbm(x) for x in (start_block, edge_weights, mass)])
+    )(panel, sub, *[in_hbm(x) for x in (start_block, edge_weights, mass)])
 
 
 def in_hbm(array):
@@ -103,6 +100,31 @@
     )(in_hbm(locked))
 
 
+def edge_kernel(sub_ref, body_ref, *refs, height, count, sides):
+    sub = sub_ref[0]
+    out_refs = refs[-sides:]
+    for out_ref, at in zip(out_refs, (1 - sub, sub)):
+        start = pl.multiple_of(at * ((height - HALO) * count), 8)
+        out_ref[0 : HALO * count] = body_ref[pl.ds(start, HALO * count)]
+        for d in range(SIDE):
+            start = pl.multiple_of(height * (count + d) + at * (height - 8), 8)
+            to = HALO * count + 8 * d
+            out_ref[to : to + 8] = body_ref[pl.ds(start, 8)]
+
+
+def edge_rows(sub, body, ahead, sides, height):
+    count = body.shape[0] // height - SIDE
+    rows = jax.ShapeDtypeStruct((HALO * count + 8 * SIDE, body.shape[1]), body.dtype)
+    return pl.pallas_call(
+        lambda *refs: edge_kernel(*refs, height=height, count=count, sides=sides),
+        in_specs=[SMEM] + [VMEM] * (1 + len(ahead)),
+        out_specs=[VMEM] * sides,
+        out_shape=[rows] * sides,
+        compiler_params=pltpu.CompilerParams(vmem_limit_bytes=2 << 20),
+        name="edge_rows",
+    )(sub, body, *ahead)
+
+
 def filter_kernel(panel_ref, sub_ref, *refs, panels, height, count, width):
     bodies = refs[0:panels]
     nears = refs[panels : 2 * panels]
@@ -113,15 +135,31 @@
     panel = panel_ref[0]
     first_sub = sub_ref[0] == 0
 
-    def source(row):
+    def fetch(row, own, above, below, size):
         if HALO <= row < HALO + height:
-            parts = [b[row - HALO] for b in bodies]
+            parts = [b[own : own + size] for b in bodies]
         elif row < HALO:
-            parts = [jnp.where(first_sub, f[row], n[row]) for n, f in zip(nears, fars)]
+            at = slice(above, above + size)
+            parts = [jnp.where(first_sub, f[at], n[at]) for n, f in zip(nears, fars)]
         else:
-            at = row - HALO - height
+            at = slice(below, below + size)
             parts = [jnp.where(first_sub, n[at], f[at]) for n, f in zip(nears, fars)]
         return jnp.concatenate(parts, axis=1)
+
+    def vectors(row):
+        return fetch(
+            row, (row - HALO) * count, row * count, (row - HALO - height) * count, count
+        )
+
+    def side(row, d):
+        base = HALO * count + 8 * d
+        return fetch(
+            row,
+            height * (count + d) + row - HALO,
+            base + row + 8 - HALO,
+            base + row - HALO - height,
+            1,
+        )
 
     lane = lax.broadcasted_iota(jnp.int32, (1, total), 1)
     column = lax.rem(lane + panel * width, total)
@@ -139,13 +177,11 @@
     weights = []
     scale = []
     for row in range(rows):
-        full = source(row)
-        y_even[row] = full[0:count]
-        side = full[count : count + SIDE]
-        mass = side[4:5]
+        y_even[row] = vectors(row)
+        mass = side(row, SIDE - 1)
         inside = mass > 0.0
         scale.append(jnp.where(inside, 1.0 / jnp.sqrt(jnp.where(inside, mass, 1.0)), 0.0))
-        weights.append([side[d : d + 1] for d in range(4)])
+        weights.append([side(row, d) for d in range(SIDE - 1)])
     edges = []
     for row in range(rows - 1):
         s0 = scale[row]
@@ -212,11 +248,16 @@
     half = products.shape[1] // 2
     lower = products[:, 0:half]
     upper = products[:, half:]
-    keep_ref[0:count] = jnp.where(first_sub, lower, upper)
-    send_ref[0:count] = jnp.where(first_sub, upper, lower)
-    dense = fold(gram, half)
-    keep_ref[count : count + 8] = dense
-    send_ref[count : count + 8] = dense
+    keep = jnp.where(first_sub, lower, upper)
+    send = jnp.where(first_sub, upper, lower)
+    for at in range(0, half, 128):
+        to = count * (at // 128)
+        keep_ref[to : to + count] = keep[:, at : at + 128]
+        send_ref[to : to + count] = send[:, at : at + 128]
+    to = count * (half // 128)
+    dense = fold(gram, 128)
+    keep_ref[to : to + 8] = dense
+    send_ref[to : to + 8] = dense
 
 
 def fold(gram, width):
@@ -228,14 +269,14 @@
     return jnp.concatenate(parts, axis=1)
 
 
-def filter_call(panel, sub, bodies, nears, fars, locked_flat):
+def filter_call(panel, sub, bodies, nears, fars, locked_flat, height):
     panels = len(bodies)
-    height, planes, width = bodies[0].shape
-    count = planes - SIDE
+    width = bodies[0].shape[1]
+    count = bodies[0].shape[0] // height - SIDE
     basis = locked_flat.shape[0]
     total = panels * width
     rows = height + 2 * HALO
-    payload = jax.ShapeDtypeStruct((count + 8, basis // 2), jnp.float32)
+    payload = jax.ShapeDtypeStruct((count * (basis // 256) + 8, 128), jnp.float32)
     return pl.pallas_call(
         lambda *refs: filter_kernel(*refs, panels=panels, height=height, count=count, width=width),
         in_specs=[SMEM, SMEM] + [VMEM] * (3 * panels + 1),
@@ -313,9 +354,7 @@
 ):
     height, count, width = own_ref.shape
     first_sub = sub_ref[0] == 0
-    half = mine_ref.shape[1]
-    mine = mine_ref[0:count]
-    other = other_ref[...]
+    blocks = other_ref.shape[0] // count
     inverse = inverse_ref[...]
 
     def times(left, right):
@@ -330,8 +369,14 @@
     ortho_copy = pltpu.make_async_copy(ortho_ref, ortho_hbm, sems.at[0])
     ortho_copy.start()
     inverse = inverse * (1.0 / math.sqrt(vertices))
-    coupling_ref[:, 0:half] = times(inverse, jnp.where(first_sub, mine, other))
-    coupling_ref[:, half:] = times(inverse, jnp.where(first_sub, other, mine))
+    for i in range(blocks):
+        mine = mine_ref[i * count : (i + 1) * count]
+        other = other_ref[i * count : (i + 1) * count]
+        for at, part in (
+            (i, jnp.where(first_sub, mine, other)),
+            (blocks + i, jnp.where(first_sub, other, mine)),
+        ):
+            coupling_ref[:, at * 128 : (at + 1) * 128] = times(inverse, part)
     coupling_copy = pltpu.make_async_copy(coupling_ref, coupling_hbm, sems.at[1])
     coupling_copy.start()
     ortho_copy.wait()
@@ -341,7 +386,7 @@
 def finish(sub, inverse, own, mine, other, vertices):
     height, count, width = own.shape
     ortho = (count, height, width)
-    coupling = (count, 2 * mine.shape[1])
+    coupling = (count, 256 * (other.shape[0] // count))
     return pl.pallas_call(
         lambda *refs: finish_kernel(*refs, vertices=float(vertices)),
         in_specs=[SMEM, VMEM, VMEM, VMEM, VMEM],
@@ -384,13 +429,14 @@
     panel = lax.axis_index("panel").astype(jnp.int32).reshape(1)
     sub = lax.axis_index("sub").astype(jnp.int32).reshape(1)
 
-    body, near, far = pack(sub, start_block, edge_weights, mass)
+    body = pack(panel, sub, start_block, edge_weights, mass)
     bodies = [body]
     for shift in range(1, panels):
         bodies.append(
             lax.ppermute(body, "panel", [((i + shift) % panels, i) for i in range(panels)])
         )
-    locked_flat = relayout(locked)
+    locked_flat = in_vmem(relayout(locked))
+    near, far = edge_rows(sub, body, [], 2, height)
 
     def far_moves(shift):
         moves = []
@@ -405,13 +451,13 @@
         lax.ppermute(far, ("strip", "panel", "sub"), far_moves(shift)) for shift in range(panels)
     ]
     nears = [swap(near, "sub", 1)]
-    first = (1 - sub[0]) * (height - HALO)
     for other in bodies[1:]:
-        nears.append(swap(lax.dynamic_slice_in_dim(other, first, HALO, 0), "sub", 1))
-    keep, send, own = filter_call(panel, sub, bodies, nears, fars, in_vmem(locked_flat))
+        nears.append(swap(edge_rows(sub, other, [locked_flat], 1, height)[0], "sub", 1))
+    keep, send, own = filter_call(panel, sub, bodies, nears, fars, locked_flat, height)
     part = strip_sum(keep + swap(send, "sub", 1))
-    other = swap(part[:count], "sub", 1)
-    factor, inverse = factorize(part[count:, : count * count // 8], count, vertices)
+    grams = part.shape[0] - 8
+    other = swap(part[:grams], "sub", 1)
+    factor, inverse = factorize(part[grams:, : count * count // 8], count, vertices)
     ortho, coupling = finish(sub, inverse, own, part, other, vertices)
     return (ortho, jnp.transpose(coupling), factor)
 

time: 34.7 us -> 32.7 us (0.942)
  waiting for transfers between devices: 8.67 us -> 7.08 us
  starting transfers between devices: 14 us -> 13.6 us
    ppermute x1, waiting for transfers between devices: 3.43 us -> 0.48 us  [on_device(): lax.ppermute(body, 'panel', [((i + shift) % panels, i) for i in range(pan...]
    ppermute x7, waiting for transfers between devices: 5.23 us -> 6.59 us  [swap(): return lax.ppermute(array, axis, [(i, i ^ distance) for i in range(size)])]
    ppermute x7, starting transfers between devices: 9.65 us -> 9.26 us  [swap(): return lax.ppermute(array, axis, [(i, i ^ distance) for i in range(size)])]
    pallas_call x1 -> x3, Pallas kernels: 1.06 us -> 1.06 us  [the longest x1 1.03 us: pack(): pl.pallas_call(pack_kernel, in_specs=[SMEM, SMEM, HBM, HBM, HBM], out_spe...]
  transfers between devices with their start and end apart: 10 -> 10, of which waited for: 5 -> 6; matrix products, arithmetic and copies ran while one was open for 0% -> 0% of each run, Pallas kernels for 11% -> 12%
where the time goes in v8:
time: 32.7 us; the launch traced here: 32.4 us
  starting transfers between devices  13.6 us (42%)
  Pallas kernels  11 us (34%)
  waiting for transfers between devices  7.08 us (22%)
  between operations  0.74 us (2%)
    ppermute x7, starting transfers between devices, swap(): return lax.ppermute(array, axis, [(i, i ^ distance) for i in range(size)])  9.26 us
    ppermute x7, waiting for transfers between devices, swap(): return lax.ppermute(array, axis, [(i, i ^ distance) for i in range(size)])  6.59 us
    pallas_call x1, Pallas kernels, filter_call(): pl.pallas_call(lambda *refs: filter_kernel(*refs, panels=panels, height=h...  5.1 us
    ppermute x1, starting transfers between devices, on_device(): lax.ppermute(body, 'panel', [((i + shift) % panels, i) for i in range(pan...  3 us
    pallas_call x1, Pallas kernels, relayout(): pl.pallas_call(relayout_kernel, in_specs=[HBM], out_specs=VMEM, out_shape...  2.34 us
    pallas_call x1, Pallas kernels, factorize(): pl.pallas_call(lambda *refs: factor_kernel(*refs, vertices=float(vertices...  1.41 us
    ppermute x2, starting transfers between devices, on_device(): lax.ppermute(far, ('strip', 'panel', 'sub'), far_moves(shift))  1.34 us
    pallas_call x1, Pallas kernels, finish(): pl.pallas_call(lambda *refs: finish_kernel(*refs, vertices=float(vertices...  1.09 us
  transfers between devices with their start and end apart: 10, of which 6 were waited for; matrix products, arithmetic and copies ran while one was open for 0% of the time, Pallas kernels for 12%

profile of v8, /device:TPU:0, one launch (start us, length us, event | category | flops | bytes accessed | tf_op | source)
XLA Modules:
  0.0 32.4 jit_solution(3250314580356070460)
XLA Ops:
  0.6 1.0 %pack.1.refs_1_.refs_2_ = f32[592,128]{1,0:T(8,128)S(1)} custom-call(s32[1]{0:T(128)} %bitcast.1.panel_ref.refs_0_, s32[1]{0:T(128)} %bitcast.sub_ref.refs_0_.refs_1_, f32[32,16,128]{2,1,0:T(8,128)} %block_hbm.1, f32[8,16,128]{2,1,0:T(8,128)} %weights_hbm.1, f32[16,128]{1,0:T(8,128)} %mass_hbm.1), custom_call_target="tpu_custom_call" | custom-call | tf_op jit(solution)/shard_map/pack/pallas_call | solution.py:47
  1.7 3.0 %collective-permute-start = (f32[592,128]{1,0:T(8,128)S(1)}, f32[592,128]{1,0:T(8,128)S(1)}, u32[]{:S(2)}, u32[]{:S(2)}) collective-permute-start(f32[592,128]{1,0:T(8,128)S(1)} %pack.1.refs_1_.refs_2_), channel_id=1, source_target_pairs={{2,0},{0,2},{3,1},{1,3},{6,4},{4,6},{7,5},{5,7},{10,8},{8,10},{11,... | collective-permute-start | bytes 909320 | tf_op jit(solution)/shard_map/ppermute | solution.py:436
  4.7 0.7 %collective-permute-start.4 = (f32[232,128]{1,0:T(8,128)S(1)}, f32[232,128]{1,0:T(8,128)S(1)}, u32[]{:S(2)}, u32[]{:S(2)}) collective-permute-start(f32[232,128]{1,0:T(8,128)S(1)} %get-tuple-element.13), channel_id=1, source_target_pairs={{1,6},{3,4},{4,3},{6,1},{5,10},{7,8},{8,7},{10,5},{9,14},{11,12},{... | collective-permute-start | bytes 356360 | tf_op jit(solution)/shard_map/ppermute | solution.py:451
  5.4 0.7 %collective-permute-start.3 = (f32[232,128]{1,0:T(8,128)S(1)}, f32[232,128]{1,0:T(8,128)S(1)}, u32[]{:S(2)}, u32[]{:S(2)}) collective-permute-start(f32[232,128]{1,0:T(8,128)S(1)} %get-tuple-element.13), channel_id=1, source_target_pairs={{1,4},{3,6},{4,1},{6,3},{5,8},{7,10},{8,5},{10,7},{9,12},{11,14},{... | collective-permute-start | bytes 356360 | tf_op jit(solution)/shard_map/ppermute | solution.py:451
  6.1 4.2 %collective-permute-start.1 = (f32[232,128]{1,0:T(8,128)S(1)}, f32[232,128]{1,0:T(8,128)S(1)}, u32[]{:S(2)}, u32[]{:S(2)}) collective-permute-start(f32[232,128]{1,0:T(8,128)S(1)} %get-tuple-element.12), channel_id=1, source_target_pairs={{0,1},{1,0},{2,3},{3,2},{4,5},{5,4},{6,7},{7,6},{8,9},{9,8},{10,11... | collective-permute-start | bytes 356360 | tf_op jit(solution)/shard_map/ppermute | solution.py:407
  10.3 2.3 %relayout.1.refs_2_.refs_8_ = bf16[512,4096]{1,0:T(8,128)(2,1)S(1)} custom-call(bf16[512,16,256]{2,1,0:T(8,128)(2,1)} %locked_hbm.1), custom_call_target="tpu_custom_call" | custom-call | tf_op jit(solution)/shard_map/relayout/pallas_call | solution.py:89
  12.7 0.5 %collective-permute-done.refs_1_.refs_3_ = f32[592,128]{1,0:T(8,128)S(1)} collective-permute-done((f32[592,128]{1,0:T(8,128)S(1)}, f32[592,128]{1,0:T(8,128)S(1)}, u32[]{:S(2)}, u32[]{:S(2)}) %collective-permute-start) | collective-permute-done | bytes 303136 | tf_op jit(solution)/shard_map/ppermute | solution.py:436
  13.1 0.1 collective-permute-start.2
  13.2 0.0 collective-permute-done.1.refs_4_
  13.2 0.0 collective-permute-done.4.refs_7_
  13.2 0.0 collective-permute-done.3.refs_6_
  13.3 1.3 %collective-permute-done.2.refs_5_ = f32[232,128]{1,0:T(8,128)S(1)} collective-permute-done((f32[232,128]{1,0:T(8,128)S(1)}, f32[232,128]{1,0:T(8,128)S(1)}, u32[]{:S(2)}, u32[]{:S(2)}) %collective-permute-start.2) | collective-permute-done | bytes 118816 | tf_op jit(solution)/shard_map/ppermute | solution.py:407
  14.5 5.1 %filter.1 = (f32[72,128]{1,0:T(8,128)S(1)}, f32[72,128]{1,0:T(8,128)S(1)}, f32[16,32,128]{2,1,0:T(8,128)S(1)}) custom-call(s32[1]{0:T(128)} %bitcast.1.panel_ref.refs_0_, s32[1]{0:T(128)} %bitcast.sub_ref.refs_0_.refs_1_, f32[592,128]{1,0:T(8,128)S(1)} %pack.1.refs_1_.refs_2_, f32[592,128]{1,0:T(8,128)S(1)} %collective-permute-done.refs_1_.refs_3_, ...), custom_call_target="tpu_custom_call" | custom-call | tf_op jit(solution)/shard_map/filter/pallas_call | solution.py:280
  19.6 0.2 collective-permute-start.5
  19.8 1.1 %collective-permute-done.5 = f32[72,128]{1,0:T(8,128)S(1)} collective-permute-done((f32[72,128]{1,0:T(8,128)S(1)}, f32[72,128]{1,0:T(8,128)S(1)}, u32[]{:S(2)}, u32[]{:S(2)}) %collective-permute-start.5) | collective-permute-done | bytes 36896 | tf_op jit(solution)/shard_map/ppermute | solution.py:407
  20.9 3.8 %collective-permute-start.8 = (f32[72,128]{1,0:T(8,128)S(1)}, f32[72,128]{1,0:T(8,128)S(1)}, u32[]{:S(2)}, u32[]{:S(2)}) collective-permute-start(f32[72,128]{1,0:T(8,128)S(1)} %add.12), channel_id=1, source_target_pairs={{0,12},{4,8},{8,4},{12,0},{1,13},{5,9},{9,5},{13,1},{2,14},{6,10},... | collective-permute-start | bytes 110600 | tf_op jit(solution)/shard_map/ppermute | solution.py:407
  24.8 0.7 %collective-permute-start.7 = (f32[72,128]{1,0:T(8,128)S(1)}, f32[72,128]{1,0:T(8,128)S(1)}, u32[]{:S(2)}, u32[]{:S(2)}) collective-permute-start(f32[72,128]{1,0:T(8,128)S(1)} %add.12), channel_id=1, source_target_pairs={{0,8},{4,12},{8,0},{12,4},{1,9},{5,13},{9,1},{13,5},{2,10},{6,14},... | collective-permute-start | bytes 110600 | tf_op jit(solution)/shard_map/ppermute | solution.py:407
  25.5 0.1 collective-permute-start.6
  25.6 1.2 %collective-permute-done.8 = f32[72,128]{1,0:T(8,128)S(1)} collective-permute-done((f32[72,128]{1,0:T(8,128)S(1)}, f32[72,128]{1,0:T(8,128)S(1)}, u32[]{:S(2)}, u32[]{:S(2)}) %collective-permute-start.8) | collective-permute-done | bytes 36896 | tf_op jit(solution)/shard_map/ppermute | solution.py:407
  26.8 2.9 %collective-permute-done.7 = f32[72,128]{1,0:T(8,128)S(1)} collective-permute-done((f32[72,128]{1,0:T(8,128)S(1)}, f32[72,128]{1,0:T(8,128)S(1)}, u32[]{:S(2)}, u32[]{:S(2)}) %collective-permute-start.7) | collective-permute-done | bytes 36896 | tf_op jit(solution)/shard_map/ppermute | solution.py:407
  29.8 0.1 collective-permute-done.6
  29.8 0.1 collective-permute-start.9
  29.9 1.4 %factor.1 = (f32[32,32]{1,0:T(8,128)}, f32[32,32]{1,0:T(8,128)S(1)}) custom-call(f32[8,128]{1,0:T(8,128)S(1)} %slice.8.refs_0_), custom_call_target="tpu_custom_call" | custom-call | tf_op jit(solution)/shard_map/factor/pallas_call | solution.py:341
  31.3 0.0 collective-permute-done.9.refs_4_
  31.4 1.1 %finish.1 = (f32[32,16,128]{2,1,0:T(8,128)}, f32[32,512]{1,0:T(8,128)}) custom-call(s32[1]{0:T(128)} %bitcast.sub_ref.refs_0_.refs_1_, f32[32,32]{1,0:T(8,128)S(1)} %get-tuple-element.16.refs_1_, f32[16,32,128]{2,1,0:T(8,128)S(1)} %get-tuple-element.17.refs_2_, f32[72,128]{1,0:T(8,128)S(1)} %add_add_fusion.refs_3_, f32[64,128]{1,0:T(8,128)S(1)} %collective-permute-done.9.refs_4_), custom_call_target="tpu_custom_call" | custom-call | tf_op jit(solution)/shard_map/finish/pallas_call | solution.py:390
  (6 shorter events, 0.1 us)
Async XLA Ops:
  1.7 11.5 %collective-permute-start = (f32[592,128]{1,0:T(8,128)S(1)}, f32[592,128]{1,0:T(8,128)S(1)}, u32[]{:S(2)}, u32[]{:S(2)}) collective-permute-start(f32[592,128]{1,0:T(8,128)S(1)} %pack.1.refs_1_.refs_2_), channel_id=1, source_target_pairs={{2,0},{0,2},{3,1},{1,3},{6,4},{4,6},{7,5},{5,7},{10,8},{8,10},{11,... | collective-permute-start | bytes 909320 | tf_op jit(solution)/shard_map/ppermute | solution.py:436
  4.7 8.5 %collective-permute-start.4 = (f32[232,128]{1,0:T(8,128)S(1)}, f32[232,128]{1,0:T(8,128)S(1)}, u32[]{:S(2)}, u32[]{:S(2)}) collective-permute-start(f32[232,128]{1,0:T(8,128)S(1)} %get-tuple-element.13), channel_id=1, source_target_pairs={{1,6},{3,4},{4,3},{6,1},{5,10},{7,8},{8,7},{10,5},{9,14},{11,12},{... | collective-permute-start | bytes 356360 | tf_op jit(solution)/shard_map/ppermute | solution.py:451
  5.4 7.9 %collective-permute-start.3 = (f32[232,128]{1,0:T(8,128)S(1)}, f32[232,128]{1,0:T(8,128)S(1)}, u32[]{:S(2)}, u32[]{:S(2)}) collective-permute-start(f32[232,128]{1,0:T(8,128)S(1)} %get-tuple-element.13), channel_id=1, source_target_pairs={{1,4},{3,6},{4,1},{6,3},{5,8},{7,10},{8,5},{10,7},{9,12},{11,14},{... | collective-permute-start | bytes 356360 | tf_op jit(solution)/shard_map/ppermute | solution.py:451
  6.1 7.2 %collective-permute-start.1 = (f32[232,128]{1,0:T(8,128)S(1)}, f32[232,128]{1,0:T(8,128)S(1)}, u32[]{:S(2)}, u32[]{:S(2)}) collective-permute-start(f32[232,128]{1,0:T(8,128)S(1)} %get-tuple-element.12), channel_id=1, source_target_pairs={{0,1},{1,0},{2,3},{3,2},{4,5},{5,4},{6,7},{7,6},{8,9},{9,8},{10,11... | collective-permute-start | bytes 356360 | tf_op jit(solution)/shard_map/ppermute | solution.py:407
  13.1 1.4 %collective-permute-start.2 = (f32[232,128]{1,0:T(8,128)S(1)}, f32[232,128]{1,0:T(8,128)S(1)}, u32[]{:S(2)}, u32[]{:S(2)}) collective-permute-start(f32[232,128]{1,0:T(8,128)S(1)} %edge_rows.3), channel_id=1, source_target_pairs={{0,1},{1,0},{2,3},{3,2},{4,5},{5,4},{6,7},{7,6},{8,9},{9,8},{10,11... | collective-permute-start | bytes 356360 | tf_op jit(solution)/shard_map/ppermute | solution.py:407
  19.6 1.3 %collective-permute-start.5 = (f32[72,128]{1,0:T(8,128)S(1)}, f32[72,128]{1,0:T(8,128)S(1)}, u32[]{:S(2)}, u32[]{:S(2)}) collective-permute-start(f32[72,128]{1,0:T(8,128)S(1)} %get-tuple-element.15), channel_id=1, source_target_pairs={{0,1},{1,0},{2,3},{3,2},{4,5},{5,4},{6,7},{7,6},{8,9},{9,8},{10,11... | collective-permute-start | bytes 110600 | tf_op jit(solution)/shard_map/ppermute | solution.py:407
  20.9 5.9 %collective-permute-start.8 = (f32[72,128]{1,0:T(8,128)S(1)}, f32[72,128]{1,0:T(8,128)S(1)}, u32[]{:S(2)}, u32[]{:S(2)}) collective-permute-start(f32[72,128]{1,0:T(8,128)S(1)} %add.12), channel_id=1, source_target_pairs={{0,12},{4,8},{8,4},{12,0},{1,13},{5,9},{9,5},{13,1},{2,14},{6,10},... | collective-permute-start | bytes 110600 | tf_op jit(solution)/shard_map/ppermute | solution.py:407
  24.8 5.0 %collective-permute-start.7 = (f32[72,128]{1,0:T(8,128)S(1)}, f32[72,128]{1,0:T(8,128)S(1)}, u32[]{:S(2)}, u32[]{:S(2)}) collective-permute-start(f32[72,128]{1,0:T(8,128)S(1)} %add.12), channel_id=1, source_target_pairs={{0,8},{4,12},{8,0},{12,4},{1,9},{5,13},{9,1},{13,5},{2,10},{6,14},... | collective-permute-start | bytes 110600 | tf_op jit(solution)/shard_map/ppermute | solution.py:407
  25.5 4.4 %collective-permute-start.6 = (f32[72,128]{1,0:T(8,128)S(1)}, f32[72,128]{1,0:T(8,128)S(1)}, u32[]{:S(2)}, u32[]{:S(2)}) collective-permute-start(f32[72,128]{1,0:T(8,128)S(1)} %add.12), channel_id=1, source_target_pairs={{0,4},{4,0},{8,12},{12,8},{1,5},{5,1},{9,13},{13,9},{2,6},{6,2},{1... | collective-permute-start | bytes 110600 | tf_op jit(solution)/shard_map/ppermute | solution.py:407
  29.8 1.5 %collective-permute-start.9 = (f32[64,128]{1,0:T(8,128)S(1)}, f32[64,128]{1,0:T(8,128)S(1)}, u32[]{:S(2)}, u32[]{:S(2)}) collective-permute-start(f32[64,128]{1,0:T(8,128)S(1)} %slice.9), channel_id=1, source_target_pairs={{0,1},{1,0},{2,3},{3,2},{4,5},{5,4},{6,7},{7,6},{8,9},{9,8},{10,11... | collective-permute-start | bytes 98312 | tf_op jit(solution)/shard_map/ppermute | solution.py:407

commit v9 on v8

--- a/solution.py
+++ b/solution.py
@@ -15,6 +15,7 @@
 HALO = DEGREE
 GRID_ROWS = ("strip", "sub")
 SIDE = 5
+CHUNK = 2
 
 VMEM = pl.BlockSpec(memory_space=pltpu.VMEM)
 SMEM = pl.BlockSpec(memory_space=pltpu.SMEM)
@@ -129,7 +130,7 @@
     bodies = refs[0:panels]
     nears = refs[panels : 2 * panels]
     fars = refs[2 * panels : 3 * panels]
-    locked_ref, keep_ref, send_ref, own_ref, y_even, y_odd, split = refs[3 * panels :]
+    locked_ref, keep_ref, send_ref, own_ref, y_even, y_odd, split, sums, squares = refs[3 * panels :]
     total = panels * width
     rows = height + 2 * HALO
     panel = panel_ref[0]
@@ -206,11 +207,15 @@
         u0, u1, u2, u3 = edges[row - 1]
         coefficients.append((diagonal, e1, u1, right(e0), right(e2), u3, e0, left(e3), u2))
 
+    dims = (((1,), (1,)), ((), ()))
     buffers = (y_even, y_odd)
-    for order in range(1, DEGREE + 1):
-        source_ref = buffers[(order - 1) % 2]
-        target_ref = buffers[order % 2]
-        for row in range(order, rows - order):
+    for wave in range(3, rows + DEGREE):
+        for order in range(1, DEGREE + 1):
+            row = wave - 2 * order
+            if not order <= row < rows - order:
+                continue
+            source_ref = buffers[(order - 1) % 2]
+            target_ref = buffers[order % 2]
             c = coefficients[row]
             ym = source_ref[row - 1]
             y0 = source_ref[row]
@@ -223,28 +228,37 @@
                 out = 0.5 * out
             else:
                 out = out - target_ref[row]
-            target_ref[row] = out
-    result = buffers[DEGREE % 2]
-
-    for row in range(height):
-        full = result[row + HALO]
-        own_ref[row] = full[:, 0:width]
-        high = full.astype(jnp.bfloat16)
-        rest = full - high.astype(jnp.float32)
+            if order < DEGREE:
+                target_ref[row] = out
+        line = wave - 2 * DEGREE - HALO
+        if not 0 <= line < height:
+            continue
+        own_ref[line] = out[:, 0:width]
+        high = out.astype(jnp.bfloat16)
+        rest = out - high.astype(jnp.float32)
         middle = rest.astype(jnp.bfloat16)
         low = (rest - middle.astype(jnp.float32)).astype(jnp.bfloat16)
         stacked = jnp.concatenate([high, middle, low], axis=0)
         for t in range(panels):
-            at = row * total + lax.rem(panel + t, panels) * width
+            at = line * total + lax.rem(panel + t, panels) * width
             split[:, pl.ds(pl.multiple_of(at, width), width)] = stacked[:, t * width : (t + 1) * width]
-
-    dims = (((1,), (1,)), ((), ()))
-    pieces = split[...]
-    gram = lax.dot_general(pieces, pieces, dims, preferred_element_type=jnp.float32)
+        if line % CHUNK == CHUNK - 1:
+            cut = slice((line + 1 - CHUNK) * total, (line + 1) * total)
+            pieces = split[:, cut]
+            part = lax.dot_general(
+                pieces, locked_ref[:, cut], dims, preferred_element_type=jnp.float32
+            )
+            square = lax.dot_general(pieces, pieces, dims, preferred_element_type=jnp.float32)
+            if line >= CHUNK:
+                part = part + sums[...]
+                square = square + squares[...]
+            sums[...] = part
+            squares[...] = square
+
+    gram = squares[...]
     gram = gram[0:count] + gram[count : 2 * count] + gram[2 * count : 3 * count]
     gram = gram[:, 0:count] + gram[:, count : 2 * count] + gram[:, 2 * count : 3 * count]
-    products = lax.dot_general(pieces, locked_ref[...], dims, preferred_element_type=jnp.float32)
-    products = products[0:count] + products[count : 2 * count] + products[2 * count : 3 * count]
+    products = sums[0:count] + sums[count : 2 * count] + sums[2 * count : 3 * count]
     half = products.shape[1] // 2
     lower = products[:, 0:half]
     upper = products[:, half:]
@@ -286,6 +300,8 @@
             pltpu.VMEM((rows, count, total), jnp.float32),
             pltpu.VMEM((rows, count, total), jnp.float32),
             pltpu.VMEM((3 * count, height * total), jnp.bfloat16),
+            pltpu.VMEM((3 * count, basis), jnp.float32),
+            pltpu.VMEM((3 * count, 3 * count), jnp.float32),
         ],
         compiler_params=pltpu.CompilerParams(vmem_limit_bytes=20 << 20),
         name="filter",

time: 32.7 us -> 32.4 us (level)
  no operation moved by 1% of the time
where the time goes in v9:
time: 32.4 us; the launch traced here: 32.2 us
  starting transfers between devices  13.6 us (42%)
  Pallas kernels  10.8 us (33%)
  waiting for transfers between devices  7.06 us (22%)
  between operations  0.74 us (2%)
    ppermute x7, starting transfers between devices, swap(): return lax.ppermute(array, axis, [(i, i ^ distance) for i in range(size)])  9.25 us
    ppermute x7, waiting for transfers between devices, swap(): return lax.ppermute(array, axis, [(i, i ^ distance) for i in range(size)])  6.57 us
    pallas_call x1, Pallas kernels, filter_call(): pl.pallas_call(lambda *refs: filter_kernel(*refs, panels=panels, height=h...  4.87 us
    ppermute x1, starting transfers between devices, on_device(): lax.ppermute(body, 'panel', [((i + shift) % panels, i) for i in range(pan...  3 us
    pallas_call x1, Pallas kernels, relayout(): pl.pallas_call(relayout_kernel, in_specs=[HBM], out_specs=VMEM, out_shape...  2.34 us
    pallas_call x1, Pallas kernels, factorize(): pl.pallas_call(lambda *refs: factor_kernel(*refs, vertices=float(vertices...  1.41 us
    ppermute x2, starting transfers between devices, on_device(): lax.ppermute(far, ('strip', 'panel', 'sub'), far_moves(shift))  1.34 us
    pallas_call x1, Pallas kernels, finish(): pl.pallas_call(lambda *refs: finish_kernel(*refs, vertices=float(vertices...  1.1 us
  transfers between devices with their start and end apart: 10, of which 6 were waited for; matrix products, arithmetic and copies ran while one was open for 0% of the time, Pallas kernels for 12%

profile of v9, /device:TPU:0, one launch (start us, length us, event | category | flops | bytes accessed | tf_op | source)
XLA Modules:
  0.0 32.2 jit_solution(7569062848797431853)
XLA Ops:
  0.6 1.0 %pack.1.refs_1_.refs_2_ = f32[592,128]{1,0:T(8,128)S(1)} custom-call(s32[1]{0:T(128)} %bitcast.1.panel_ref.refs_0_, s32[1]{0:T(128)} %bitcast.sub_ref.refs_0_.refs_1_, f32[32,16,128]{2,1,0:T(8,128)} %block_hbm.1, f32[8,16,128]{2,1,0:T(8,128)} %weights_hbm.1, f32[16,128]{1,0:T(8,128)} %mass_hbm.1), custom_call_target="tpu_custom_call" | custom-call | tf_op jit(solution)/shard_map/pack/pallas_call | solution.py:48
  1.7 3.0 %collective-permute-start = (f32[592,128]{1,0:T(8,128)S(1)}, f32[592,128]{1,0:T(8,128)S(1)}, u32[]{:S(2)}, u32[]{:S(2)}) collective-permute-start(f32[592,128]{1,0:T(8,128)S(1)} %pack.1.refs_1_.refs_2_), channel_id=1, source_target_pairs={{2,0},{0,2},{3,1},{1,3},{6,4},{4,6},{7,5},{5,7},{10,8},{8,10},{11,... | collective-permute-start | bytes 909320 | tf_op jit(solution)/shard_map/ppermute | solution.py:452
  4.7 0.7 %collective-permute-start.4 = (f32[232,128]{1,0:T(8,128)S(1)}, f32[232,128]{1,0:T(8,128)S(1)}, u32[]{:S(2)}, u32[]{:S(2)}) collective-permute-start(f32[232,128]{1,0:T(8,128)S(1)} %get-tuple-element.13), channel_id=1, source_target_pairs={{1,6},{3,4},{4,3},{6,1},{5,10},{7,8},{8,7},{10,5},{9,14},{11,12},{... | collective-permute-start | bytes 356360 | tf_op jit(solution)/shard_map/ppermute | solution.py:467
  5.4 0.7 %collective-permute-start.3 = (f32[232,128]{1,0:T(8,128)S(1)}, f32[232,128]{1,0:T(8,128)S(1)}, u32[]{:S(2)}, u32[]{:S(2)}) collective-permute-start(f32[232,128]{1,0:T(8,128)S(1)} %get-tuple-element.13), channel_id=1, source_target_pairs={{1,4},{3,6},{4,1},{6,3},{5,8},{7,10},{8,5},{10,7},{9,12},{11,14},{... | collective-permute-start | bytes 356360 | tf_op jit(solution)/shard_map/ppermute | solution.py:467
  6.1 4.2 %collective-permute-start.1 = (f32[232,128]{1,0:T(8,128)S(1)}, f32[232,128]{1,0:T(8,128)S(1)}, u32[]{:S(2)}, u32[]{:S(2)}) collective-permute-start(f32[232,128]{1,0:T(8,128)S(1)} %get-tuple-element.12), channel_id=1, source_target_pairs={{0,1},{1,0},{2,3},{3,2},{4,5},{5,4},{6,7},{7,6},{8,9},{9,8},{10,11... | collective-permute-start | bytes 356360 | tf_op jit(solution)/shard_map/ppermute | solution.py:423
  10.3 2.3 %relayout.1.refs_2_.refs_8_ = bf16[512,4096]{1,0:T(8,128)(2,1)S(1)} custom-call(bf16[512,16,256]{2,1,0:T(8,128)(2,1)} %locked_hbm.1), custom_call_target="tpu_custom_call" | custom-call | tf_op jit(solution)/shard_map/relayout/pallas_call | solution.py:90
  12.7 0.5 %collective-permute-done.refs_1_.refs_3_ = f32[592,128]{1,0:T(8,128)S(1)} collective-permute-done((f32[592,128]{1,0:T(8,128)S(1)}, f32[592,128]{1,0:T(8,128)S(1)}, u32[]{:S(2)}, u32[]{:S(2)}) %collective-permute-start) | collective-permute-done | bytes 303136 | tf_op jit(solution)/shard_map/ppermute | solution.py:452
  13.1 0.1 collective-permute-start.2
  13.2 0.0 collective-permute-done.1.refs_4_
  13.2 0.0 collective-permute-done.4.refs_7_
  13.2 0.0 collective-permute-done.3.refs_6_
  13.3 1.3 %collective-permute-done.2.refs_5_ = f32[232,128]{1,0:T(8,128)S(1)} collective-permute-done((f32[232,128]{1,0:T(8,128)S(1)}, f32[232,128]{1,0:T(8,128)S(1)}, u32[]{:S(2)}, u32[]{:S(2)}) %collective-permute-start.2) | collective-permute-done | bytes 118816 | tf_op jit(solution)/shard_map/ppermute | solution.py:423
  14.5 4.9 %filter.1 = (f32[72,128]{1,0:T(8,128)S(1)}, f32[72,128]{1,0:T(8,128)S(1)}, f32[16,32,128]{2,1,0:T(8,128)S(1)}) custom-call(s32[1]{0:T(128)} %bitcast.1.panel_ref.refs_0_, s32[1]{0:T(128)} %bitcast.sub_ref.refs_0_.refs_1_, f32[592,128]{1,0:T(8,128)S(1)} %pack.1.refs_1_.refs_2_, f32[592,128]{1,0:T(8,128)S(1)} %collective-permute-done.refs_1_.refs_3_, ...), custom_call_target="tpu_custom_call" | custom-call | tf_op jit(solution)/shard_map/filter/pallas_call | solution.py:294
  19.4 0.2 collective-permute-start.5
  19.6 1.1 %collective-permute-done.5 = f32[72,128]{1,0:T(8,128)S(1)} collective-permute-done((f32[72,128]{1,0:T(8,128)S(1)}, f32[72,128]{1,0:T(8,128)S(1)}, u32[]{:S(2)}, u32[]{:S(2)}) %collective-permute-start.5) | collective-permute-done | bytes 36896 | tf_op jit(solution)/shard_map/ppermute | solution.py:423
  20.7 3.9 %collective-permute-start.8 = (f32[72,128]{1,0:T(8,128)S(1)}, f32[72,128]{1,0:T(8,128)S(1)}, u32[]{:S(2)}, u32[]{:S(2)}) collective-permute-start(f32[72,128]{1,0:T(8,128)S(1)} %add.12), channel_id=1, source_target_pairs={{0,12},{4,8},{8,4},{12,0},{1,13},{5,9},{9,5},{13,1},{2,14},{6,10},... | collective-permute-start | bytes 110600 | tf_op jit(solution)/shard_map/ppermute | solution.py:423
  24.5 0.7 %collective-permute-start.7 = (f32[72,128]{1,0:T(8,128)S(1)}, f32[72,128]{1,0:T(8,128)S(1)}, u32[]{:S(2)}, u32[]{:S(2)}) collective-permute-start(f32[72,128]{1,0:T(8,128)S(1)} %add.12), channel_id=1, source_target_pairs={{0,8},{4,12},{8,0},{12,4},{1,9},{5,13},{9,1},{13,5},{2,10},{6,14},... | collective-permute-start | bytes 110600 | tf_op jit(solution)/shard_map/ppermute | solution.py:423
  25.2 0.1 collective-permute-start.6
  25.3 1.2 %collective-permute-done.8 = f32[72,128]{1,0:T(8,128)S(1)} collective-permute-done((f32[72,128]{1,0:T(8,128)S(1)}, f32[72,128]{1,0:T(8,128)S(1)}, u32[]{:S(2)}, u32[]{:S(2)}) %collective-permute-start.8) | collective-permute-done | bytes 36896 | tf_op jit(solution)/shard_map/ppermute | solution.py:423
  26.6 2.9 %collective-permute-done.7 = f32[72,128]{1,0:T(8,128)S(1)} collective-permute-done((f32[72,128]{1,0:T(8,128)S(1)}, f32[72,128]{1,0:T(8,128)S(1)}, u32[]{:S(2)}, u32[]{:S(2)}) %collective-permute-start.7) | collective-permute-done | bytes 36896 | tf_op jit(solution)/shard_map/ppermute | solution.py:423
  29.5 0.1 collective-permute-done.6
  29.6 0.1 collective-permute-start.9
  29.7 1.4 %factor.1 = (f32[32,32]{1,0:T(8,128)}, f32[32,32]{1,0:T(8,128)S(1)}) custom-call(f32[8,128]{1,0:T(8,128)S(1)} %slice.8.refs_0_), custom_call_target="tpu_custom_call" | custom-call | tf_op jit(solution)/shard_map/factor/pallas_call | solution.py:357
  31.1 0.0 collective-permute-done.9.refs_4_
  31.1 1.1 %finish.1 = (f32[32,16,128]{2,1,0:T(8,128)}, f32[32,512]{1,0:T(8,128)}) custom-call(s32[1]{0:T(128)} %bitcast.sub_ref.refs_0_.refs_1_, f32[32,32]{1,0:T(8,128)S(1)} %get-tuple-element.16.refs_1_, f32[16,32,128]{2,1,0:T(8,128)S(1)} %get-tuple-element.17.refs_2_, f32[72,128]{1,0:T(8,128)S(1)} %add_add_fusion.refs_3_, f32[64,128]{1,0:T(8,128)S(1)} %collective-permute-done.9.refs_4_), custom_call_target="tpu_custom_call" | custom-call | tf_op jit(solution)/shard_map/finish/pallas_call | solution.py:406
  (6 shorter events, 0.1 us)
Async XLA Ops:
  1.7 11.5 %collective-permute-start = (f32[592,128]{1,0:T(8,128)S(1)}, f32[592,128]{1,0:T(8,128)S(1)}, u32[]{:S(2)}, u32[]{:S(2)}) collective-permute-start(f32[592,128]{1,0:T(8,128)S(1)} %pack.1.refs_1_.refs_2_), channel_id=1, source_target_pairs={{2,0},{0,2},{3,1},{1,3},{6,4},{4,6},{7,5},{5,7},{10,8},{8,10},{11,... | collective-permute-start | bytes 909320 | tf_op jit(solution)/shard_map/ppermute | solution.py:452
  4.7 8.5 %collective-permute-start.4 = (f32[232,128]{1,0:T(8,128)S(1)}, f32[232,128]{1,0:T(8,128)S(1)}, u32[]{:S(2)}, u32[]{:S(2)}) collective-permute-start(f32[232,128]{1,0:T(8,128)S(1)} %get-tuple-element.13), channel_id=1, source_target_pairs={{1,6},{3,4},{4,3},{6,1},{5,10},{7,8},{8,7},{10,5},{9,14},{11,12},{... | collective-permute-start | bytes 356360 | tf_op jit(solution)/shard_map/ppermute | solution.py:467
  5.4 7.9 %collective-permute-start.3 = (f32[232,128]{1,0:T(8,128)S(1)}, f32[232,128]{1,0:T(8,128)S(1)}, u32[]{:S(2)}, u32[]{:S(2)}) collective-permute-start(f32[232,128]{1,0:T(8,128)S(1)} %get-tuple-element.13), channel_id=1, source_target_pairs={{1,4},{3,6},{4,1},{6,3},{5,8},{7,10},{8,5},{10,7},{9,12},{11,14},{... | collective-permute-start | bytes 356360 | tf_op jit(solution)/shard_map/ppermute | solution.py:467
  6.1 7.2 %collective-permute-start.1 = (f32[232,128]{1,0:T(8,128)S(1)}, f32[232,128]{1,0:T(8,128)S(1)}, u32[]{:S(2)}, u32[]{:S(2)}) collective-permute-start(f32[232,128]{1,0:T(8,128)S(1)} %get-tuple-element.12), channel_id=1, source_target_pairs={{0,1},{1,0},{2,3},{3,2},{4,5},{5,4},{6,7},{7,6},{8,9},{9,8},{10,11... | collective-permute-start | bytes 356360 | tf_op jit(solution)/shard_map/ppermute | solution.py:423
  13.1 1.4 %collective-permute-start.2 = (f32[232,128]{1,0:T(8,128)S(1)}, f32[232,128]{1,0:T(8,128)S(1)}, u32[]{:S(2)}, u32[]{:S(2)}) collective-permute-start(f32[232,128]{1,0:T(8,128)S(1)} %edge_rows.3), channel_id=1, source_target_pairs={{0,1},{1,0},{2,3},{3,2},{4,5},{5,4},{6,7},{7,6},{8,9},{9,8},{10,11... | collective-permute-start | bytes 356360 | tf_op jit(solution)/shard_map/ppermute | solution.py:423
  19.4 1.2 %collective-permute-start.5 = (f32[72,128]{1,0:T(8,128)S(1)}, f32[72,128]{1,0:T(8,128)S(1)}, u32[]{:S(2)}, u32[]{:S(2)}) collective-permute-start(f32[72,128]{1,0:T(8,128)S(1)} %get-tuple-element.15), channel_id=1, source_target_pairs={{0,1},{1,0},{2,3},{3,2},{4,5},{5,4},{6,7},{7,6},{8,9},{9,8},{10,11... | collective-permute-start | bytes 110600 | tf_op jit(solution)/shard_map/ppermute | solution.py:423
  20.7 5.9 %collective-permute-start.8 = (f32[72,128]{1,0:T(8,128)S(1)}, f32[72,128]{1,0:T(8,128)S(1)}, u32[]{:S(2)}, u32[]{:S(2)}) collective-permute-start(f32[72,128]{1,0:T(8,128)S(1)} %add.12), channel_id=1, source_target_pairs={{0,12},{4,8},{8,4},{12,0},{1,13},{5,9},{9,5},{13,1},{2,14},{6,10},... | collective-permute-start | bytes 110600 | tf_op jit(solution)/shard_map/ppermute | solution.py:423
  24.5 5.0 %collective-permute-start.7 = (f32[72,128]{1,0:T(8,128)S(1)}, f32[72,128]{1,0:T(8,128)S(1)}, u32[]{:S(2)}, u32[]{:S(2)}) collective-permute-start(f32[72,128]{1,0:T(8,128)S(1)} %add.12), channel_id=1, source_target_pairs={{0,8},{4,12},{8,0},{12,4},{1,9},{5,13},{9,1},{13,5},{2,10},{6,14},... | collective-permute-start | bytes 110600 | tf_op jit(solution)/shard_map/ppermute | solution.py:423
  25.2 4.4 %collective-permute-start.6 = (f32[72,128]{1,0:T(8,128)S(1)}, f32[72,128]{1,0:T(8,128)S(1)}, u32[]{:S(2)}, u32[]{:S(2)}) collective-permute-start(f32[72,128]{1,0:T(8,128)S(1)} %add.12), channel_id=1, source_target_pairs={{0,4},{4,0},{8,12},{12,8},{1,5},{5,1},{9,13},{13,9},{2,6},{6,2},{1... | collective-permute-start | bytes 110600 | tf_op jit(solution)/shard_map/ppermute | solution.py:423
  29.6 1.5 %collective-permute-start.9 = (f32[64,128]{1,0:T(8,128)S(1)}, f32[64,128]{1,0:T(8,128)S(1)}, u32[]{:S(2)}, u32[]{:S(2)}) collective-permute-start(f32[64,128]{1,0:T(8,128)S(1)} %slice.9), channel_id=1, source_target_pairs={{0,1},{1,0},{2,3},{3,2},{4,5},{5,4},{6,7},{7,6},{8,9},{9,8},{10,11... | collective-permute-start | bytes 98312 | tf_op jit(solution)/shard_map/ppermute | solution.py:423

commit v10 on v9

--- a/solution.py
+++ b/solution.py
@@ -26,17 +26,26 @@
     panel_ref, sub_ref, block_hbm, weights_hbm, mass_hbm, body_ref,
     block_ref, weights_ref, mass_ref, sems,
 ):
-    copies = [
-        pltpu.make_async_copy(block_hbm, block_ref, sems.at[0]),
-        pltpu.make_async_copy(weights_hbm.at[0:4], weights_ref, sems.at[1]),
-        pltpu.make_async_copy(mass_hbm, mass_ref, sems.at[2]),
+    count, height, width = block_ref.shape
+    lines = range(0, height, 8)
+    block_copies = [
+        pltpu.make_async_copy(
+            block_hbm.at[:, at : at + 8], block_ref.at[:, at : at + 8], sems.at[2 + at // 8]
+        )
+        for at in lines
     ]
-    for copy in copies:
+    side_copies = [
+        pltpu.make_async_copy(weights_hbm.at[0:4], weights_ref, sems.at[0]),
+        pltpu.make_async_copy(mass_hbm, mass_ref, sems.at[1]),
+    ]
+    for copy in block_copies + side_copies:
         copy.start()
-    for copy in copies:
+    for at, copy in zip(lines, block_copies):
         copy.wait()
-    count, height, width = block_ref.shape
-    body_ref[0 : height * count] = pltpu.einshape("brc->rbc", block_ref[...]).reshape(-1, width)
+        rows = pltpu.einshape("brc->rbc", block_ref[:, at : at + 8])
+        body_ref[at * count : (at + 8) * count] = rows.reshape(-1, width)
+    for copy in side_copies:
+        copy.wait()
     for d in range(SIDE - 1):
         at = height * (count + d)
         body_ref[at : at + height] = weights_ref[d]
@@ -54,7 +63,7 @@
             pltpu.VMEM((count, height, width), jnp.float32),
             pltpu.VMEM((4, height, width), jnp.float32),
             pltpu.VMEM((height, width), jnp.float32),
-            pltpu.SemaphoreType.DMA((3,)),
+            pltpu.SemaphoreType.DMA((2 + height // 8,)),
         ],
         compiler_params=pltpu.CompilerParams(vmem_limit_bytes=8 << 20),
         name="pack",
@@ -332,19 +341,30 @@
             for k in range(8)
         }
         pivots = jnp.ones((8, 128), jnp.float32)
-        for j in range(8):
-            pivot = fill(columns[b, j][j : j + 1])
-            pivots = jnp.where(row == j, pivot, pivots)
+        for j in range(0, 8, 2):
+            first, second = columns[b, j], columns[b, j + 1]
+            pivot = fill(first[j : j + 1])
+            off = fill(first[j + 1 : j + 2])
+            det = pivot * fill(second[j + 1 : j + 2]) - off * off
             inverse = 1.0 / pivot
-            pivot_row = fill(work[b][j : j + 1])
-            entries = {k: fill(columns[b, k][j : j + 1]) for k in range(j + 1, 8)}
+            inverse_det = 1.0 / det
+            pivots = jnp.where(row == j, pivot, jnp.where(row == j + 1, det * inverse, pivots))
+            ratio = off * inverse
+            top = fill(work[b][j : j + 1])
+            low = fill(work[b][j + 1 : j + 2]) - ratio * top
+            tops = {k: fill(columns[b, k][j : j + 1]) for k in range(j + 2, 8)}
+            lows = {
+                k: fill(columns[b, k][j + 1 : j + 2]) - ratio * tops[k] for k in range(j + 2, 8)
+            }
             for t in range(b, tiles):
-                multiplier = columns[t, j] * inverse
+                one = columns[t, j] * inverse
+                two = (columns[t, j + 1] * pivot - columns[t, j] * off) * inverse_det
                 if t == b:
-                    multiplier = jnp.where(row > j, multiplier, 0.0)
-                for k in range(j + 1, 8):
-                    columns[t, k] = columns[t, k] - multiplier * entries[k]
-                work[t] = work[t] - multiplier * pivot_row
+                    one = jnp.where(row > j, one, 0.0)
+                    two = jnp.where(row > j + 1, two, 0.0)
+                for k in range(j + 2, 8):
+                    columns[t, k] = columns[t, k] - (one * tops[k] + two * lows[k])
+                work[t] = work[t] - (one * top + two * low)
         work[b] = work[b] * (1.0 / jnp.sqrt(pivots))
     for t in range(tiles):
         upper = jnp.where(row + 8 * t <= col, work[t], 0.0)

time: 32.4 us -> 32.4 us (level)
  no operation moved by 1% of the time
where the time goes in v10:
time: 32.4 us; the launch traced here: 32.2 us
  starting transfers between devices  13.6 us (42%)
  Pallas kernels  10.7 us (33%)
  waiting for transfers between devices  7.08 us (22%)
  between operations  0.74 us (2%)
    ppermute x7, starting transfers between devices, swap(): return lax.ppermute(array, axis, [(i, i ^ distance) for i in range(size)])  9.24 us
    ppermute x7, waiting for transfers between devices, swap(): return lax.ppermute(array, axis, [(i, i ^ distance) for i in range(size)])  6.59 us
    pallas_call x1, Pallas kernels, filter_call(): pl.pallas_call(lambda *refs: filter_kernel(*refs, panels=panels, height=h...  4.87 us
    ppermute x1, starting transfers between devices, on_device(): lax.ppermute(body, 'panel', [((i + shift) % panels, i) for i in range(pan...  3 us
    pallas_call x1, Pallas kernels, relayout(): pl.pallas_call(relayout_kernel, in_specs=[HBM], out_specs=VMEM, out_shape...  2.34 us
    pallas_call x1, Pallas kernels, factorize(): pl.pallas_call(lambda *refs: factor_kernel(*refs, vertices=float(vertices...  1.36 us
    ppermute x2, starting transfers between devices, on_device(): lax.ppermute(far, ('strip', 'panel', 'sub'), far_moves(shift))  1.34 us
    pallas_call x1, Pallas kernels, finish(): pl.pallas_call(lambda *refs: finish_kernel(*refs, vertices=float(vertices...  1.09 us
  transfers between devices with their start and end apart: 10, of which 6 were waited for; matrix products, arithmetic and copies ran while one was open for 0% of the time, Pallas kernels for 12%

profile of v10, /device:TPU:0, one launch (start us, length us, event | category | flops | bytes accessed | tf_op | source)
XLA Modules:
  0.0 32.2 jit_solution(12887496173694776235)
XLA Ops:
  0.6 1.0 %pack.1.refs_1_.refs_2_ = f32[592,128]{1,0:T(8,128)S(1)} custom-call(s32[1]{0:T(128)} %bitcast.1.panel_ref.refs_0_, s32[1]{0:T(128)} %bitcast.sub_ref.refs_0_.refs_1_, f32[32,16,128]{2,1,0:T(8,128)} %block_hbm.1, f32[8,16,128]{2,1,0:T(8,128)} %weights_hbm.1, f32[16,128]{1,0:T(8,128)} %mass_hbm.1), custom_call_target="tpu_custom_call" | custom-call | tf_op jit(solution)/shard_map/pack/pallas_call | solution.py:57
  1.7 3.0 %collective-permute-start = (f32[592,128]{1,0:T(8,128)S(1)}, f32[592,128]{1,0:T(8,128)S(1)}, u32[]{:S(2)}, u32[]{:S(2)}) collective-permute-start(f32[592,128]{1,0:T(8,128)S(1)} %pack.1.refs_1_.refs_2_), channel_id=1, source_target_pairs={{2,0},{0,2},{3,1},{1,3},{6,4},{4,6},{7,5},{5,7},{10,8},{8,10},{11,... | collective-permute-start | bytes 909320 | tf_op jit(solution)/shard_map/ppermute | solution.py:472
  4.7 0.7 %collective-permute-start.4 = (f32[232,128]{1,0:T(8,128)S(1)}, f32[232,128]{1,0:T(8,128)S(1)}, u32[]{:S(2)}, u32[]{:S(2)}) collective-permute-start(f32[232,128]{1,0:T(8,128)S(1)} %get-tuple-element.13), channel_id=1, source_target_pairs={{1,6},{3,4},{4,3},{6,1},{5,10},{7,8},{8,7},{10,5},{9,14},{11,12},{... | collective-permute-start | bytes 356360 | tf_op jit(solution)/shard_map/ppermute | solution.py:487
  5.4 0.7 %collective-permute-start.3 = (f32[232,128]{1,0:T(8,128)S(1)}, f32[232,128]{1,0:T(8,128)S(1)}, u32[]{:S(2)}, u32[]{:S(2)}) collective-permute-start(f32[232,128]{1,0:T(8,128)S(1)} %get-tuple-element.13), channel_id=1, source_target_pairs={{1,4},{3,6},{4,1},{6,3},{5,8},{7,10},{8,5},{10,7},{9,12},{11,14},{... | collective-permute-start | bytes 356360 | tf_op jit(solution)/shard_map/ppermute | solution.py:487
  6.1 4.2 %collective-permute-start.1 = (f32[232,128]{1,0:T(8,128)S(1)}, f32[232,128]{1,0:T(8,128)S(1)}, u32[]{:S(2)}, u32[]{:S(2)}) collective-permute-start(f32[232,128]{1,0:T(8,128)S(1)} %get-tuple-element.12), channel_id=1, source_target_pairs={{0,1},{1,0},{2,3},{3,2},{4,5},{5,4},{6,7},{7,6},{8,9},{9,8},{10,11... | collective-permute-start | bytes 356360 | tf_op jit(solution)/shard_map/ppermute | solution.py:443
  10.3 2.3 %relayout.1.refs_2_.refs_8_ = bf16[512,4096]{1,0:T(8,128)(2,1)S(1)} custom-call(bf16[512,16,256]{2,1,0:T(8,128)(2,1)} %locked_hbm.1), custom_call_target="tpu_custom_call" | custom-call | tf_op jit(solution)/shard_map/relayout/pallas_call | solution.py:99
  12.7 0.5 %collective-permute-done.refs_1_.refs_3_ = f32[592,128]{1,0:T(8,128)S(1)} collective-permute-done((f32[592,128]{1,0:T(8,128)S(1)}, f32[592,128]{1,0:T(8,128)S(1)}, u32[]{:S(2)}, u32[]{:S(2)}) %collective-permute-start) | collective-permute-done | bytes 303136 | tf_op jit(solution)/shard_map/ppermute | solution.py:472
  13.2 0.1 collective-permute-start.2
  13.2 0.0 collective-permute-done.1.refs_4_
  13.2 0.0 collective-permute-done.4.refs_7_
  13.3 0.0 collective-permute-done.3.refs_6_
  13.3 1.3 %collective-permute-done.2.refs_5_ = f32[232,128]{1,0:T(8,128)S(1)} collective-permute-done((f32[232,128]{1,0:T(8,128)S(1)}, f32[232,128]{1,0:T(8,128)S(1)}, u32[]{:S(2)}, u32[]{:S(2)}) %collective-permute-start.2) | collective-permute-done | bytes 118816 | tf_op jit(solution)/shard_map/ppermute | solution.py:443
  14.5 4.9 %filter.1 = (f32[72,128]{1,0:T(8,128)S(1)}, f32[72,128]{1,0:T(8,128)S(1)}, f32[16,32,128]{2,1,0:T(8,128)S(1)}) custom-call(s32[1]{0:T(128)} %bitcast.1.panel_ref.refs_0_, s32[1]{0:T(128)} %bitcast.sub_ref.refs_0_.refs_1_, f32[592,128]{1,0:T(8,128)S(1)} %pack.1.refs_1_.refs_2_, f32[592,128]{1,0:T(8,128)S(1)} %collective-permute-done.refs_1_.refs_3_, ...), custom_call_target="tpu_custom_call" | custom-call | tf_op jit(solution)/shard_map/filter/pallas_call | solution.py:303
  19.4 0.2 collective-permute-start.5
  19.6 1.1 %collective-permute-done.5 = f32[72,128]{1,0:T(8,128)S(1)} collective-permute-done((f32[72,128]{1,0:T(8,128)S(1)}, f32[72,128]{1,0:T(8,128)S(1)}, u32[]{:S(2)}, u32[]{:S(2)}) %collective-permute-start.5) | collective-permute-done | bytes 36896 | tf_op jit(solution)/shard_map/ppermute | solution.py:443
  20.7 3.8 %collective-permute-start.8 = (f32[72,128]{1,0:T(8,128)S(1)}, f32[72,128]{1,0:T(8,128)S(1)}, u32[]{:S(2)}, u32[]{:S(2)}) collective-permute-start(f32[72,128]{1,0:T(8,128)S(1)} %add.12), channel_id=1, source_target_pairs={{0,12},{4,8},{8,4},{12,0},{1,13},{5,9},{9,5},{13,1},{2,14},{6,10},... | collective-permute-start | bytes 110600 | tf_op jit(solution)/shard_map/ppermute | solution.py:443
  24.5 0.7 %collective-permute-start.7 = (f32[72,128]{1,0:T(8,128)S(1)}, f32[72,128]{1,0:T(8,128)S(1)}, u32[]{:S(2)}, u32[]{:S(2)}) collective-permute-start(f32[72,128]{1,0:T(8,128)S(1)} %add.12), channel_id=1, source_target_pairs={{0,8},{4,12},{8,0},{12,4},{1,9},{5,13},{9,1},{13,5},{2,10},{6,14},... | collective-permute-start | bytes 110600 | tf_op jit(solution)/shard_map/ppermute | solution.py:443
  25.2 0.1 collective-permute-start.6
  25.3 1.2 %collective-permute-done.8 = f32[72,128]{1,0:T(8,128)S(1)} collective-permute-done((f32[72,128]{1,0:T(8,128)S(1)}, f32[72,128]{1,0:T(8,128)S(1)}, u32[]{:S(2)}, u32[]{:S(2)}) %collective-permute-start.8) | collective-permute-done | bytes 36896 | tf_op jit(solution)/shard_map/ppermute | solution.py:443
  26.6 2.9 %collective-permute-done.7 = f32[72,128]{1,0:T(8,128)S(1)} collective-permute-done((f32[72,128]{1,0:T(8,128)S(1)}, f32[72,128]{1,0:T(8,128)S(1)}, u32[]{:S(2)}, u32[]{:S(2)}) %collective-permute-start.7) | collective-permute-done | bytes 36896 | tf_op jit(solution)/shard_map/ppermute | solution.py:443
  29.5 0.1 collective-permute-done.6
  29.6 0.1 collective-permute-start.9
  29.7 1.4 %factor.1 = (f32[32,32]{1,0:T(8,128)}, f32[32,32]{1,0:T(8,128)S(1)}) custom-call(f32[8,128]{1,0:T(8,128)S(1)} %slice.8.refs_0_), custom_call_target="tpu_custom_call" | custom-call | tf_op jit(solution)/shard_map/factor/pallas_call | solution.py:377
  31.1 0.0 collective-permute-done.9.refs_4_
  31.1 1.1 %finish.1 = (f32[32,16,128]{2,1,0:T(8,128)}, f32[32,512]{1,0:T(8,128)}) custom-call(s32[1]{0:T(128)} %bitcast.sub_ref.refs_0_.refs_1_, f32[32,32]{1,0:T(8,128)S(1)} %get-tuple-element.16.refs_1_, f32[16,32,128]{2,1,0:T(8,128)S(1)} %get-tuple-element.17.refs_2_, f32[72,128]{1,0:T(8,128)S(1)} %add_add_fusion.refs_3_, f32[64,128]{1,0:T(8,128)S(1)} %collective-permute-done.9.refs_4_), custom_call_target="tpu_custom_call" | custom-call | tf_op jit(solution)/shard_map/finish/pallas_call | solution.py:426
  (6 shorter events, 0.1 us)
Async XLA Ops:
  1.7 11.5 %collective-permute-start = (f32[592,128]{1,0:T(8,128)S(1)}, f32[592,128]{1,0:T(8,128)S(1)}, u32[]{:S(2)}, u32[]{:S(2)}) collective-permute-start(f32[592,128]{1,0:T(8,128)S(1)} %pack.1.refs_1_.refs_2_), channel_id=1, source_target_pairs={{2,0},{0,2},{3,1},{1,3},{6,4},{4,6},{7,5},{5,7},{10,8},{8,10},{11,... | collective-permute-start | bytes 909320 | tf_op jit(solution)/shard_map/ppermute | solution.py:472
  4.7 8.5 %collective-permute-start.4 = (f32[232,128]{1,0:T(8,128)S(1)}, f32[232,128]{1,0:T(8,128)S(1)}, u32[]{:S(2)}, u32[]{:S(2)}) collective-permute-start(f32[232,128]{1,0:T(8,128)S(1)} %get-tuple-element.13), channel_id=1, source_target_pairs={{1,6},{3,4},{4,3},{6,1},{5,10},{7,8},{8,7},{10,5},{9,14},{11,12},{... | collective-permute-start | bytes 356360 | tf_op jit(solution)/shard_map/ppermute | solution.py:487
  5.4 7.9 %collective-permute-start.3 = (f32[232,128]{1,0:T(8,128)S(1)}, f32[232,128]{1,0:T(8,128)S(1)}, u32[]{:S(2)}, u32[]{:S(2)}) collective-permute-start(f32[232,128]{1,0:T(8,128)S(1)} %get-tuple-element.13), channel_id=1, source_target_pairs={{1,4},{3,6},{4,1},{6,3},{5,8},{7,10},{8,5},{10,7},{9,12},{11,14},{... | collective-permute-start | bytes 356360 | tf_op jit(solution)/shard_map/ppermute | solution.py:487
  6.1 7.2 %collective-permute-start.1 = (f32[232,128]{1,0:T(8,128)S(1)}, f32[232,128]{1,0:T(8,128)S(1)}, u32[]{:S(2)}, u32[]{:S(2)}) collective-permute-start(f32[232,128]{1,0:T(8,128)S(1)} %get-tuple-element.12), channel_id=1, source_target_pairs={{0,1},{1,0},{2,3},{3,2},{4,5},{5,4},{6,7},{7,6},{8,9},{9,8},{10,11... | collective-permute-start | bytes 356360 | tf_op jit(solution)/shard_map/ppermute | solution.py:443
  13.2 1.4 %collective-permute-start.2 = (f32[232,128]{1,0:T(8,128)S(1)}, f32[232,128]{1,0:T(8,128)S(1)}, u32[]{:S(2)}, u32[]{:S(2)}) collective-permute-start(f32[232,128]{1,0:T(8,128)S(1)} %edge_rows.3), channel_id=1, source_target_pairs={{0,1},{1,0},{2,3},{3,2},{4,5},{5,4},{6,7},{7,6},{8,9},{9,8},{10,11... | collective-permute-start | bytes 356360 | tf_op jit(solution)/shard_map/ppermute | solution.py:443
  19.4 1.2 %collective-permute-start.5 = (f32[72,128]{1,0:T(8,128)S(1)}, f32[72,128]{1,0:T(8,128)S(1)}, u32[]{:S(2)}, u32[]{:S(2)}) collective-permute-start(f32[72,128]{1,0:T(8,128)S(1)} %get-tuple-element.15), channel_id=1, source_target_pairs={{0,1},{1,0},{2,3},{3,2},{4,5},{5,4},{6,7},{7,6},{8,9},{9,8},{10,11... | collective-permute-start | bytes 110600 | tf_op jit(solution)/shard_map/ppermute | solution.py:443
  20.7 5.9 %collective-permute-start.8 = (f32[72,128]{1,0:T(8,128)S(1)}, f32[72,128]{1,0:T(8,128)S(1)}, u32[]{:S(2)}, u32[]{:S(2)}) collective-permute-start(f32[72,128]{1,0:T(8,128)S(1)} %add.12), channel_id=1, source_target_pairs={{0,12},{4,8},{8,4},{12,0},{1,13},{5,9},{9,5},{13,1},{2,14},{6,10},... | collective-permute-start | bytes 110600 | tf_op jit(solution)/shard_map/ppermute | solution.py:443
  24.5 5.0 %collective-permute-start.7 = (f32[72,128]{1,0:T(8,128)S(1)}, f32[72,128]{1,0:T(8,128)S(1)}, u32[]{:S(2)}, u32[]{:S(2)}) collective-permute-start(f32[72,128]{1,0:T(8,128)S(1)} %add.12), channel_id=1, source_target_pairs={{0,8},{4,12},{8,0},{12,4},{1,9},{5,13},{9,1},{13,5},{2,10},{6,14},... | collective-permute-start | bytes 110600 | tf_op jit(solution)/shard_map/ppermute | solution.py:443
  25.2 4.4 %collective-permute-start.6 = (f32[72,128]{1,0:T(8,128)S(1)}, f32[72,128]{1,0:T(8,128)S(1)}, u32[]{:S(2)}, u32[]{:S(2)}) collective-permute-start(f32[72,128]{1,0:T(8,128)S(1)} %add.12), channel_id=1, source_target_pairs={{0,4},{4,0},{8,12},{12,8},{1,5},{5,1},{9,13},{13,9},{2,6},{6,2},{1... | collective-permute-start | bytes 110600 | tf_op jit(solution)/shard_map/ppermute | solution.py:443
  29.6 1.5 %collective-permute-start.9 = (f32[64,128]{1,0:T(8,128)S(1)}, f32[64,128]{1,0:T(8,128)S(1)}, u32[]{:S(2)}, u32[]{:S(2)}) collective-permute-start(f32[64,128]{1,0:T(8,128)S(1)} %slice.9), channel_id=1, source_target_pairs={{0,1},{1,0},{2,3},{3,2},{4,5},{5,4},{6,7},{7,6},{8,9},{9,8},{10,11... | collective-permute-start | bytes 98312 | tf_op jit(solution)/shard_map/ppermute | solution.py:443

commit v11 on v10

--- a/solution.py
+++ b/solution.py
@@ -15,7 +15,7 @@
 HALO = DEGREE
 GRID_ROWS = ("strip", "sub")
 SIDE = 5
-CHUNK = 2
+CHUNK = 1
 
 VMEM = pl.BlockSpec(memory_space=pltpu.VMEM)
 SMEM = pl.BlockSpec(memory_space=pltpu.SMEM)

time: 32.4 us -> 32.3 us (level)
  no operation moved by 1% of the time
where the time goes in v11:
time: 32.3 us; the launch traced here: 32.1 us
  starting transfers between devices  13.6 us (42%)
  Pallas kernels  10.7 us (33%)
  waiting for transfers between devices  7.08 us (22%)
  between operations  0.74 us (2%)
    ppermute x7, starting transfers between devices, swap(): return lax.ppermute(array, axis, [(i, i ^ distance) for i in range(size)])  9.23 us
    ppermute x7, waiting for transfers between devices, swap(): return lax.ppermute(array, axis, [(i, i ^ distance) for i in range(size)])  6.59 us
    pallas_call x1, Pallas kernels, filter_call(): pl.pallas_call(lambda *refs: filter_kernel(*refs, panels=panels, height=h...  4.86 us
    ppermute x1, starting transfers between devices, on_device(): lax.ppermute(body, 'panel', [((i + shift) % panels, i) for i in range(pan...  3 us
    pallas_call x1, Pallas kernels, relayout(): pl.pallas_call(relayout_kernel, in_specs=[HBM], out_specs=VMEM, out_shape...  2.34 us
    pallas_call x1, Pallas kernels, factorize(): pl.pallas_call(lambda *refs: factor_kernel(*refs, vertices=float(vertices...  1.36 us
    ppermute x2, starting transfers between devices, on_device(): lax.ppermute(far, ('strip', 'panel', 'sub'), far_moves(shift))  1.34 us
    pallas_call x1, Pallas kernels, finish(): pl.pallas_call(lambda *refs: finish_kernel(*refs, vertices=float(vertices...  1.1 us
  transfers between devices with their start and end apart: 10, of which 6 were waited for; matrix products, arithmetic and copies ran while one was open for 0% of the time, Pallas kernels for 12%

profile of v11, /device:TPU:0, one launch (start us, length us, event | category | flops | bytes accessed | tf_op | source)
XLA Modules:
  0.0 32.1 jit_solution(12502539292051745088)
XLA Ops:
  0.6 1.0 %pack.1.refs_1_.refs_2_ = f32[592,128]{1,0:T(8,128)S(1)} custom-call(s32[1]{0:T(128)} %bitcast.1.panel_ref.refs_0_, s32[1]{0:T(128)} %bitcast.sub_ref.refs_0_.refs_1_, f32[32,16,128]{2,1,0:T(8,128)} %block_hbm.1, f32[8,16,128]{2,1,0:T(8,128)} %weights_hbm.1, f32[16,128]{1,0:T(8,128)} %mass_hbm.1), custom_call_target="tpu_custom_call" | custom-call | tf_op jit(solution)/shard_map/pack/pallas_call | solution.py:57
  1.7 3.0 %collective-permute-start = (f32[592,128]{1,0:T(8,128)S(1)}, f32[592,128]{1,0:T(8,128)S(1)}, u32[]{:S(2)}, u32[]{:S(2)}) collective-permute-start(f32[592,128]{1,0:T(8,128)S(1)} %pack.1.refs_1_.refs_2_), channel_id=1, source_target_pairs={{2,0},{0,2},{3,1},{1,3},{6,4},{4,6},{7,5},{5,7},{10,8},{8,10},{11,... | collective-permute-start | bytes 909320 | tf_op jit(solution)/shard_map/ppermute | solution.py:472
  4.7 0.7 %collective-permute-start.4 = (f32[232,128]{1,0:T(8,128)S(1)}, f32[232,128]{1,0:T(8,128)S(1)}, u32[]{:S(2)}, u32[]{:S(2)}) collective-permute-start(f32[232,128]{1,0:T(8,128)S(1)} %get-tuple-element.13), channel_id=1, source_target_pairs={{1,6},{3,4},{4,3},{6,1},{5,10},{7,8},{8,7},{10,5},{9,14},{11,12},{... | collective-permute-start | bytes 356360 | tf_op jit(solution)/shard_map/ppermute | solution.py:487
  5.4 0.7 %collective-permute-start.3 = (f32[232,128]{1,0:T(8,128)S(1)}, f32[232,128]{1,0:T(8,128)S(1)}, u32[]{:S(2)}, u32[]{:S(2)}) collective-permute-start(f32[232,128]{1,0:T(8,128)S(1)} %get-tuple-element.13), channel_id=1, source_target_pairs={{1,4},{3,6},{4,1},{6,3},{5,8},{7,10},{8,5},{10,7},{9,12},{11,14},{... | collective-permute-start | bytes 356360 | tf_op jit(solution)/shard_map/ppermute | solution.py:487
  6.1 4.2 %collective-permute-start.1 = (f32[232,128]{1,0:T(8,128)S(1)}, f32[232,128]{1,0:T(8,128)S(1)}, u32[]{:S(2)}, u32[]{:S(2)}) collective-permute-start(f32[232,128]{1,0:T(8,128)S(1)} %get-tuple-element.12), channel_id=1, source_target_pairs={{0,1},{1,0},{2,3},{3,2},{4,5},{5,4},{6,7},{7,6},{8,9},{9,8},{10,11... | collective-permute-start | bytes 356360 | tf_op jit(solution)/shard_map/ppermute | solution.py:443
  10.3 2.3 %relayout.1.refs_2_.refs_8_ = bf16[512,4096]{1,0:T(8,128)(2,1)S(1)} custom-call(bf16[512,16,256]{2,1,0:T(8,128)(2,1)} %locked_hbm.1), custom_call_target="tpu_custom_call" | custom-call | tf_op jit(solution)/shard_map/relayout/pallas_call | solution.py:99
  12.7 0.5 %collective-permute-done.refs_1_.refs_3_ = f32[592,128]{1,0:T(8,128)S(1)} collective-permute-done((f32[592,128]{1,0:T(8,128)S(1)}, f32[592,128]{1,0:T(8,128)S(1)}, u32[]{:S(2)}, u32[]{:S(2)}) %collective-permute-start) | collective-permute-done | bytes 303136 | tf_op jit(solution)/shard_map/ppermute | solution.py:472
  13.2 0.1 collective-permute-start.2
  13.2 0.0 collective-permute-done.1.refs_4_
  13.2 0.0 collective-permute-done.4.refs_7_
  13.3 0.0 collective-permute-done.3.refs_6_
  13.3 1.3 %collective-permute-done.2.refs_5_ = f32[232,128]{1,0:T(8,128)S(1)} collective-permute-done((f32[232,128]{1,0:T(8,128)S(1)}, f32[232,128]{1,0:T(8,128)S(1)}, u32[]{:S(2)}, u32[]{:S(2)}) %collective-permute-start.2) | collective-permute-done | bytes 118816 | tf_op jit(solution)/shard_map/ppermute | solution.py:443
  14.5 4.9 %filter.1 = (f32[72,128]{1,0:T(8,128)S(1)}, f32[72,128]{1,0:T(8,128)S(1)}, f32[16,32,128]{2,1,0:T(8,128)S(1)}) custom-call(s32[1]{0:T(128)} %bitcast.1.panel_ref.refs_0_, s32[1]{0:T(128)} %bitcast.sub_ref.refs_0_.refs_1_, f32[592,128]{1,0:T(8,128)S(1)} %pack.1.refs_1_.refs_2_, f32[592,128]{1,0:T(8,128)S(1)} %collective-permute-done.refs_1_.refs_3_, ...), custom_call_target="tpu_custom_call" | custom-call | tf_op jit(solution)/shard_map/filter/pallas_call | solution.py:303
  19.4 0.2 collective-permute-start.5
  19.6 1.1 %collective-permute-done.5 = f32[72,128]{1,0:T(8,128)S(1)} collective-permute-done((f32[72,128]{1,0:T(8,128)S(1)}, f32[72,128]{1,0:T(8,128)S(1)}, u32[]{:S(2)}, u32[]{:S(2)}) %collective-permute-start.5) | collective-permute-done | bytes 36896 | tf_op jit(solution)/shard_map/ppermute | solution.py:443
  20.6 3.8 %collective-permute-start.8 = (f32[72,128]{1,0:T(8,128)S(1)}, f32[72,128]{1,0:T(8,128)S(1)}, u32[]{:S(2)}, u32[]{:S(2)}) collective-permute-start(f32[72,128]{1,0:T(8,128)S(1)} %add.12), channel_id=1, source_target_pairs={{0,12},{4,8},{8,4},{12,0},{1,13},{5,9},{9,5},{13,1},{2,14},{6,10},... | collective-permute-start | bytes 110600 | tf_op jit(solution)/shard_map/ppermute | solution.py:443
  24.5 0.7 %collective-permute-start.7 = (f32[72,128]{1,0:T(8,128)S(1)}, f32[72,128]{1,0:T(8,128)S(1)}, u32[]{:S(2)}, u32[]{:S(2)}) collective-permute-start(f32[72,128]{1,0:T(8,128)S(1)} %add.12), channel_id=1, source_target_pairs={{0,8},{4,12},{8,0},{12,4},{1,9},{5,13},{9,1},{13,5},{2,10},{6,14},... | collective-permute-start | bytes 110600 | tf_op jit(solution)/shard_map/ppermute | solution.py:443
  25.2 0.1 collective-permute-start.6
  25.3 1.2 %collective-permute-done.8 = f32[72,128]{1,0:T(8,128)S(1)} collective-permute-done((f32[72,128]{1,0:T(8,128)S(1)}, f32[72,128]{1,0:T(8,128)S(1)}, u32[]{:S(2)}, u32[]{:S(2)}) %collective-permute-start.8) | collective-permute-done | bytes 36896 | tf_op jit(solution)/shard_map/ppermute | solution.py:443
  26.5 2.9 %collective-permute-done.7 = f32[72,128]{1,0:T(8,128)S(1)} collective-permute-done((f32[72,128]{1,0:T(8,128)S(1)}, f32[72,128]{1,0:T(8,128)S(1)}, u32[]{:S(2)}, u32[]{:S(2)}) %collective-permute-start.7) | collective-permute-done | bytes 36896 | tf_op jit(solution)/shard_map/ppermute | solution.py:443
  29.5 0.1 collective-permute-done.6
  29.6 0.1 collective-permute-start.9
  29.7 1.4 %factor.1 = (f32[32,32]{1,0:T(8,128)}, f32[32,32]{1,0:T(8,128)S(1)}) custom-call(f32[8,128]{1,0:T(8,128)S(1)} %slice.8.refs_0_), custom_call_target="tpu_custom_call" | custom-call | tf_op jit(solution)/shard_map/factor/pallas_call | solution.py:377
  31.0 0.0 collective-permute-done.9.refs_4_
  31.0 1.1 %finish.1 = (f32[32,16,128]{2,1,0:T(8,128)}, f32[32,512]{1,0:T(8,128)}) custom-call(s32[1]{0:T(128)} %bitcast.sub_ref.refs_0_.refs_1_, f32[32,32]{1,0:T(8,128)S(1)} %get-tuple-element.16.refs_1_, f32[16,32,128]{2,1,0:T(8,128)S(1)} %get-tuple-element.17.refs_2_, f32[72,128]{1,0:T(8,128)S(1)} %add_add_fusion.refs_3_, f32[64,128]{1,0:T(8,128)S(1)} %collective-permute-done.9.refs_4_), custom_call_target="tpu_custom_call" | custom-call | tf_op jit(solution)/shard_map/finish/pallas_call | solution.py:426
  (6 shorter events, 0.1 us)
Async XLA Ops:
  1.7 11.5 %collective-permute-start = (f32[592,128]{1,0:T(8,128)S(1)}, f32[592,128]{1,0:T(8,128)S(1)}, u32[]{:S(2)}, u32[]{:S(2)}) collective-permute-start(f32[592,128]{1,0:T(8,128)S(1)} %pack.1.refs_1_.refs_2_), channel_id=1, source_target_pairs={{2,0},{0,2},{3,1},{1,3},{6,4},{4,6},{7,5},{5,7},{10,8},{8,10},{11,... | collective-permute-start | bytes 909320 | tf_op jit(solution)/shard_map/ppermute | solution.py:472
  4.7 8.5 %collective-permute-start.4 = (f32[232,128]{1,0:T(8,128)S(1)}, f32[232,128]{1,0:T(8,128)S(1)}, u32[]{:S(2)}, u32[]{:S(2)}) collective-permute-start(f32[232,128]{1,0:T(8,128)S(1)} %get-tuple-element.13), channel_id=1, source_target_pairs={{1,6},{3,4},{4,3},{6,1},{5,10},{7,8},{8,7},{10,5},{9,14},{11,12},{... | collective-permute-start | bytes 356360 | tf_op jit(solution)/shard_map/ppermute | solution.py:487
  5.4 7.9 %collective-permute-start.3 = (f32[232,128]{1,0:T(8,128)S(1)}, f32[232,128]{1,0:T(8,128)S(1)}, u32[]{:S(2)}, u32[]{:S(2)}) collective-permute-start(f32[232,128]{1,0:T(8,128)S(1)} %get-tuple-element.13), channel_id=1, source_target_pairs={{1,4},{3,6},{4,1},{6,3},{5,8},{7,10},{8,5},{10,7},{9,12},{11,14},{... | collective-permute-start | bytes 356360 | tf_op jit(solution)/shard_map/ppermute | solution.py:487
  6.1 7.2 %collective-permute-start.1 = (f32[232,128]{1,0:T(8,128)S(1)}, f32[232,128]{1,0:T(8,128)S(1)}, u32[]{:S(2)}, u32[]{:S(2)}) collective-permute-start(f32[232,128]{1,0:T(8,128)S(1)} %get-tuple-element.12), channel_id=1, source_target_pairs={{0,1},{1,0},{2,3},{3,2},{4,5},{5,4},{6,7},{7,6},{8,9},{9,8},{10,11... | collective-permute-start | bytes 356360 | tf_op jit(solution)/shard_map/ppermute | solution.py:443
  13.2 1.4 %collective-permute-start.2 = (f32[232,128]{1,0:T(8,128)S(1)}, f32[232,128]{1,0:T(8,128)S(1)}, u32[]{:S(2)}, u32[]{:S(2)}) collective-permute-start(f32[232,128]{1,0:T(8,128)S(1)} %edge_rows.3), channel_id=1, source_target_pairs={{0,1},{1,0},{2,3},{3,2},{4,5},{5,4},{6,7},{7,6},{8,9},{9,8},{10,11... | collective-permute-start | bytes 356360 | tf_op jit(solution)/shard_map/ppermute | solution.py:443
  19.4 1.2 %collective-permute-start.5 = (f32[72,128]{1,0:T(8,128)S(1)}, f32[72,128]{1,0:T(8,128)S(1)}, u32[]{:S(2)}, u32[]{:S(2)}) collective-permute-start(f32[72,128]{1,0:T(8,128)S(1)} %get-tuple-element.15), channel_id=1, source_target_pairs={{0,1},{1,0},{2,3},{3,2},{4,5},{5,4},{6,7},{7,6},{8,9},{9,8},{10,11... | collective-permute-start | bytes 110600 | tf_op jit(solution)/shard_map/ppermute | solution.py:443
  20.6 5.9 %collective-permute-start.8 = (f32[72,128]{1,0:T(8,128)S(1)}, f32[72,128]{1,0:T(8,128)S(1)}, u32[]{:S(2)}, u32[]{:S(2)}) collective-permute-start(f32[72,128]{1,0:T(8,128)S(1)} %add.12), channel_id=1, source_target_pairs={{0,12},{4,8},{8,4},{12,0},{1,13},{5,9},{9,5},{13,1},{2,14},{6,10},... | collective-permute-start | bytes 110600 | tf_op jit(solution)/shard_map/ppermute | solution.py:443
  24.5 5.0 %collective-permute-start.7 = (f32[72,128]{1,0:T(8,128)S(1)}, f32[72,128]{1,0:T(8,128)S(1)}, u32[]{:S(2)}, u32[]{:S(2)}) collective-permute-start(f32[72,128]{1,0:T(8,128)S(1)} %add.12), channel_id=1, source_target_pairs={{0,8},{4,12},{8,0},{12,4},{1,9},{5,13},{9,1},{13,5},{2,10},{6,14},... | collective-permute-start | bytes 110600 | tf_op jit(solution)/shard_map/ppermute | solution.py:443
  25.2 4.4 %collective-permute-start.6 = (f32[72,128]{1,0:T(8,128)S(1)}, f32[72,128]{1,0:T(8,128)S(1)}, u32[]{:S(2)}, u32[]{:S(2)}) collective-permute-start(f32[72,128]{1,0:T(8,128)S(1)} %add.12), channel_id=1, source_target_pairs={{0,4},{4,0},{8,12},{12,8},{1,5},{5,1},{9,13},{13,9},{2,6},{6,2},{1... | collective-permute-start | bytes 110600 | tf_op jit(solution)/shard_map/ppermute | solution.py:443
  29.6 1.5 %collective-permute-start.9 = (f32[64,128]{1,0:T(8,128)S(1)}, f32[64,128]{1,0:T(8,128)S(1)}, u32[]{:S(2)}, u32[]{:S(2)}) collective-permute-start(f32[64,128]{1,0:T(8,128)S(1)} %slice.9), channel_id=1, source_target_pairs={{0,1},{1,0},{2,3},{3,2},{4,5},{5,4},{6,7},{7,6},{8,9},{9,8},{10,11... | collective-permute-start | bytes 98312 | tf_op jit(solution)/shard_map/ppermute | solution.py:443
